TPU v7x, 128 devices: a whole 4x4x4 slice. The times are simulated.
128 devices in a mesh: space: 16 (over z, x_lo, core), samp: 8 (over y, x_hi).
Axes of the slice: x: 4 (x_hi: 2, x_lo: 2; x = x_hi * 2 + x_lo), y: 4, z: 4, core: 2. Of those that a mesh axis runs over, the one named last changes fastest.
Arguments:
- basis_u: bfloat16 [128, 32, 8, 128], P('samp', 'space'), may hold values from -0.75 to 0.75
- basis_v: bfloat16 [128, 65536], P('space', 'samp'), may hold values from -0.75 to 0.75
- core_s: float32 [128, 128], replicated, may hold values from -4 to 4
- face_class: int32 [6, 32, 8, 128], P(None, 'space'), may hold values from 0 to 3
- sample_class: int32 [65536], P('samp'), may hold values from 0 to 3
Outputs:
- k_new: float32 [128, 32, 8, 128], P('samp', 'space')
- l_new: float32 [128, 65536], P('space', 'samp')
All inputs are finite; a program needn't handle non-finite values.
Results may differ from a plain program's by a relative error of at most 0.0046.
Values may be sent and summed in bfloat16 or wider, within the bound.
No kernel may reach another device: no remote copies, remote signals or barrier semaphores. Data moves between devices by JAX's collectives and lax.ppermute only.
A program may use at most 64 MiB of HBM per device.

v0:
```python
import functools

import jax
import jax.numpy as jnp
from jax import lax
from jax.experimental import pallas as pl
from jax.experimental.pallas import tpu as pltpu
from jax.sharding import Mesh, PartitionSpec as P

step_size = 0.1
SPACE = ("z", "xl", "c")
SAMP = ("y", "xh")
BLOCK = 2048
bf16, f32 = jnp.bfloat16, jnp.float32


def dot(a, b, ca, cb):
    return lax.dot_general(a, b, (((ca,), (cb,)), ((), ())), preferred_element_type=f32)


def resident(x):
    return pltpu.with_memory_space_constraint(x, pltpu.MemorySpace.VMEM)


def small(body, args, outs, scratch=(), at=None, held=(), limit=24):
    vm = pl.BlockSpec(memory_space=pltpu.VMEM)
    scalars = [] if at is None else [at]
    n_read = len(scalars) + len(args)

    def reading(*refs):
        body(*refs[:n_read], *refs[n_read + len(held) :])

    return pl.pallas_call(
        reading,
        in_specs=[pl.BlockSpec(memory_space=pltpu.SMEM)] * len(scalars)
        + [vm] * (len(args) + len(held)),
        out_specs=[vm] * len(outs),
        out_shape=[(pltpu.VMEM if keep else pltpu.HBM)(shape, dtype) for shape, dtype, keep in outs],
        scratch_shapes=[pltpu.VMEM(shape, dtype) for shape, dtype in scratch],
        compiler_params=pltpu.CompilerParams(vmem_limit_bytes=limit << 20),
    )(*scalars, *args, *held)


def head_body(u_ref, v_ref, flat_ref, out_ref, u_s):
    _, depth, rows, cols = u_ref.shape
    u_s[...] = u_ref[...].astype(f32)
    for x in range(depth):
        for y in range(rows):
            at = (x * rows + y) * cols
            flat_ref[:, at : at + cols] = u_s[:, x, y, :].astype(bf16)
    half = out_ref.shape[-1]
    for k in range(out_ref.shape[0]):
        out_ref[k, 0] = v_ref[:, :half]
        out_ref[k, 1] = v_ref[:, half:]


def prep_body(at_ref, u_ref, w_ref, a_ref, b_ref, c_ref, core_ref, full_ref, k_ref, kt_ref, halo_ref):
    narrow, cells = u_ref.shape
    half = cells // 2
    y, xh = at_ref[2], at_ref[3]

    def put(turn, flip, value):
        row = (((y + turn) % 4) * 2 + (xh if flip == 0 else 1 - xh)) * narrow
        full_ref[pl.ds(pl.multiple_of(row, narrow), narrow), :] = value

    put(0, 0, u_ref[...])
    put(0, 1, w_ref[...])
    for turn, ref in ((3, a_ref), (1, b_ref), (2, c_ref)):
        put(turn, 0, ref[:narrow, :])
        put(turn, 1, ref[narrow:, :])
    k_own = dot(core_ref[...].astype(bf16), full_ref[...], 0, 0).astype(bf16)
    k_ref[...] = k_own
    kt_ref[...] = k_own.T
    first = at_ref[0] == 0

    @pl.when(first)
    def _():
        halo_ref[...] = k_own[:, :half]

    @pl.when(jnp.logical_not(first))
    def _():
        halo_ref[...] = k_own[:, half:]


def mid_body(rows, cols, c_ref, oth_ref, core_ref, k_ref, halo_ref, face_ref, u_ref, kt_ref, base_ref, m_ref, base_s, lap_s):
    half = oth_ref.shape[1] // 2
    k_oth = dot(core_ref[...].astype(bf16), oth_ref[...], 0, 0).astype(bf16)
    kt_ref[...] = k_oth.T
    first = c_ref[0] == 0
    near = jnp.where(first, k_oth[:, :half].astype(f32), k_oth[:, half:].astype(f32))
    halo = halo_ref[...].astype(f32)
    before = jnp.where(first, halo, near)
    after = jnp.where(first, near, halo)
    plane = rows * cols
    lane = lax.broadcasted_iota(jnp.int32, (1, cols), 1)
    for x in range(2):
        for y in range(rows):
            at = (x * rows + y) * cols
            mid = k_ref[:, at : at + cols].astype(f32)
            w = [0.25 * lax.shift_left(1, face_ref[f, x, y : y + 1, :]).astype(f32) for f in range(6)]
            total = ((w[0] + w[1]) + (w[2] + w[3])) + (w[4] + w[5])
            down = before[:, y * cols : (y + 1) * cols] if x == 0 else k_ref[:, at - plane : at - plane + cols].astype(f32)
            up = after[:, y * cols : (y + 1) * cols] if x == 1 else k_ref[:, at + plane : at + plane + cols].astype(f32)
            out = w[0] * down + w[1] * up - total * mid
            if y > 0:
                out += w[2] * k_ref[:, at - cols : at].astype(f32)
            if y < rows - 1:
                out += w[3] * k_ref[:, at + cols : at + 2 * cols].astype(f32)
            out += jnp.where(lane == 0, 0.0, w[4]) * pltpu.roll(mid, 1, 1)
            out += jnp.where(lane == cols - 1, 0.0, w[5]) * pltpu.roll(mid, cols - 1, 1)
            base_s[:, at : at + cols] = mid + step_size * out
            lap_s[:, at : at + cols] = out.astype(bf16)
    base_ref[...] = base_s[pl.ds(pl.multiple_of(c_ref[1] * base_ref.shape[0], 8), base_ref.shape[0]), :]
    m_ref[...] = dot(u_ref[...], lap_s[...], 1, 1)


def sweep(kt_ref, u_ref, v_ref, g_ref, ov_ref, start, stop, store, tile=512):
    block = min(BLOCK, stop - start)

    def turn(i, _):
        at = pl.multiple_of(start + i * block, block)
        v = v_ref[:, pl.ds(at, block)]
        g = g_ref[:, pl.ds(at, block)]
        acc = None
        for row in range(0, u_ref.shape[1], tile):
            field = dot(kt_ref[row : row + tile, :], v, 1, 0)
            react = (field * (g - field * field)).astype(bf16)
            ov_ref[row : row + tile, :] += dot(react, v, 1, 1)
            part = dot(u_ref[:, row : row + tile], react, 1, 0)
            acc = part if acc is None else acc + part
        store(pl.ds(pl.multiple_of(at - start, block), block), acc)
        return 0

    lax.fori_loop(0, (stop - start) // block, turn, 0)


def part_body(start, has_old, back, kt_ref, u_ref, v_ref, g_ref, *refs):
    refs = list(refs)
    old_ref = refs.pop(0) if has_old & 1 else None
    far_ref = refs.pop(0) if has_old & 2 else None
    l_ref, ov_ref = refs[:2]
    ov_s = refs[2] if back else ov_ref
    ov_s[...] = jnp.zeros_like(ov_s) if far_ref is None else far_ref[...]

    def store(here, acc):
        l_ref[:, here] = acc if old_ref is None else old_ref[:, here] + acc

    stop = start + l_ref.shape[1]
    done = 0 if old_ref is None else old_ref.shape[1]
    if done:
        sweep(kt_ref, u_ref, v_ref, g_ref, ov_s, start, start + done, store)
    if start + done < stop:

        def rest(here, acc):
            l_ref[:, pl.ds(pl.multiple_of(here.start + done, done or BLOCK), here.size)] = acc

        sweep(kt_ref, u_ref, v_ref, g_ref, ov_s, start + done, stop, rest)
    if back:
        ov_ref[...] = ov_s[...].T.astype(bf16)


def last_body(
    scale, at_ref, kt_ref, u_ref, v_ref, g_ref, l_ref, more_ref, ov_ref, got_ref, ma_ref, mb_ref, core_ref,
    out_ref, me_ref, up_ref, dn_ref, away_ref, ov_s, tot_s, w_s,
):
    rank, count = out_ref.shape
    middle = count - count // 2
    start = middle + more_ref.shape[1]
    ov_s[...] = ov_ref[...]
    w = core_ref[...].astype(bf16).astype(f32) * 0.125 + scale * (ma_ref[...] + mb_ref[...])
    high = w.astype(bf16)
    w_s[:rank, :] = high
    w_s[rank:, :] = (w - high.astype(f32)).astype(bf16)

    def send(at, size, total):
        side = dot(w_s[...], v_ref[:, at : at + size], 1, 0)
        out_ref[:, at : at + size] = (scale * total + (side[:rank] + side[rank:])).astype(bf16)

    send(0, middle, l_ref[:, :middle])
    send(middle, start - middle, l_ref[:, middle:start] + more_ref[...])

    def store(here, acc):
        send(start, count - start, l_ref[:, start:] + acc)

    sweep(kt_ref, u_ref, v_ref, g_ref, ov_s, start, count, store)
    tot_s[...] = ov_s[...].T + got_ref[...].astype(f32)
    rows = me_ref.shape[0]
    y = at_ref[2]

    def part(turn):
        return tot_s[pl.ds(pl.multiple_of(((y + turn) % 4) * rows, rows), rows), :]

    me_ref[...] = part(0)
    up_ref[...] = part(1).astype(bf16)
    away_ref[...] = part(2).astype(bf16)
    dn_ref[...] = part(3).astype(bf16)


def done_body(scale, base_ref, mine_ref, got_ref, out_ref):
    _, depth, rows, cols = out_ref.shape
    new = base_ref[...] + scale * (mine_ref[...] + got_ref[...].astype(f32))
    for x in range(depth):
        for y in range(rows):
            at = (x * rows + y) * cols
            out_ref[:, x, y, :] = new[:, at : at + cols]


def pair_body(at_ref, me_ref, rc_ref, rd_ref, re_ref, mine_ref, send_ref, tot_s):
    rows = mine_ref.shape[0]
    tot_s[...] = (me_ref[...] + rc_ref[...].astype(f32)) + (rd_ref[...].astype(f32) + re_ref[...].astype(f32))
    xh = at_ref[3]
    mine_ref[...] = tot_s[pl.ds(pl.multiple_of(xh * rows, rows), rows), :]
    send_ref[...] = tot_s[pl.ds(pl.multiple_of((1 - xh) * rows, rows), rows), :].astype(bf16)


def ring(n, k):
    return [(i, (i + k) % n) for i in range(n)]


def per_device(basis_u, basis_v, core_s, face_class, sample_class):
    narrow, depth_x, rows_y, cols_z = basis_u.shape
    rank = core_s.shape[0]
    n_samp, n_space = 8, 16
    cells = depth_x * rows_y * cols_z
    lanes, samp_rows = basis_v.shape
    half = samp_rows // 2
    cell_weight = rank / (cells * n_space)
    samp_weight = rank / (samp_rows * n_samp)
    core_at = lax.axis_index("c")
    where_at = jnp.stack([core_at, lax.axis_index(SAMP), lax.axis_index("y"), lax.axis_index("xh")]).astype(jnp.int32)
    swap = ring(2, 1)

    u0, v_wide = small(
        head_body,
        [basis_u, basis_v],
        [((narrow, cells), bf16, True), ((n_space // 2, 2, lanes, half), bf16, False)],
        [(basis_u.shape, f32)],
    )
    v = resident(lax.all_to_all(v_wide.reshape(rank, half), SPACE, 0, 0, tiled=True))
    u1 = lax.ppermute(u0, "xh", swap)
    pair = jnp.concatenate([u0, u1], 0)
    around = [resident(lax.ppermute(pair, "y", ring(4, k))) for k in (1, 3, 2)]
    u_own, k_own, kt_own, edge = small(
        prep_body,
        [u0, resident(u1), *around, core_s],
        [((rank, cells), bf16, True), ((rank, cells), bf16, True), ((cells, rank), bf16, True), ((rank, cells // 2), bf16, True)],
        at=where_at,
    )
    u_oth = resident(lax.ppermute(u_own, "c", swap))
    chips = n_space // 2
    hops = [(2 * i + 1, 2 * i + 2) for i in range(chips - 1)] + [(2 * i + 2, 2 * i + 1) for i in range(chips - 1)]
    halo = resident(lax.ppermute(edge, SPACE, hops))

    growth = 0.5 + 0.5 * lax.dynamic_slice_in_dim(sample_class, core_at * half, half, 0).astype(f32)
    growth = resident(growth.reshape(1, half))
    scale = step_size * cell_weight
    quart = half // 2
    main = lambda start, kinds, back: functools.partial(part_body, start, kinds, back)
    l_first, ov_first = small(
        main(0, 0, False), [kt_own, u_own, v, growth], [((rank, quart), f32, True), ((cells, rank), f32, True)]
    )
    kt_oth, base, m_own = small(
        functools.partial(mid_body, rows_y, cols_z),
        [u_oth, core_s, k_own, halo, face_class, u_own],
        [((cells, rank), bf16, True), ((narrow, cells), f32, False), ((rank, rank), f32, True)],
        [((rank, cells), f32), ((rank, cells), bf16)],
        at=where_at,
        held=(ov_first, kt_own, l_first),
    )
    m_oth = resident(lax.ppermute(m_own, "c", swap))
    l_most, ov_send = small(
        main(0, 1, True),
        [kt_oth, u_oth, v, growth, l_first],
        [((rank, half), f32, True), ((rank, cells), bf16, True)],
        [((cells, rank), f32)],
        held=(ov_first, kt_own, u_own),
    )
    got = resident(lax.ppermute(ov_send, "c", swap))
    l_more, ov_more = small(
        main(quart, 2, False),
        [kt_own, u_own, v, growth, ov_first],
        [((rank, quart // 2), f32, True), ((cells, rank), f32, True)],
        held=(l_most, ov_send),
    )
    rows = rank // 4
    l_part, me, up, dn, away = small(
        functools.partial(last_body, scale),
        [kt_own, u_own, v, growth, l_most, l_more, ov_more, got, m_own, m_oth, core_s],
        [((rank, half), bf16, False), ((rows, cells), f32, True)] + [((rows, cells), bf16, True)] * 3,
        [((cells, rank), f32), ((rank, cells), f32), ((2 * rank, rank), bf16)],
        at=where_at,
    )

    l_got = lax.all_to_all(l_part, SPACE, 0, 0, tiled=True)
    l_new = l_got.reshape(n_space // 2, 2, lanes, half).astype(f32).sum(0)
    l_new = jnp.transpose(l_new, (1, 0, 2)).reshape(lanes, samp_rows)

    near = [resident(lax.ppermute(part, "y", ring(4, k))) for part, k in ((up, 1), (dn, 3), (away, 2))]
    mine, send = small(
        pair_body,
        [me, *near],
        [((narrow, cells), f32, True), ((narrow, cells), bf16, True)],
        [((rows, cells), f32)],
        at=where_at,
    )
    (k_new,) = small(
        functools.partial(done_body, step_size * samp_weight),
        [base, mine, resident(lax.ppermute(send, "xh", swap))],
        [(basis_u.shape, f32, False)],
    )
    return (k_new, l_new)


def solution(mesh):
    fine = Mesh(mesh.devices.reshape(4, 2, 2, 4, 2), SPACE + SAMP)
    return jax.shard_map(
        per_device,
        mesh=fine,
        in_specs=(P(SAMP, SPACE, None, None), P(SPACE, SAMP), P(), P(None, SPACE, None, None), P(SAMP)),
        out_specs=(P(SAMP, SPACE, None, None), P(SPACE, SAMP)),
        check_vma=False,
    )
```

profile of v0, /device:TPU:0, one launch (start us, length us, event | category | flops | bytes accessed | tf_op | source)
XLA Modules:
  0.0 95.8 jit_solution(12193285059085038568)
XLA Ops:
  0.6 0.9 copy-done.2
  2.4 1.2 %shard_map.68 = (bf16[16,2048]{1,0:T(8,128)(2,1)S(1)}, bf16[8,2,8,4096]{3,2,1,0:T(8,128)(2,1)}) custom-call(bf16[16,2,8,128]{3,2,1,0:T(8,128)(2,1)S(1)} %copy-done.3, bf16[8,8192]{1,0:T(8,128)(2,1)S(1)} %copy-done.2), custom_call_target="tpu_custom_call" | custom-call | tf_op jit(solution)/shard_map/pallas_call | solution.py:33
  3.6 6.6 %all-to-all-start = ((bf16[16,8,4096]{2,1,0:T(8,128)(2,1)}), bf16[16,8,4096]{2,1,0:T(8,128)(2,1)S(1)}, u32[]{:S(2)}, u32[]{:S(2)}) async-start(bf16[16,8,4096]{2,1,0:T(8,128)(2,1)} %bitcast.22), calls=%async_computation | async-start | bytes 2097152 | tf_op jit(solution)/shard_map/all_to_all | solution.py:239
  10.2 2.8 %collective-permute-start = (bf16[16,2048]{1,0:T(8,128)(2,1)S(1)}, bf16[16,2048]{1,0:T(8,128)(2,1)S(1)}, u32[]{:S(2)}, u32[]{:S(2)}) collective-permute-start(bf16[16,2048]{1,0:T(8,128)(2,1)S(1)} %get-tuple-element.24.refs_1_), channel_id=1, source_target_pairs={{0,1},{1,0},{2,3},{3,2},{4,5},{5,4},{6,7},{7,6},{8,9},{9,8},{10,11... | collective-permute-start | bytes 196616 | tf_op jit(solution)/shard_map/ppermute | solution.py:240
  13.0 14.4 %collective-permute-done.refs_2_ = bf16[16,2048]{1,0:T(8,128)(2,1)S(1)} collective-permute-done((bf16[16,2048]{1,0:T(8,128)(2,1)S(1)}, bf16[16,2048]{1,0:T(8,128)(2,1)S(1)}, u32[]{:S(2)}, u32[]{:S(2)}) %collective-permute-start) | collective-permute-done | bytes 65568 | tf_op jit(solution)/shard_map/ppermute | solution.py:240
  27.4 3.2 %collective-permute-start.3 = (bf16[32,2048]{1,0:T(8,128)(2,1)S(1)}, bf16[32,2048]{1,0:T(8,128)(2,1)S(1)}, u32[]{:S(2)}, u32[]{:S(2)}) collective-permute-start(bf16[32,2048]{1,0:T(8,128)(2,1)S(1)} %constant_dynamic-update-slice_fusion), channel_id=1, source_target_pairs={{0,4},{2,6},{4,0},{6,2},{1,5},{3,7},{5,1},{7,3},{8,12},{10,14},{12... | collective-permute-start | bytes 393224 | tf_op jit(solution)/shard_map/ppermute | solution.py:242
  30.6 1.1 %collective-permute-start.2 = (bf16[32,2048]{1,0:T(8,128)(2,1)S(1)}, bf16[32,2048]{1,0:T(8,128)(2,1)S(1)}, u32[]{:S(2)}, u32[]{:S(2)}) collective-permute-start(bf16[32,2048]{1,0:T(8,128)(2,1)S(1)} %constant_dynamic-update-slice_fusion), channel_id=1, source_target_pairs={{0,6},{2,0},{4,2},{6,4},{1,7},{3,1},{5,3},{7,5},{8,14},{10,8},{12,... | collective-permute-start | bytes 393224 | tf_op jit(solution)/shard_map/ppermute | solution.py:242
  31.6 1.0 %collective-permute-start.1 = (bf16[32,2048]{1,0:T(8,128)(2,1)S(1)}, bf16[32,2048]{1,0:T(8,128)(2,1)S(1)}, u32[]{:S(2)}, u32[]{:S(2)}) collective-permute-start(bf16[32,2048]{1,0:T(8,128)(2,1)S(1)} %constant_dynamic-update-slice_fusion), channel_id=1, source_target_pairs={{0,2},{2,4},{4,6},{6,0},{1,3},{3,5},{5,7},{7,1},{8,10},{10,12},{12... | collective-permute-start | bytes 393224 | tf_op jit(solution)/shard_map/ppermute | solution.py:242
  32.7 2.2 %collective-permute-done.3.refs_5_ = bf16[32,2048]{1,0:T(8,128)(2,1)S(1)} collective-permute-done((bf16[32,2048]{1,0:T(8,128)(2,1)S(1)}, bf16[32,2048]{1,0:T(8,128)(2,1)S(1)}, u32[]{:S(2)}, u32[]{:S(2)}) %collective-permute-start.3) | collective-permute-done | bytes 131104 | tf_op jit(solution)/shard_map/ppermute | solution.py:242
  34.9 2.5 %collective-permute-done.2.refs_4_ = bf16[32,2048]{1,0:T(8,128)(2,1)S(1)} collective-permute-done((bf16[32,2048]{1,0:T(8,128)(2,1)S(1)}, bf16[32,2048]{1,0:T(8,128)(2,1)S(1)}, u32[]{:S(2)}, u32[]{:S(2)}) %collective-permute-start.2) | collective-permute-done | bytes 131104 | tf_op jit(solution)/shard_map/ppermute | solution.py:242
  37.8 1.7 %shard_map.69 = (bf16[128,2048]{1,0:T(8,128)(2,1)S(1)}, bf16[128,2048]{1,0:T(8,128)(2,1)S(1)}, bf16[2048,128]{1,0:T(8,128)(2,1)S(1)}, bf16[128,1024]{1,0:T(8,128)(2,1)}) custom-call(s32[4]{0:T(128)S(1)} %pad_add_fusion.refs_0_, bf16[16,2048]{1,0:T(8,128)(2,1)S(1)} %get-tuple-element.24.refs_1_, bf16[16,2048]{1,0:T(8,128)(2,1)S(1)} %collective-permute-done.refs_2_, ...), custom_call_target="tpu_custom_call" | custom-call | tf_op jit(solution)/shard_map/pallas_call | solution.py:33
  41.1 5.6 %shard_map.70 = (f32[128,2048]{1,0:T(8,128)S(1)}, f32[2048,128]{1,0:T(8,128)S(1)}) custom-call(bf16[2048,128]{1,0:T(8,128)(2,1)S(1)} %get-tuple-element.28.refs_0_.refs_8_.refs_6_.refs_1_, bf16[128,2048]{1,0:T(8,128)(2,1)S(1)} %get-tuple-element.25.refs_1_.refs_6_.refs_7_.refs_2_, bf16[128,4096]{1,0:T(8,128)(2,1)S(1)} %bitcast.13, f32[1,4096]{1,0:T(1,128)S(1)} %bitcast.17), custom_call_target="tpu_custom_call" | custom-call | tf_op jit(solution)/shard_map/pallas_call | solution.py:33
  46.7 2.5 %shard_map.71 = (bf16[2048,128]{1,0:T(8,128)(2,1)S(1)}, f32[16,2048]{1,0:T(8,128)}, f32[128,128]{1,0:T(8,128)S(1)}) custom-call(s32[4]{0:T(128)S(1)} %pad_add_fusion.refs_0_, bf16[128,2048]{1,0:T(8,128)(2,1)S(1)} %collective-permute-done.4.refs_1_, f32[128,128]{1,0:T(8,128)S(1)} %copy-done, bf16[128,2048]{1,0:T(8,128)(2,1)S(1)} %get-tuple-element.26.refs_3_, ...), custom_call_target="tpu_custom_call" | custom-call | tf_op jit(solution)/shard_map/pallas_call | solution.py:33
  49.2 11.4 %shard_map.72 = (f32[128,4096]{1,0:T(8,128)S(1)}, bf16[128,2048]{1,0:T(8,128)(2,1)S(1)}) custom-call(bf16[2048,128]{1,0:T(8,128)(2,1)S(1)} %get-tuple-element.33.refs_0_, bf16[128,2048]{1,0:T(8,128)(2,1)S(1)} %collective-permute-done.4.refs_1_, bf16[128,4096]{1,0:T(8,128)(2,1)S(1)} %bitcast.14, f32[1,4096]{1,0:T(1,128)S(1)} %bitcast.18, ...), custom_call_target="tpu_custom_call" | custom-call | tf_op jit(solution)/shard_map/pallas_call | solution.py:33
  60.6 4.0 %collective-permute-start.6 = (bf16[128,2048]{1,0:T(8,128)(2,1)S(1)}, bf16[128,2048]{1,0:T(8,128)(2,1)S(1)}, u32[]{:S(2)}, u32[]{:S(2)}) collective-permute-start(bf16[128,2048]{1,0:T(8,128)(2,1)S(1)} %get-tuple-element.35.refs_6_), channel_id=1, source_target_pairs={{0,8},{8,0},{1,9},{9,1},{2,10},{10,2},{3,11},{11,3},{4,12},{12,4},... | collective-permute-start | bytes 1572872 | tf_op jit(solution)/shard_map/ppermute | solution.py:278
  64.9 2.9 %shard_map.73 = (f32[128,1024]{1,0:T(8,128)S(1)}, f32[2048,128]{1,0:T(8,128)S(1)}) custom-call(bf16[2048,128]{1,0:T(8,128)(2,1)S(1)} %get-tuple-element.28.refs_0_.refs_8_.refs_6_.refs_1_, bf16[128,2048]{1,0:T(8,128)(2,1)S(1)} %get-tuple-element.25.refs_1_.refs_6_.refs_7_.refs_2_, bf16[128,4096]{1,0:T(8,128)(2,1)S(1)} %bitcast.15, f32[1,4096]{1,0:T(1,128)S(1)} %bitcast.19, ...), custom_call_target="tpu_custom_call" | custom-call | tf_op jit(solution)/shard_map/pallas_call | solution.py:33
  67.9 5.1 %shard_map.74 = (bf16[128,4096]{1,0:T(8,128)(2,1)}, f32[32,2048]{1,0:T(8,128)S(1)}, bf16[32,2048]{1,0:T(8,128)(2,1)S(1)}, bf16[32,2048]{1,0:T(8,128)(2,1)S(1)}, bf16[32,2048]{1,0:T(8,128)(2,1)S(1)}) custom-call(s32[4]{0:T(128)S(1)} %pad_add_fusion.refs_0_, bf16[2048,128]{1,0:T(8,128)(2,1)S(1)} %get-tuple-element.28.refs_0_.refs_8_.refs_6_.refs_1_, ...), custom_call_target="tpu_custom_call" | custom-call | tf_op jit(solution)/shard_map/pallas_call | solution.py:33
  73.0 4.8 %all-to-all-start.1 = ((bf16[16,8,4096]{2,1,0:T(8,128)(2,1)}), bf16[16,8,4096]{2,1,0:T(8,128)(2,1)S(1)}, u32[]{:S(2)}, u32[]{:S(2)}) async-start(bf16[16,8,4096]{2,1,0:T(8,128)(2,1)} %bitcast.23), calls=%async_computation.1 | async-start | bytes 2097152 | tf_op jit(solution)/shard_map/all_to_all | solution.py:294
  78.3 2.7 %collective-permute-start.9 = (bf16[32,2048]{1,0:T(8,128)(2,1)S(1)}, bf16[32,2048]{1,0:T(8,128)(2,1)S(1)}, u32[]{:S(2)}, u32[]{:S(2)}) collective-permute-start(bf16[32,2048]{1,0:T(8,128)(2,1)S(1)} %get-tuple-element.41), channel_id=1, source_target_pairs={{0,6},{2,0},{4,2},{6,4},{1,7},{3,1},{5,3},{7,5},{8,14},{10,8},{12,... | collective-permute-start | bytes 393224 | tf_op jit(solution)/shard_map/ppermute | solution.py:298
  81.8 2.9 %collective-permute-done.8.refs_2_ = bf16[32,2048]{1,0:T(8,128)(2,1)S(1)} collective-permute-done((bf16[32,2048]{1,0:T(8,128)(2,1)S(1)}, bf16[32,2048]{1,0:T(8,128)(2,1)S(1)}, u32[]{:S(2)}, u32[]{:S(2)}) %collective-permute-start.8) | collective-permute-done | bytes 131104 | tf_op jit(solution)/shard_map/ppermute | solution.py:298
  84.7 2.1 %collective-permute-done.9.refs_3_ = bf16[32,2048]{1,0:T(8,128)(2,1)S(1)} collective-permute-done((bf16[32,2048]{1,0:T(8,128)(2,1)S(1)}, bf16[32,2048]{1,0:T(8,128)(2,1)S(1)}, u32[]{:S(2)}, u32[]{:S(2)}) %collective-permute-start.9) | collective-permute-done | bytes 131104 | tf_op jit(solution)/shard_map/ppermute | solution.py:298
  86.9 0.9 collective-permute-done.10.refs_4_
  88.4 2.0 %collective-permute-start.11 = (bf16[16,2048]{1,0:T(8,128)(2,1)S(1)}, bf16[16,2048]{1,0:T(8,128)(2,1)S(1)}, u32[]{:S(2)}, u32[]{:S(2)}) collective-permute-start(bf16[16,2048]{1,0:T(8,128)(2,1)S(1)} %get-tuple-element.44), channel_id=1, source_target_pairs={{0,1},{1,0},{2,3},{3,2},{4,5},{5,4},{6,7},{7,6},{8,9},{9,8},{10,11... | collective-permute-start | bytes 196616 | tf_op jit(solution)/shard_map/ppermute | solution.py:308
  90.4 3.8 %collective-permute-done.11.refs_2_ = bf16[16,2048]{1,0:T(8,128)(2,1)S(1)} collective-permute-done((bf16[16,2048]{1,0:T(8,128)(2,1)S(1)}, bf16[16,2048]{1,0:T(8,128)(2,1)S(1)}, u32[]{:S(2)}, u32[]{:S(2)}) %collective-permute-start.11) | collective-permute-done | bytes 65568 | tf_op jit(solution)/shard_map/ppermute | solution.py:308
  (28 shorter events, 6.9 us)
Async XLA Ops:
  0.6 37.2 %copy-start = (f32[128,128]{1,0:T(8,128)S(1)}, f32[128,128]{1,0:T(8,128)}, u32[]{:S(2)}) copy-start(f32[128,128]{1,0:T(8,128)} %refs_11_.1) | copy-start | bytes 196612
  0.6 0.9 copy-start.2
  1.6 0.8 copy-start.3
  3.6 43.1 %copy-start.4 = (s32[6,2,8,128]{3,2,1,0:T(8,128)S(1)}, s32[6,2,8,128]{3,2,1,0:T(8,128)}, u32[]{:S(2)}) copy-start(s32[6,2,8,128]{3,2,1,0:T(8,128)} %refs_5_.1) | copy-start | bytes 147460
  3.6 37.5 %all-to-all-start = ((bf16[16,8,4096]{2,1,0:T(8,128)(2,1)}), bf16[16,8,4096]{2,1,0:T(8,128)(2,1)S(1)}, u32[]{:S(2)}, u32[]{:S(2)}) async-start(bf16[16,8,4096]{2,1,0:T(8,128)(2,1)} %bitcast.22), calls=%async_computation | async-start | bytes 2097152 | tf_op jit(solution)/shard_map/all_to_all | solution.py:239
  10.2 17.2 %collective-permute-start = (bf16[16,2048]{1,0:T(8,128)(2,1)S(1)}, bf16[16,2048]{1,0:T(8,128)(2,1)S(1)}, u32[]{:S(2)}, u32[]{:S(2)}) collective-permute-start(bf16[16,2048]{1,0:T(8,128)(2,1)S(1)} %get-tuple-element.24.refs_1_), channel_id=1, source_target_pairs={{0,1},{1,0},{2,3},{3,2},{4,5},{5,4},{6,7},{7,6},{8,9},{9,8},{10,11... | collective-permute-start | bytes 196616 | tf_op jit(solution)/shard_map/ppermute | solution.py:240
  27.4 7.5 %collective-permute-start.3 = (bf16[32,2048]{1,0:T(8,128)(2,1)S(1)}, bf16[32,2048]{1,0:T(8,128)(2,1)S(1)}, u32[]{:S(2)}, u32[]{:S(2)}) collective-permute-start(bf16[32,2048]{1,0:T(8,128)(2,1)S(1)} %constant_dynamic-update-slice_fusion), channel_id=1, source_target_pairs={{0,4},{2,6},{4,0},{6,2},{1,5},{3,7},{5,1},{7,3},{8,12},{10,14},{12... | collective-permute-start | bytes 393224 | tf_op jit(solution)/shard_map/ppermute | solution.py:242
  30.6 6.8 %collective-permute-start.2 = (bf16[32,2048]{1,0:T(8,128)(2,1)S(1)}, bf16[32,2048]{1,0:T(8,128)(2,1)S(1)}, u32[]{:S(2)}, u32[]{:S(2)}) collective-permute-start(bf16[32,2048]{1,0:T(8,128)(2,1)S(1)} %constant_dynamic-update-slice_fusion), channel_id=1, source_target_pairs={{0,6},{2,0},{4,2},{6,4},{1,7},{3,1},{5,3},{7,5},{8,14},{10,8},{12,... | collective-permute-start | bytes 393224 | tf_op jit(solution)/shard_map/ppermute | solution.py:242
  31.6 6.2 %collective-permute-start.1 = (bf16[32,2048]{1,0:T(8,128)(2,1)S(1)}, bf16[32,2048]{1,0:T(8,128)(2,1)S(1)}, u32[]{:S(2)}, u32[]{:S(2)}) collective-permute-start(bf16[32,2048]{1,0:T(8,128)(2,1)S(1)} %constant_dynamic-update-slice_fusion), channel_id=1, source_target_pairs={{0,2},{2,4},{4,6},{6,0},{1,3},{3,5},{5,7},{7,1},{8,10},{10,12},{12... | collective-permute-start | bytes 393224 | tf_op jit(solution)/shard_map/ppermute | solution.py:242
  39.5 7.2 %collective-permute-start.4 = (bf16[128,2048]{1,0:T(8,128)(2,1)S(1)}, bf16[128,2048]{1,0:T(8,128)(2,1)S(1)}, u32[]{:S(2)}, u32[]{:S(2)}) collective-permute-start(bf16[128,2048]{1,0:T(8,128)(2,1)S(1)} %get-tuple-element.25.refs_1_.refs_6_.refs_7_.refs_2_), channel_id=1, source_target_pairs={{0,8},{8,0},{1,9},{9,1},{2,10},{10,2},{3,11},{11,3},{4,12},{12,4},... | collective-permute-start | bytes 1572872 | tf_op jit(solution)/shard_map/ppermute | solution.py:249
  39.5 7.2 %collective-permute-start.5 = (bf16[128,1024]{1,0:T(8,128)(2,1)}, bf16[128,1024]{1,0:T(8,128)(2,1)S(1)}, u32[]{:S(2)}, u32[]{:S(2)}) collective-permute-start(bf16[128,1024]{1,0:T(8,128)(2,1)} %get-tuple-element.27), channel_id=1, source_target_pairs={{8,16},{24,32},{40,48},{56,64},{72,80},{88,96},{104,112},{16,8},{3... | collective-permute-start | bytes 786440 | tf_op jit(solution)/shard_map/ppermute | solution.py:252
  60.6 7.2 %collective-permute-start.6 = (bf16[128,2048]{1,0:T(8,128)(2,1)S(1)}, bf16[128,2048]{1,0:T(8,128)(2,1)S(1)}, u32[]{:S(2)}, u32[]{:S(2)}) collective-permute-start(bf16[128,2048]{1,0:T(8,128)(2,1)S(1)} %get-tuple-element.35.refs_6_), channel_id=1, source_target_pairs={{0,8},{8,0},{1,9},{9,1},{2,10},{10,2},{3,11},{11,3},{4,12},{12,4},... | collective-permute-start | bytes 1572872 | tf_op jit(solution)/shard_map/ppermute | solution.py:278
  64.6 3.3 %collective-permute-start.7 = (f32[128,128]{1,0:T(8,128)S(1)}, f32[128,128]{1,0:T(8,128)S(1)}, u32[]{:S(2)}, u32[]{:S(2)}) collective-permute-start(f32[128,128]{1,0:T(8,128)S(1)} %get-tuple-element.38.refs_9_), channel_id=1, source_target_pairs={{0,8},{8,0},{1,9},{9,1},{2,10},{10,2},{3,11},{11,3},{4,12},{12,4},... | collective-permute-start | bytes 196616 | tf_op jit(solution)/shard_map/ppermute | solution.py:270
  73.0 21.2 %copy-start.1 = (f32[16,2048]{1,0:T(8,128)S(1)}, f32[16,2048]{1,0:T(8,128)}, u32[]{:S(2)}) copy-start(f32[16,2048]{1,0:T(8,128)} %get-tuple-element.32.refs_0_) | copy-start | bytes 393220
  73.0 22.0 %all-to-all-start.1 = ((bf16[16,8,4096]{2,1,0:T(8,128)(2,1)}), bf16[16,8,4096]{2,1,0:T(8,128)(2,1)S(1)}, u32[]{:S(2)}, u32[]{:S(2)}) async-start(bf16[16,8,4096]{2,1,0:T(8,128)(2,1)} %bitcast.23), calls=%async_computation.1 | async-start | bytes 2097152 | tf_op jit(solution)/shard_map/all_to_all | solution.py:294
  77.7 7.0 %collective-permute-start.8 = (bf16[32,2048]{1,0:T(8,128)(2,1)S(1)}, bf16[32,2048]{1,0:T(8,128)(2,1)S(1)}, u32[]{:S(2)}, u32[]{:S(2)}) collective-permute-start(bf16[32,2048]{1,0:T(8,128)(2,1)S(1)} %get-tuple-element.40), channel_id=1, source_target_pairs={{0,2},{2,4},{4,6},{6,0},{1,3},{3,5},{5,7},{7,1},{8,10},{10,12},{12... | collective-permute-start | bytes 393224 | tf_op jit(solution)/shard_map/ppermute | solution.py:298
  78.3 8.5 %collective-permute-start.9 = (bf16[32,2048]{1,0:T(8,128)(2,1)S(1)}, bf16[32,2048]{1,0:T(8,128)(2,1)S(1)}, u32[]{:S(2)}, u32[]{:S(2)}) collective-permute-start(bf16[32,2048]{1,0:T(8,128)(2,1)S(1)} %get-tuple-element.41), channel_id=1, source_target_pairs={{0,6},{2,0},{4,2},{6,4},{1,7},{3,1},{5,3},{7,5},{8,14},{10,8},{12,... | collective-permute-start | bytes 393224 | tf_op jit(solution)/shard_map/ppermute | solution.py:298
  81.0 6.7 %collective-permute-start.10 = (bf16[32,2048]{1,0:T(8,128)(2,1)S(1)}, bf16[32,2048]{1,0:T(8,128)(2,1)S(1)}, u32[]{:S(2)}, u32[]{:S(2)}) collective-permute-start(bf16[32,2048]{1,0:T(8,128)(2,1)S(1)} %get-tuple-element.42), channel_id=1, source_target_pairs={{0,4},{2,6},{4,0},{6,2},{1,5},{3,7},{5,1},{7,3},{8,12},{10,14},{12... | collective-permute-start | bytes 393224 | tf_op jit(solution)/shard_map/ppermute | solution.py:298
  88.4 5.8 %collective-permute-start.11 = (bf16[16,2048]{1,0:T(8,128)(2,1)S(1)}, bf16[16,2048]{1,0:T(8,128)(2,1)S(1)}, u32[]{:S(2)}, u32[]{:S(2)}) collective-permute-start(bf16[16,2048]{1,0:T(8,128)(2,1)S(1)} %get-tuple-element.44), channel_id=1, source_target_pairs={{0,1},{1,0},{2,3},{3,2},{4,5},{5,4},{6,7},{7,6},{8,9},{9,8},{10,11... | collective-permute-start | bytes 196616 | tf_op jit(solution)/shard_map/ppermute | solution.py:308
where the time goes:
time: 96.3 us; the launch traced here: 95.8 us
  Pallas kernels  31.7 us (33%)
  starting transfers between devices  30.6 us (32%)
  waiting for transfers between devices  29.2 us (30%)
  local copies, waits for them, and re-layouts  1.79 us (2%)
  other arithmetic  1.64 us (2%)
    pallas_call x9, Pallas kernels, small(): pl.pallas_call(reading, in_specs=[pl.BlockSpec(memory_space=pltpu.SMEM)]...  31.7 us
    ppermute x1, waiting for transfers between devices, per_device(): u1 = lax.ppermute(u0, 'xh', swap)  14.4 us
    all_to_all x1, starting transfers between devices, per_device(): lax.all_to_all(v_wide.reshape(rank, half), SPACE, 0, 0, tiled=True)  6.59 us
    ppermute x3, waiting for transfers between devices, per_device(): lax.ppermute(part, 'y', ring(4, k))  5.89 us
    ppermute x3, starting transfers between devices, per_device(): around = [resident(lax.ppermute(pair, 'y', ring(4, k))) for k in (1, 3, 2)]  5.22 us
    ppermute x3, waiting for transfers between devices, per_device(): around = [resident(lax.ppermute(pair, 'y', ring(4, k))) for k in (1, 3, 2)]  5.13 us
    all_to_all x1, starting transfers between devices, per_device(): l_got = lax.all_to_all(l_part, SPACE, 0, 0, tiled=True)  4.75 us
    ppermute x3, starting transfers between devices, per_device(): lax.ppermute(part, 'y', ring(4, k))  4.1 us
  transfers between devices with their start and end apart: 14, of which 8 were waited for; matrix products, arithmetic and copies ran while one was open for 1% of the time, Pallas kernels for 12%

commit v1 on v0

v1 whole, which is shorter than its diff:
```python
import functools

import jax
import jax.numpy as jnp
from jax import lax
from jax.experimental import pallas as pl
from jax.experimental.pallas import tpu as pltpu
from jax.sharding import Mesh, PartitionSpec as P

step_size = 0.1
SPACE = ("z", "xl", "c")
SAMP = ("y", "xh")
BLOCK = 2048
bf16, f32 = jnp.bfloat16, jnp.float32


def dot(a, b, ca, cb):
    return lax.dot_general(a, b, (((ca,), (cb,)), ((), ())), preferred_element_type=f32)


def resident(x):
    return pltpu.with_memory_space_constraint(x, pltpu.MemorySpace.VMEM)


def small(body, args, outs, scratch=(), at=None, held=(), limit=24):
    vm = pl.BlockSpec(memory_space=pltpu.VMEM)
    scalars = [] if at is None else [at]
    n_read = len(scalars) + len(args)

    def reading(*refs):
        body(*refs[:n_read], *refs[n_read + len(held) :])

    return pl.pallas_call(
        reading,
        in_specs=[pl.BlockSpec(memory_space=pltpu.SMEM)] * len(scalars)
        + [vm] * (len(args) + len(held)),
        out_specs=[vm] * len(outs),
        out_shape=[(pltpu.VMEM if keep else pltpu.HBM)(shape, dtype) for shape, dtype, keep in outs],
        scratch_shapes=[pltpu.VMEM(shape, dtype) for shape, dtype in scratch],
        compiler_params=pltpu.CompilerParams(vmem_limit_bytes=limit << 20),
    )(*scalars, *args, *held)


def head_body(at_ref, u_hbm, v_hbm, flat_ref, keep_ref, send_ref, u_s, w_s, v_s, sems):
    fetch = [pltpu.make_async_copy(v_hbm, v_s, sems.at[0]), pltpu.make_async_copy(u_hbm, u_s, sems.at[1])]
    for copy in fetch:
        copy.start()
    half = keep_ref.shape[1]
    first = at_ref[0] == 0
    fetch[0].wait()

    @pl.when(first)
    def _():
        keep_ref[...] = v_s[:, :half]
        send_ref[...] = v_s[:, half:]

    @pl.when(jnp.logical_not(first))
    def _():
        keep_ref[...] = v_s[:, half:]
        send_ref[...] = v_s[:, :half]

    fetch[1].wait()
    _, depth, rows, cols = u_s.shape
    w_s[...] = u_s[...].astype(f32)
    for x in range(depth):
        for y in range(rows):
            at = (x * rows + y) * cols
            flat_ref[:, at : at + cols] = w_s[:, x, y, :].astype(bf16)


def stack_body(which, at_ref, mine_ref, got_ref, *outs):
    rows = mine_ref.shape[0]
    width = outs[0].shape[1]

    def put(top_ref, low_ref):
        for i, out_ref in enumerate(outs):
            out_ref[:rows, :] = top_ref[:, i * width : (i + 1) * width]
            out_ref[rows:, :] = low_ref[:, i * width : (i + 1) * width]

    first = at_ref[which] == 0

    @pl.when(first)
    def _():
        put(mine_ref, got_ref)

    @pl.when(jnp.logical_not(first))
    def _():
        put(got_ref, mine_ref)


def gather_rows(z, pieces, v_ref):
    rows = pieces[0].shape[0]
    for turn, piece in zip((0, 3, 1, 2), pieces):
        v_ref[pl.ds(pl.multiple_of(((z + turn) % 4) * rows, rows), rows), :] = piece[...]


def prep_body(at_ref, p0, p1, p2, p3, core_ref, full_ref, k_ref, kt_ref, halo_ref):
    half = full_ref.shape[1] // 2
    gather_rows(at_ref[2], (p0, p1, p2, p3), full_ref)
    k_own = dot(core_ref[...].astype(bf16), full_ref[...], 0, 0).astype(bf16)
    k_ref[...] = k_own
    kt_ref[...] = k_own.T
    first = at_ref[0] == 0

    @pl.when(first)
    def _():
        halo_ref[...] = k_own[:, :half]

    @pl.when(jnp.logical_not(first))
    def _():
        halo_ref[...] = k_own[:, half:]


def mid_body(rows, cols, c_ref, oth_ref, core_ref, k_ref, halo_ref, face_ref, u_ref, kt_ref, base_ref, m_ref, base_s, lap_s):
    half = oth_ref.shape[1] // 2
    k_oth = dot(core_ref[...].astype(bf16), oth_ref[...], 0, 0).astype(bf16)
    kt_ref[...] = k_oth.T
    first = c_ref[0] == 0
    near = jnp.where(first, k_oth[:, :half].astype(f32), k_oth[:, half:].astype(f32))
    halo = halo_ref[...].astype(f32)
    before = jnp.where(first, halo, near)
    after = jnp.where(first, near, halo)
    plane = rows * cols
    lane = lax.broadcasted_iota(jnp.int32, (1, cols), 1)
    for x in range(2):
        for y in range(rows):
            at = (x * rows + y) * cols
            mid = k_ref[:, at : at + cols].astype(f32)
            w = [0.25 * lax.shift_left(1, face_ref[f, x, y : y + 1, :]).astype(f32) for f in range(6)]
            total = ((w[0] + w[1]) + (w[2] + w[3])) + (w[4] + w[5])
            down = before[:, y * cols : (y + 1) * cols] if x == 0 else k_ref[:, at - plane : at - plane + cols].astype(f32)
            up = after[:, y * cols : (y + 1) * cols] if x == 1 else k_ref[:, at + plane : at + plane + cols].astype(f32)
            out = w[0] * down + w[1] * up - total * mid
            if y > 0:
                out += w[2] * k_ref[:, at - cols : at].astype(f32)
            if y < rows - 1:
                out += w[3] * k_ref[:, at + cols : at + 2 * cols].astype(f32)
            out += jnp.where(lane == 0, 0.0, w[4]) * pltpu.roll(mid, 1, 1)
            out += jnp.where(lane == cols - 1, 0.0, w[5]) * pltpu.roll(mid, cols - 1, 1)
            base_s[:, at : at + cols] = mid + step_size * out
            lap_s[:, at : at + cols] = out.astype(bf16)
    base_ref[...] = base_s[pl.ds(pl.multiple_of(c_ref[1] * base_ref.shape[0], 8), base_ref.shape[0]), :]
    m_ref[...] = dot(u_ref[...], lap_s[...], 1, 1)


def sweep(kt_ref, u_ref, v_ref, g_ref, ov_ref, store, start=0, stop=None, tile=512):
    stop = v_ref.shape[1] if stop is None else stop
    block = min(BLOCK, stop - start)
    for at in range(start, stop, block):
        v = v_ref[:, at : at + block]
        g = g_ref[:, at : at + block]
        acc = None
        for row in range(0, u_ref.shape[1], tile):
            field = dot(kt_ref[row : row + tile, :], v, 1, 0)
            react = (field * (g - field * field)).astype(bf16)
            ov_ref[row : row + tile, :] += dot(react, v, 1, 1)
            part = dot(u_ref[:, row : row + tile], react, 1, 0)
            acc = part if acc is None else acc + part
        store(at, block, acc)


def own_body(at_ref, kt_ref, u_ref, g_ref, p0, p1, p2, p3, l_ref, ov_ref, v_ref):
    gather_rows(at_ref[4], (p0, p1, p2, p3), v_ref)
    ov_ref[...] = jnp.zeros_like(ov_ref)

    def store(at, size, acc):
        l_ref[:, at : at + size] = acc

    sweep(kt_ref, u_ref, v_ref, g_ref, ov_ref, store)


def oth_body(at_ref, kt_ref, u_ref, g0_ref, g1_ref, v0_ref, old_ref, p0, p1, p2, p3, l0_ref, l1_ref, send_ref, v1_ref, ov_s):
    gather_rows(at_ref[4], (p0, p1, p2, p3), v1_ref)
    ov_s[...] = jnp.zeros_like(ov_s)

    def store0(at, size, acc):
        l0_ref[:, at : at + size] = old_ref[:, at : at + size] + acc

    def store1(at, size, acc):
        l1_ref[:, at : at + size] = acc

    sweep(kt_ref, u_ref, v0_ref, g0_ref, ov_s, store0)
    sweep(kt_ref, u_ref, v1_ref, g1_ref, ov_s, store1)
    send_ref[...] = ov_s[...].T.astype(bf16)


def last_body(
    scale, kt_ref, u_ref, g_ref, v0_ref, v1_ref, l0_ref, l1_ref, ov_old_ref, ma_ref, mb_ref, core_ref, out_ref, ov_ref, w_s
):
    rank = out_ref.shape[0]
    half = v0_ref.shape[1]
    ov_ref[...] = ov_old_ref[...]
    w = core_ref[...].astype(bf16).astype(f32) * 0.125 + scale * (ma_ref[...] + mb_ref[...])
    high = w.astype(bf16)
    w_s[:rank, :] = high
    w_s[rank:, :] = (w - high.astype(f32)).astype(bf16)

    def send(v, at, total):
        side = dot(w_s[...], v, 1, 0)
        out_ref[:, at : at + total.shape[1]] = (scale * total + (side[:rank] + side[rank:])).astype(bf16)

    send(v0_ref[...], 0, l0_ref[...])

    def store(at, size, acc):
        send(v1_ref[:, at : at + size], half + at, l1_ref[:, at : at + size] + acc)

    sweep(kt_ref, u_ref, v1_ref, g_ref, ov_ref, store)


def turn_body(at_ref, ov_ref, got_ref, me_ref, *refs):
    outs, tot_s = refs[:-1], refs[-1]
    tot_s[...] = ov_ref[...].T + got_ref[...].astype(f32)
    rows = me_ref.shape[0]
    n_samp = tot_s.shape[0] // rows

    def part(turn):
        return tot_s[pl.ds(pl.multiple_of(((at_ref[1] + turn) % n_samp) * rows, rows), rows), :]

    me_ref[...] = part(0)
    for turn, out_ref in enumerate(outs, 1):
        out_ref[...] = part(turn).astype(bf16)


def done_body(scale, base_ref, mine_ref, *refs):
    parts, out_ref = refs[:-1], refs[-1]
    _, depth, rows, cols = out_ref.shape
    total = mine_ref[...]
    for part in parts:
        total = total + part[...].astype(f32)
    new = base_ref[...] + scale * total
    for x in range(depth):
        for y in range(rows):
            at = (x * rows + y) * cols
            out_ref[:, x, y, :] = new[:, at : at + cols]


def send(x, axis, hops):
    return resident(lax.ppermute(x, axis, hops))


def ring(n, k):
    return [(i, (i + k) % n) for i in range(n)]


def per_device(basis_u, basis_v, core_s, face_class, sample_class):
    narrow, depth_x, rows_y, cols_z = basis_u.shape
    rank = core_s.shape[0]
    n_samp, n_space = 8, 16
    cells = depth_x * rows_y * cols_z
    lanes, samp_rows = basis_v.shape
    half = samp_rows // 2
    cell_weight = rank / (cells * n_space)
    samp_weight = rank / (samp_rows * n_samp)
    core_at = lax.axis_index("c")
    places = (core_at, lax.axis_index(SAMP)) + tuple(lax.axis_index(n) for n in ("y", "xh", "z", "xl"))
    where_at = jnp.stack(places).astype(jnp.int32)
    swap = ring(2, 1)

    quart = half // 2
    far = pl.BlockSpec(memory_space=pltpu.MemorySpace.HBM)
    vmem = pl.BlockSpec(memory_space=pltpu.VMEM)
    u0, v_keep, v_send = pl.pallas_call(
        head_body,
        in_specs=[pl.BlockSpec(memory_space=pltpu.SMEM), far, far],
        out_specs=[vmem] * 3,
        out_shape=[pltpu.VMEM((narrow, cells), bf16)] + [pltpu.VMEM((lanes, half), bf16)] * 2,
        scratch_shapes=[
            pltpu.VMEM(basis_u.shape, bf16),
            pltpu.VMEM(basis_u.shape, f32),
            pltpu.VMEM(basis_v.shape, bf16),
            pltpu.SemaphoreType.DMA((2,)),
        ],
        compiler_params=pltpu.CompilerParams(vmem_limit_bytes=24 << 20),
    )(where_at, basis_u, basis_v)
    u1 = send(u0, "xh", swap)
    v_got = send(v_send, "c", swap)
    (v_chip,) = small(functools.partial(stack_body, 0), [v_keep, v_got], [((2 * lanes, half), bf16, True)], at=where_at)
    v_next = send(v_chip, "xl", swap)
    v_mine = small(functools.partial(stack_body, 5), [v_chip, v_next], [((4 * lanes, quart), bf16, True)] * 2, at=where_at)
    v_pieces = [[m] + [send(m, "z", ring(4, k)) for k in (1, 3, 2)] for m in v_mine]
    (pair,) = small(functools.partial(stack_body, 3), [u0, u1], [((2 * narrow, cells), bf16, True)], at=where_at)
    around = [send(pair, "y", ring(4, k)) for k in (1, 3, 2)]
    u_own, k_own, kt_own, edge = small(
        prep_body,
        [pair, *around, core_s],
        [((rank, cells), bf16, True), ((rank, cells), bf16, True), ((cells, rank), bf16, True), ((rank, cells // 2), bf16, True)],
        at=where_at,
    )
    u_oth = send(u_own, "c", swap)
    chips = n_space // 2
    hops = [(2 * i + 1, 2 * i + 2) for i in range(chips - 1)] + [(2 * i + 2, 2 * i + 1) for i in range(chips - 1)]
    halo = send(edge, SPACE, hops)

    growth = 0.5 + 0.5 * lax.dynamic_slice_in_dim(sample_class, core_at * half, half, 0).astype(f32)
    growth = [resident(growth[i * quart : (i + 1) * quart].reshape(1, quart)) for i in range(2)]
    scale = step_size * cell_weight
    l_first, ov_first, v0 = small(
        own_body,
        [kt_own, u_own, growth[0], *v_pieces[0]],
        [((rank, quart), f32, True), ((cells, rank), f32, True), ((rank, quart), bf16, True)],
        at=where_at,
    )
    kt_oth, base, m_own = small(
        functools.partial(mid_body, rows_y, cols_z),
        [u_oth, core_s, k_own, halo, face_class, u_own],
        [((cells, rank), bf16, True), ((narrow, cells), f32, False), ((rank, rank), f32, True)],
        [((rank, cells), f32), ((rank, cells), bf16)],
        at=where_at,
        held=(ov_first, kt_own, l_first),
    )
    m_oth = send(m_own, "c", swap)
    l0, l1, ov_send, v1 = small(
        oth_body,
        [kt_oth, u_oth, *growth, v0, l_first, *v_pieces[1]],
        [((rank, quart), f32, True), ((rank, quart), f32, True), ((rank, cells), bf16, True), ((rank, quart), bf16, True)],
        [((cells, rank), f32)],
        at=where_at,
        held=(ov_first, kt_own, u_own),
    )
    got = send(ov_send, "c", swap)
    l_part, ov_own = small(
        functools.partial(last_body, scale),
        [kt_own, u_own, growth[1], v0, v1, l0, l1, ov_first, m_own, m_oth, core_s],
        [((rank, half), bf16, False), ((cells, rank), f32, True)],
        [((2 * rank, rank), bf16)],
    )

    l_got = lax.all_to_all(l_part, SPACE, 0, 0, tiled=True)
    l_new = l_got.reshape(n_space // 2, 2, lanes, half).astype(f32).sum(0)
    l_new = jnp.transpose(l_new, (1, 0, 2)).reshape(lanes, samp_rows)

    me, *others = small(
        turn_body,
        [ov_own, got],
        [((narrow, cells), f32, True)] + [((narrow, cells), bf16, True)] * (n_samp - 1),
        [((rank, cells), f32)],
        at=where_at,
    )
    sums = [send(part, SAMP, ring(n_samp, turn)) for turn, part in enumerate(others, 1)]
    (k_new,) = small(
        functools.partial(done_body, step_size * samp_weight), [base, me, *sums], [(basis_u.shape, f32, False)]
    )
    return (k_new, l_new)


def solution(mesh):
    fine = Mesh(mesh.devices.reshape(4, 2, 2, 4, 2), SPACE + SAMP)
    return jax.shard_map(
        per_device,
        mesh=fine,
        in_specs=(P(SAMP, SPACE, None, None), P(SPACE, SAMP), P(), P(None, SPACE, None, None), P(SAMP)),
        out_specs=(P(SAMP, SPACE, None, None), P(SPACE, SAMP)),
        check_vma=False,
    )
```

time: 96.3 us -> 102 us (1.059)
  starting transfers between devices: 30.6 us -> 42.2 us
  waiting for transfers between devices: 29.2 us -> 22.2 us
  Pallas kernels: 31.7 us -> 33.3 us
    ppermute x12 -> x23, starting transfers between devices: 19.3 us -> 37.7 us  [send(): return resident(lax.ppermute(x, axis, hops))]
    ppermute x12 -> x23, waiting for transfers between devices: 29.2 us -> 22.2 us  [send(): return resident(lax.ppermute(x, axis, hops))]
    all_to_all x1 -> x0, starting transfers between devices: 6.59 us -> none  [per_device(): lax.all_to_all(v_wide.reshape(rank, half), SPACE, 0, 0, tiled=True)]
    unnamed x11 -> x14, local copies, waits for them, and re-layouts: 1.78 us -> 2.61 us
    pallas_call x9 -> x10, Pallas kernels: 31.7 us -> 32.3 us  [small(): pl.pallas_call(reading, in_specs=[pl.BlockSpec(memory_space=pltpu.SMEM)]...]
  transfers between devices with their start and end apart: 14 -> 24, of which waited for: 8 -> 10; matrix products, arithmetic and copies ran while one was open for 1% -> 0% of each run, Pallas kernels for 12% -> 24%
where the time goes in v1:
time: 102 us
  starting transfers between devices  42.2 us (41%)
  Pallas kernels  33.3 us (33%)
  waiting for transfers between devices  22.2 us (22%)
  local copies, waits for them, and re-layouts  2.7 us (3%)
    ppermute x23, starting transfers between devices, send(): return resident(lax.ppermute(x, axis, hops))  37.7 us
    pallas_call x10, Pallas kernels, small(): pl.pallas_call(reading, in_specs=[pl.BlockSpec(memory_space=pltpu.SMEM)]...  32.3 us
    ppermute x23, waiting for transfers between devices, send(): return resident(lax.ppermute(x, axis, hops))  22.2 us
    all_to_all x1, starting transfers between devices, per_device(): l_got = lax.all_to_all(l_part, SPACE, 0, 0, tiled=True)  4.51 us
    unnamed x14, local copies, waits for them, and re-layouts  2.61 us
  transfers between devices with their start and end apart: 24, of which 10 were waited for; matrix products, arithmetic and copies ran while one was open for 0% of the time, Pallas kernels for 24%

profile of v1, /device:TPU:0, one launch (start us, length us, event | category | flops | bytes accessed | tf_op | source)
XLA Modules:
  0.0 102.0 jit_solution(3189275647991960699)
XLA Ops:
  3.5 3.2 %collective-permute-start = (bf16[16,2048]{1,0:T(8,128)(2,1)S(1)}, bf16[16,2048]{1,0:T(8,128)(2,1)S(1)}, u32[]{:S(2)}, u32[]{:S(2)}) collective-permute-start(bf16[16,2048]{1,0:T(8,128)(2,1)S(1)} %get-tuple-element.31.refs_1_), channel_id=1, source_target_pairs={{0,1},{1,0},{2,3},{3,2},{4,5},{5,4},{6,7},{7,6},{8,9},{9,8},{10,11... | collective-permute-start | bytes 196616 | tf_op jit(solution)/shard_map/ppermute | solution.py:238
  6.7 2.6 %collective-permute-done.refs_2_ = bf16[16,2048]{1,0:T(8,128)(2,1)S(1)} collective-permute-done((bf16[16,2048]{1,0:T(8,128)(2,1)S(1)}, bf16[16,2048]{1,0:T(8,128)(2,1)S(1)}, u32[]{:S(2)}, u32[]{:S(2)}) %collective-permute-start) | collective-permute-done | bytes 65568 | tf_op jit(solution)/shard_map/ppermute | solution.py:238
  9.9 1.8 %collective-permute-start.1 = (bf16[32,2048]{1,0:T(8,128)(2,1)S(1)}, bf16[32,2048]{1,0:T(8,128)(2,1)S(1)}, u32[]{:S(2)}, u32[]{:S(2)}) collective-permute-start(bf16[32,2048]{1,0:T(8,128)(2,1)S(1)} %shard_map.69.refs_1_), channel_id=1, source_target_pairs={{0,2},{2,4},{4,6},{6,0},{1,3},{3,5},{5,7},{7,1},{8,10},{10,12},{12... | collective-permute-start | bytes 393224 | tf_op jit(solution)/shard_map/ppermute | solution.py:238
  13.2 2.1 %collective-permute-start.3 = (bf16[32,2048]{1,0:T(8,128)(2,1)S(1)}, bf16[32,2048]{1,0:T(8,128)(2,1)S(1)}, u32[]{:S(2)}, u32[]{:S(2)}) collective-permute-start(bf16[32,2048]{1,0:T(8,128)(2,1)S(1)} %shard_map.69.refs_1_), channel_id=1, source_target_pairs={{0,4},{2,6},{4,0},{6,2},{1,5},{3,7},{5,1},{7,3},{8,12},{10,14},{12... | collective-permute-start | bytes 393224 | tf_op jit(solution)/shard_map/ppermute | solution.py:238
  15.3 1.7 %collective-permute-done.1.refs_2_ = bf16[32,2048]{1,0:T(8,128)(2,1)S(1)} collective-permute-done((bf16[32,2048]{1,0:T(8,128)(2,1)S(1)}, bf16[32,2048]{1,0:T(8,128)(2,1)S(1)}, u32[]{:S(2)}, u32[]{:S(2)}) %collective-permute-start.1) | collective-permute-done | bytes 131104 | tf_op jit(solution)/shard_map/ppermute | solution.py:238
  17.5 2.4 %collective-permute-done.3.refs_4_ = bf16[32,2048]{1,0:T(8,128)(2,1)S(1)} collective-permute-done((bf16[32,2048]{1,0:T(8,128)(2,1)S(1)}, bf16[32,2048]{1,0:T(8,128)(2,1)S(1)}, u32[]{:S(2)}, u32[]{:S(2)}) %collective-permute-start.3) | collective-permute-done | bytes 131104 | tf_op jit(solution)/shard_map/ppermute | solution.py:238
  23.9 4.4 %collective-permute-done.7.refs_2_ = bf16[16,4096]{1,0:T(8,128)(2,1)S(1)} collective-permute-done((bf16[16,4096]{1,0:T(8,128)(2,1)S(1)}, bf16[16,4096]{1,0:T(8,128)(2,1)S(1)}, u32[]{:S(2)}, u32[]{:S(2)}) %collective-permute-start.7) | collective-permute-done | bytes 131104 | tf_op jit(solution)/shard_map/ppermute | solution.py:238
  28.9 4.0 %collective-permute-start.10 = (bf16[32,2048]{1,0:T(8,128)(2,1)S(1)}, bf16[32,2048]{1,0:T(8,128)(2,1)S(1)}, u32[]{:S(2)}, u32[]{:S(2)}) collective-permute-start(bf16[32,2048]{1,0:T(8,128)(2,1)S(1)} %get-tuple-element.38.refs_4_), channel_id=1, source_target_pairs={{0,64},{32,96},{64,0},{96,32},{1,65},{33,97},{65,1},{97,33},{2,66}... | collective-permute-start | bytes 393224 | tf_op jit(solution)/shard_map/ppermute | solution.py:238
  33.9 2.2 %collective-permute-start.9 = (bf16[32,2048]{1,0:T(8,128)(2,1)S(1)}, bf16[32,2048]{1,0:T(8,128)(2,1)S(1)}, u32[]{:S(2)}, u32[]{:S(2)}) collective-permute-start(bf16[32,2048]{1,0:T(8,128)(2,1)S(1)} %get-tuple-element.38.refs_4_), channel_id=1, source_target_pairs={{0,96},{32,0},{64,32},{96,64},{1,97},{33,1},{65,33},{97,65},{2,98}... | collective-permute-start | bytes 393224 | tf_op jit(solution)/shard_map/ppermute | solution.py:238
  37.2 2.2 %collective-permute-start.11 = (bf16[32,2048]{1,0:T(8,128)(2,1)S(1)}, bf16[32,2048]{1,0:T(8,128)(2,1)S(1)}, u32[]{:S(2)}, u32[]{:S(2)}) collective-permute-start(bf16[32,2048]{1,0:T(8,128)(2,1)S(1)} %get-tuple-element.44.refs_7_), channel_id=1, source_target_pairs={{0,32},{32,64},{64,96},{96,0},{1,33},{33,65},{65,97},{97,1},{2,34}... | collective-permute-start | bytes 393224 | tf_op jit(solution)/shard_map/ppermute | solution.py:238
  40.9 1.9 %collective-permute-start.13 = (bf16[32,2048]{1,0:T(8,128)(2,1)S(1)}, bf16[32,2048]{1,0:T(8,128)(2,1)S(1)}, u32[]{:S(2)}, u32[]{:S(2)}) collective-permute-start(bf16[32,2048]{1,0:T(8,128)(2,1)S(1)} %get-tuple-element.44.refs_7_), channel_id=1, source_target_pairs={{0,64},{32,96},{64,0},{96,32},{1,65},{33,97},{65,1},{97,33},{2,66}... | collective-permute-start | bytes 393224 | tf_op jit(solution)/shard_map/ppermute | solution.py:238
  42.8 6.2 %shard_map.73 = (f32[128,2048]{1,0:T(8,128)S(1)}, f32[2048,128]{1,0:T(8,128)S(1)}, bf16[128,2048]{1,0:T(8,128)(2,1)S(1)}) custom-call(s32[6]{0:T(128)S(1)} %stack.27.at_ref.refs_0_, bf16[2048,128]{1,0:T(8,128)(2,1)S(1)} %get-tuple-element.35.refs_1_.refs_8_.refs_12_.refs_0_, bf16[128,2048]{1,0:T(8,128)(2,1)S(1)} %get-tuple-element.32.refs_2_.refs_6_.refs_13_.refs_1_, ...), custom_call_target="tpu_custom_call" | custom-call | tf_op jit(solution)/shard_map/pallas_call | solution.py:33
  49.1 2.5 %shard_map.74 = (bf16[2048,128]{1,0:T(8,128)(2,1)S(1)}, f32[16,2048]{1,0:T(8,128)}, f32[128,128]{1,0:T(8,128)S(1)}) custom-call(s32[6]{0:T(128)S(1)} %stack.27.at_ref.refs_0_, bf16[128,2048]{1,0:T(8,128)(2,1)S(1)} %collective-permute-done.4.refs_1_.refs_2_, f32[128,128]{1,0:T(8,128)S(1)} %copy-done.1, bf16[128,2048]{1,0:T(8,128)(2,1)S(1)} %get-tuple-element.33.refs_3_, ...), custom_call_target="tpu_custom_call" | custom-call | tf_op jit(solution)/shard_map/pallas_call | solution.py:33
  51.5 11.8 %shard_map.75 = (f32[128,2048]{1,0:T(8,128)S(1)}, f32[128,2048]{1,0:T(8,128)S(1)}, bf16[128,2048]{1,0:T(8,128)(2,1)S(1)}, bf16[128,2048]{1,0:T(8,128)(2,1)S(1)}) custom-call(s32[6]{0:T(128)S(1)} %stack.27.at_ref.refs_0_, bf16[2048,128]{1,0:T(8,128)(2,1)S(1)} %get-tuple-element.43.refs_1_, bf16[128,2048]{1,0:T(8,128)(2,1)S(1)} %collective-permute-done.4.refs_1_.refs_2_, ...), custom_call_target="tpu_custom_call" | custom-call | tf_op jit(solution)/shard_map/pallas_call | solution.py:33
  63.3 7.5 %shard_map.76 = (bf16[128,4096]{1,0:T(8,128)(2,1)}, f32[2048,128]{1,0:T(8,128)S(1)}) custom-call(bf16[2048,128]{1,0:T(8,128)(2,1)S(1)} %get-tuple-element.35.refs_1_.refs_8_.refs_12_.refs_0_, bf16[128,2048]{1,0:T(8,128)(2,1)S(1)} %get-tuple-element.32.refs_2_.refs_6_.refs_13_.refs_1_, f32[1,2048]{1,0:T(1,128)S(1)} %bitcast.15, ...), custom_call_target="tpu_custom_call" | custom-call | tf_op jit(solution)/shard_map/pallas_call | solution.py:33
  70.8 4.5 %all-to-all-start = ((bf16[16,8,4096]{2,1,0:T(8,128)(2,1)}), bf16[16,8,4096]{2,1,0:T(8,128)(2,1)S(1)}, u32[]{:S(2)}, u32[]{:S(2)}) async-start(bf16[16,8,4096]{2,1,0:T(8,128)(2,1)} %bitcast.19), calls=%async_computation | async-start | bytes 2097152 | tf_op jit(solution)/shard_map/all_to_all | solution.py:328
  75.8 1.6 %collective-permute-done.15.refs_2_ = bf16[128,2048]{1,0:T(8,128)(2,1)S(1)} collective-permute-done((bf16[128,2048]{1,0:T(8,128)(2,1)S(1)}, bf16[128,2048]{1,0:T(8,128)(2,1)S(1)}, u32[]{:S(2)}, u32[]{:S(2)}) %collective-permute-start.15) | collective-permute-done | bytes 524320 | tf_op jit(solution)/shard_map/ppermute | solution.py:238
  78.4 2.8 %collective-permute-start.16 = (bf16[16,2048]{1,0:T(8,128)(2,1)S(1)}, bf16[16,2048]{1,0:T(8,128)(2,1)S(1)}, u32[]{:S(2)}, u32[]{:S(2)}) collective-permute-start(bf16[16,2048]{1,0:T(8,128)(2,1)S(1)} %get-tuple-element.52), channel_id=1, source_target_pairs={{0,1},{1,2},{2,3},{3,4},{4,5},{5,6},{6,7},{7,0},{8,9},{9,10},{10,1... | collective-permute-start | bytes 196616 | tf_op jit(solution)/shard_map/ppermute | solution.py:238
  81.9 2.2 %collective-permute-start.18 = (bf16[16,2048]{1,0:T(8,128)(2,1)S(1)}, bf16[16,2048]{1,0:T(8,128)(2,1)S(1)}, u32[]{:S(2)}, u32[]{:S(2)}) collective-permute-start(bf16[16,2048]{1,0:T(8,128)(2,1)S(1)} %get-tuple-element.54), channel_id=1, source_target_pairs={{0,3},{1,4},{2,5},{3,6},{4,7},{5,0},{6,1},{7,2},{8,11},{9,12},{10,... | collective-permute-start | bytes 196616 | tf_op jit(solution)/shard_map/ppermute | solution.py:238
  84.1 2.2 %collective-permute-start.19 = (bf16[16,2048]{1,0:T(8,128)(2,1)S(1)}, bf16[16,2048]{1,0:T(8,128)(2,1)S(1)}, u32[]{:S(2)}, u32[]{:S(2)}) collective-permute-start(bf16[16,2048]{1,0:T(8,128)(2,1)S(1)} %get-tuple-element.55), channel_id=1, source_target_pairs={{0,4},{1,5},{2,6},{3,7},{4,0},{5,1},{6,2},{7,3},{8,12},{9,13},{10,... | collective-permute-start | bytes 196616 | tf_op jit(solution)/shard_map/ppermute | solution.py:238
  86.2 4.1 %collective-permute-start.20 = (bf16[16,2048]{1,0:T(8,128)(2,1)S(1)}, bf16[16,2048]{1,0:T(8,128)(2,1)S(1)}, u32[]{:S(2)}, u32[]{:S(2)}) collective-permute-start(bf16[16,2048]{1,0:T(8,128)(2,1)S(1)} %get-tuple-element.56), channel_id=1, source_target_pairs={{0,5},{1,6},{2,7},{3,0},{4,1},{5,2},{6,3},{7,4},{8,13},{9,14},{10,... | collective-permute-start | bytes 196616 | tf_op jit(solution)/shard_map/ppermute | solution.py:238
  90.4 3.6 %collective-permute-done.16.refs_2_ = bf16[16,2048]{1,0:T(8,128)(2,1)S(1)} collective-permute-done((bf16[16,2048]{1,0:T(8,128)(2,1)S(1)}, bf16[16,2048]{1,0:T(8,128)(2,1)S(1)}, u32[]{:S(2)}, u32[]{:S(2)}) %collective-permute-start.16) | collective-permute-done | bytes 65568 | tf_op jit(solution)/shard_map/ppermute | solution.py:238
  95.5 2.7 %collective-permute-done.21.refs_7_ = bf16[16,2048]{1,0:T(8,128)(2,1)S(1)} collective-permute-done((bf16[16,2048]{1,0:T(8,128)(2,1)S(1)}, bf16[16,2048]{1,0:T(8,128)(2,1)S(1)}, u32[]{:S(2)}, u32[]{:S(2)}) %collective-permute-start.21) | collective-permute-done | bytes 65568 | tf_op jit(solution)/shard_map/ppermute | solution.py:238
  98.2 2.2 %collective-permute-done.22.refs_8_ = bf16[16,2048]{1,0:T(8,128)(2,1)S(1)} collective-permute-done((bf16[16,2048]{1,0:T(8,128)(2,1)S(1)}, bf16[16,2048]{1,0:T(8,128)(2,1)S(1)}, u32[]{:S(2)}, u32[]{:S(2)}) %collective-permute-start.22) | collective-permute-done | bytes 65568 | tf_op jit(solution)/shard_map/ppermute | solution.py:238
  (53 shorter events, 18.8 us)
Async XLA Ops:
  3.5 5.8 %collective-permute-start = (bf16[16,2048]{1,0:T(8,128)(2,1)S(1)}, bf16[16,2048]{1,0:T(8,128)(2,1)S(1)}, u32[]{:S(2)}, u32[]{:S(2)}) collective-permute-start(bf16[16,2048]{1,0:T(8,128)(2,1)S(1)} %get-tuple-element.31.refs_1_), channel_id=1, source_target_pairs={{0,1},{1,0},{2,3},{3,2},{4,5},{5,4},{6,7},{7,6},{8,9},{9,8},{10,11... | collective-permute-start | bytes 196616 | tf_op jit(solution)/shard_map/ppermute | solution.py:238
  9.9 7.1 %collective-permute-start.1 = (bf16[32,2048]{1,0:T(8,128)(2,1)S(1)}, bf16[32,2048]{1,0:T(8,128)(2,1)S(1)}, u32[]{:S(2)}, u32[]{:S(2)}) collective-permute-start(bf16[32,2048]{1,0:T(8,128)(2,1)S(1)} %shard_map.69.refs_1_), channel_id=1, source_target_pairs={{0,2},{2,4},{4,6},{6,0},{1,3},{3,5},{5,7},{7,1},{8,10},{10,12},{12... | collective-permute-start | bytes 393224 | tf_op jit(solution)/shard_map/ppermute | solution.py:238
  11.6 5.8 %collective-permute-start.2 = (bf16[32,2048]{1,0:T(8,128)(2,1)S(1)}, bf16[32,2048]{1,0:T(8,128)(2,1)S(1)}, u32[]{:S(2)}, u32[]{:S(2)}) collective-permute-start(bf16[32,2048]{1,0:T(8,128)(2,1)S(1)} %shard_map.69.refs_1_), channel_id=1, source_target_pairs={{0,6},{2,0},{4,2},{6,4},{1,7},{3,1},{5,3},{7,5},{8,14},{10,8},{12,... | collective-permute-start | bytes 393224 | tf_op jit(solution)/shard_map/ppermute | solution.py:238
  13.2 6.7 %collective-permute-start.3 = (bf16[32,2048]{1,0:T(8,128)(2,1)S(1)}, bf16[32,2048]{1,0:T(8,128)(2,1)S(1)}, u32[]{:S(2)}, u32[]{:S(2)}) collective-permute-start(bf16[32,2048]{1,0:T(8,128)(2,1)S(1)} %shard_map.69.refs_1_), channel_id=1, source_target_pairs={{0,4},{2,6},{4,0},{6,2},{1,5},{3,7},{5,1},{7,3},{8,12},{10,14},{12... | collective-permute-start | bytes 393224 | tf_op jit(solution)/shard_map/ppermute | solution.py:238
  15.3 6.5 %collective-permute-start.6 = (bf16[8,4096]{1,0:T(8,128)(2,1)S(1)}, bf16[8,4096]{1,0:T(8,128)(2,1)S(1)}, u32[]{:S(2)}, u32[]{:S(2)}) collective-permute-start(bf16[8,4096]{1,0:T(8,128)(2,1)S(1)} %get-tuple-element.37), channel_id=1, source_target_pairs={{0,8},{8,0},{1,9},{9,1},{2,10},{10,2},{3,11},{11,3},{4,12},{12,4},... | collective-permute-start | bytes 196616 | tf_op jit(solution)/shard_map/ppermute | solution.py:238
  21.7 27.4 %collective-permute-start.4 = (bf16[128,2048]{1,0:T(8,128)(2,1)S(1)}, bf16[128,2048]{1,0:T(8,128)(2,1)S(1)}, u32[]{:S(2)}, u32[]{:S(2)}) collective-permute-start(bf16[128,2048]{1,0:T(8,128)(2,1)S(1)} %get-tuple-element.32.refs_2_.refs_6_.refs_13_.refs_1_), channel_id=1, source_target_pairs={{0,8},{8,0},{1,9},{9,1},{2,10},{10,2},{3,11},{11,3},{4,12},{12,4},... | collective-permute-start | bytes 1572872 | tf_op jit(solution)/shard_map/ppermute | solution.py:238
  22.4 6.0 %collective-permute-start.7 = (bf16[16,4096]{1,0:T(8,128)(2,1)S(1)}, bf16[16,4096]{1,0:T(8,128)(2,1)S(1)}, u32[]{:S(2)}, u32[]{:S(2)}) collective-permute-start(bf16[16,4096]{1,0:T(8,128)(2,1)S(1)} %shard_map.71.refs_1_), channel_id=1, source_target_pairs={{0,16},{16,0},{1,17},{17,1},{2,18},{18,2},{3,19},{19,3},{4,20},{20... | collective-permute-start | bytes 393224 | tf_op jit(solution)/shard_map/ppermute | solution.py:238
  28.9 8.3 %collective-permute-start.10 = (bf16[32,2048]{1,0:T(8,128)(2,1)S(1)}, bf16[32,2048]{1,0:T(8,128)(2,1)S(1)}, u32[]{:S(2)}, u32[]{:S(2)}) collective-permute-start(bf16[32,2048]{1,0:T(8,128)(2,1)S(1)} %get-tuple-element.38.refs_4_), channel_id=1, source_target_pairs={{0,64},{32,96},{64,0},{96,32},{1,65},{33,97},{65,1},{97,33},{2,66}... | collective-permute-start | bytes 393224 | tf_op jit(solution)/shard_map/ppermute | solution.py:238
  32.9 6.6 %collective-permute-start.8 = (bf16[32,2048]{1,0:T(8,128)(2,1)S(1)}, bf16[32,2048]{1,0:T(8,128)(2,1)S(1)}, u32[]{:S(2)}, u32[]{:S(2)}) collective-permute-start(bf16[32,2048]{1,0:T(8,128)(2,1)S(1)} %get-tuple-element.38.refs_4_), channel_id=1, source_target_pairs={{0,32},{32,64},{64,96},{96,0},{1,33},{33,65},{65,97},{97,1},{2,34}... | collective-permute-start | bytes 393224 | tf_op jit(solution)/shard_map/ppermute | solution.py:238
  33.9 7.0 %collective-permute-start.9 = (bf16[32,2048]{1,0:T(8,128)(2,1)S(1)}, bf16[32,2048]{1,0:T(8,128)(2,1)S(1)}, u32[]{:S(2)}, u32[]{:S(2)}) collective-permute-start(bf16[32,2048]{1,0:T(8,128)(2,1)S(1)} %get-tuple-element.38.refs_4_), channel_id=1, source_target_pairs={{0,96},{32,0},{64,32},{96,64},{1,97},{33,1},{65,33},{97,65},{2,98}... | collective-permute-start | bytes 393224 | tf_op jit(solution)/shard_map/ppermute | solution.py:238
  36.1 12.9 %collective-permute-start.5 = (bf16[128,1024]{1,0:T(8,128)(2,1)S(1)}, bf16[128,1024]{1,0:T(8,128)(2,1)S(1)}, u32[]{:S(2)}, u32[]{:S(2)}) collective-permute-start(bf16[128,1024]{1,0:T(8,128)(2,1)S(1)} %get-tuple-element.34), channel_id=1, source_target_pairs={{8,16},{24,32},{40,48},{56,64},{72,80},{88,96},{104,112},{16,8},{3... | collective-permute-start | bytes 786440 | tf_op jit(solution)/shard_map/ppermute | solution.py:238
  37.2 14.3 %collective-permute-start.11 = (bf16[32,2048]{1,0:T(8,128)(2,1)S(1)}, bf16[32,2048]{1,0:T(8,128)(2,1)S(1)}, u32[]{:S(2)}, u32[]{:S(2)}) collective-permute-start(bf16[32,2048]{1,0:T(8,128)(2,1)S(1)} %get-tuple-element.44.refs_7_), channel_id=1, source_target_pairs={{0,32},{32,64},{64,96},{96,0},{1,33},{33,65},{65,97},{97,1},{2,34}... | collective-permute-start | bytes 393224 | tf_op jit(solution)/shard_map/ppermute | solution.py:238
  39.4 12.1 %collective-permute-start.12 = (bf16[32,2048]{1,0:T(8,128)(2,1)S(1)}, bf16[32,2048]{1,0:T(8,128)(2,1)S(1)}, u32[]{:S(2)}, u32[]{:S(2)}) collective-permute-start(bf16[32,2048]{1,0:T(8,128)(2,1)S(1)} %get-tuple-element.44.refs_7_), channel_id=1, source_target_pairs={{0,96},{32,0},{64,32},{96,64},{1,97},{33,1},{65,33},{97,65},{2,98}... | collective-permute-start | bytes 393224 | tf_op jit(solution)/shard_map/ppermute | solution.py:238
  40.9 10.7 %collective-permute-start.13 = (bf16[32,2048]{1,0:T(8,128)(2,1)S(1)}, bf16[32,2048]{1,0:T(8,128)(2,1)S(1)}, u32[]{:S(2)}, u32[]{:S(2)}) collective-permute-start(bf16[32,2048]{1,0:T(8,128)(2,1)S(1)} %get-tuple-element.44.refs_7_), channel_id=1, source_target_pairs={{0,64},{32,96},{64,0},{96,32},{1,65},{33,97},{65,1},{97,33},{2,66}... | collective-permute-start | bytes 393224 | tf_op jit(solution)/shard_map/ppermute | solution.py:238
  51.5 11.8 %collective-permute-start.14 = (f32[128,128]{1,0:T(8,128)S(1)}, f32[128,128]{1,0:T(8,128)S(1)}, u32[]{:S(2)}, u32[]{:S(2)}) collective-permute-start(f32[128,128]{1,0:T(8,128)S(1)} %get-tuple-element.48.refs_8_), channel_id=1, source_target_pairs={{0,8},{8,0},{1,9},{9,1},{2,10},{10,2},{3,11},{11,3},{4,12},{12,4},... | collective-permute-start | bytes 196616 | tf_op jit(solution)/shard_map/ppermute | solution.py:238
  70.8 30.3 %all-to-all-start = ((bf16[16,8,4096]{2,1,0:T(8,128)(2,1)}), bf16[16,8,4096]{2,1,0:T(8,128)(2,1)S(1)}, u32[]{:S(2)}, u32[]{:S(2)}) async-start(bf16[16,8,4096]{2,1,0:T(8,128)(2,1)} %bitcast.19), calls=%async_computation | async-start | bytes 2097152 | tf_op jit(solution)/shard_map/all_to_all | solution.py:328
  75.4 2.1 %collective-permute-start.15 = (bf16[128,2048]{1,0:T(8,128)(2,1)S(1)}, bf16[128,2048]{1,0:T(8,128)(2,1)S(1)}, u32[]{:S(2)}, u32[]{:S(2)}) collective-permute-start(bf16[128,2048]{1,0:T(8,128)(2,1)S(1)} %get-tuple-element.50), channel_id=1, source_target_pairs={{0,8},{8,0},{1,9},{9,1},{2,10},{10,2},{3,11},{11,3},{4,12},{12,4},... | collective-permute-start | bytes 1572872 | tf_op jit(solution)/shard_map/ppermute | solution.py:238
  78.4 15.5 %collective-permute-start.16 = (bf16[16,2048]{1,0:T(8,128)(2,1)S(1)}, bf16[16,2048]{1,0:T(8,128)(2,1)S(1)}, u32[]{:S(2)}, u32[]{:S(2)}) collective-permute-start(bf16[16,2048]{1,0:T(8,128)(2,1)S(1)} %get-tuple-element.52), channel_id=1, source_target_pairs={{0,1},{1,2},{2,3},{3,4},{4,5},{5,6},{6,7},{7,0},{8,9},{9,10},{10,1... | collective-permute-start | bytes 196616 | tf_op jit(solution)/shard_map/ppermute | solution.py:238
  81.2 13.4 %collective-permute-start.17 = (bf16[16,2048]{1,0:T(8,128)(2,1)S(1)}, bf16[16,2048]{1,0:T(8,128)(2,1)S(1)}, u32[]{:S(2)}, u32[]{:S(2)}) collective-permute-start(bf16[16,2048]{1,0:T(8,128)(2,1)S(1)} %get-tuple-element.53), channel_id=1, source_target_pairs={{0,2},{1,3},{2,4},{3,5},{4,6},{5,7},{6,0},{7,1},{8,10},{9,11},{10,... | collective-permute-start | bytes 196616 | tf_op jit(solution)/shard_map/ppermute | solution.py:238
  81.9 13.6 %collective-permute-start.18 = (bf16[16,2048]{1,0:T(8,128)(2,1)S(1)}, bf16[16,2048]{1,0:T(8,128)(2,1)S(1)}, u32[]{:S(2)}, u32[]{:S(2)}) collective-permute-start(bf16[16,2048]{1,0:T(8,128)(2,1)S(1)} %get-tuple-element.54), channel_id=1, source_target_pairs={{0,3},{1,4},{2,5},{3,6},{4,7},{5,0},{6,1},{7,2},{8,11},{9,12},{10,... | collective-permute-start | bytes 196616 | tf_op jit(solution)/shard_map/ppermute | solution.py:238
  84.1 11.4 %collective-permute-start.19 = (bf16[16,2048]{1,0:T(8,128)(2,1)S(1)}, bf16[16,2048]{1,0:T(8,128)(2,1)S(1)}, u32[]{:S(2)}, u32[]{:S(2)}) collective-permute-start(bf16[16,2048]{1,0:T(8,128)(2,1)S(1)} %get-tuple-element.55), channel_id=1, source_target_pairs={{0,4},{1,5},{2,6},{3,7},{4,0},{5,1},{6,2},{7,3},{8,12},{9,13},{10,... | collective-permute-start | bytes 196616 | tf_op jit(solution)/shard_map/ppermute | solution.py:238
  86.2 9.2 %collective-permute-start.20 = (bf16[16,2048]{1,0:T(8,128)(2,1)S(1)}, bf16[16,2048]{1,0:T(8,128)(2,1)S(1)}, u32[]{:S(2)}, u32[]{:S(2)}) collective-permute-start(bf16[16,2048]{1,0:T(8,128)(2,1)S(1)} %get-tuple-element.56), channel_id=1, source_target_pairs={{0,5},{1,6},{2,7},{3,0},{4,1},{5,2},{6,3},{7,4},{8,13},{9,14},{10,... | collective-permute-start | bytes 196616 | tf_op jit(solution)/shard_map/ppermute | solution.py:238
  93.9 4.3 %collective-permute-start.21 = (bf16[16,2048]{1,0:T(8,128)(2,1)S(1)}, bf16[16,2048]{1,0:T(8,128)(2,1)S(1)}, u32[]{:S(2)}, u32[]{:S(2)}) collective-permute-start(bf16[16,2048]{1,0:T(8,128)(2,1)S(1)} %get-tuple-element.57), channel_id=1, source_target_pairs={{0,6},{1,7},{2,0},{3,1},{4,2},{5,3},{6,4},{7,5},{8,14},{9,15},{10,... | collective-permute-start | bytes 196616 | tf_op jit(solution)/shard_map/ppermute | solution.py:238
  94.6 5.8 %collective-permute-start.22 = (bf16[16,2048]{1,0:T(8,128)(2,1)S(1)}, bf16[16,2048]{1,0:T(8,128)(2,1)S(1)}, u32[]{:S(2)}, u32[]{:S(2)}) collective-permute-start(bf16[16,2048]{1,0:T(8,128)(2,1)S(1)} %get-tuple-element.58), channel_id=1, source_target_pairs={{0,7},{1,0},{2,1},{3,2},{4,3},{5,4},{6,5},{7,6},{8,15},{9,8},{10,9... | collective-permute-start | bytes 196616 | tf_op jit(solution)/shard_map/ppermute | solution.py:238
  (7 other events, 118.3 us)

commit v2 on v1

--- a/solution.py
+++ b/solution.py
@@ -39,33 +39,6 @@
         scratch_shapes=[pltpu.VMEM(shape, dtype) for shape, dtype in scratch],
         compiler_params=pltpu.CompilerParams(vmem_limit_bytes=limit << 20),
     )(*scalars, *args, *held)
-
-
-def head_body(at_ref, u_hbm, v_hbm, flat_ref, keep_ref, send_ref, u_s, w_s, v_s, sems):
-    fetch = [pltpu.make_async_copy(v_hbm, v_s, sems.at[0]), pltpu.make_async_copy(u_hbm, u_s, sems.at[1])]
-    for copy in fetch:
-        copy.start()
-    half = keep_ref.shape[1]
-    first = at_ref[0] == 0
-    fetch[0].wait()
-
-    @pl.when(first)
-    def _():
-        keep_ref[...] = v_s[:, :half]
-        send_ref[...] = v_s[:, half:]
-
-    @pl.when(jnp.logical_not(first))
-    def _():
-        keep_ref[...] = v_s[:, half:]
-        send_ref[...] = v_s[:, :half]
-
-    fetch[1].wait()
-    _, depth, rows, cols = u_s.shape
-    w_s[...] = u_s[...].astype(f32)
-    for x in range(depth):
-        for y in range(rows):
-            at = (x * rows + y) * cols
-            flat_ref[:, at : at + cols] = w_s[:, x, y, :].astype(bf16)
 
 
 def stack_body(which, at_ref, mine_ref, got_ref, *outs):
@@ -159,66 +132,64 @@
         store(at, block, acc)
 
 
-def own_body(at_ref, kt_ref, u_ref, g_ref, p0, p1, p2, p3, l_ref, ov_ref, v_ref):
-    gather_rows(at_ref[4], (p0, p1, p2, p3), v_ref)
+def own_body(kt_ref, u_ref, v_ref, g_ref, l_ref, ov_ref):
     ov_ref[...] = jnp.zeros_like(ov_ref)
 
     def store(at, size, acc):
         l_ref[:, at : at + size] = acc
 
-    sweep(kt_ref, u_ref, v_ref, g_ref, ov_ref, store)
-
-
-def oth_body(at_ref, kt_ref, u_ref, g0_ref, g1_ref, v0_ref, old_ref, p0, p1, p2, p3, l0_ref, l1_ref, send_ref, v1_ref, ov_s):
-    gather_rows(at_ref[4], (p0, p1, p2, p3), v1_ref)
+    sweep(kt_ref, u_ref, v_ref, g_ref, ov_ref, store, 0, l_ref.shape[1])
+
+
+def oth_body(kt_ref, u_ref, v_ref, g_ref, old_ref, l_ref, send_ref, ov_s):
     ov_s[...] = jnp.zeros_like(ov_s)
-
-    def store0(at, size, acc):
-        l0_ref[:, at : at + size] = old_ref[:, at : at + size] + acc
-
-    def store1(at, size, acc):
-        l1_ref[:, at : at + size] = acc
-
-    sweep(kt_ref, u_ref, v0_ref, g0_ref, ov_s, store0)
-    sweep(kt_ref, u_ref, v1_ref, g1_ref, ov_s, store1)
+    done = old_ref.shape[1]
+
+    def store(at, size, acc):
+        l_ref[:, at : at + size] = acc + old_ref[:, at : at + size] if at < done else acc
+
+    sweep(kt_ref, u_ref, v_ref, g_ref, ov_s, store)
     send_ref[...] = ov_s[...].T.astype(bf16)
 
 
-def last_body(
-    scale, kt_ref, u_ref, g_ref, v0_ref, v1_ref, l0_ref, l1_ref, ov_old_ref, ma_ref, mb_ref, core_ref, out_ref, ov_ref, w_s
-):
-    rank = out_ref.shape[0]
-    half = v0_ref.shape[1]
+def last_body(scale, kt_ref, u_ref, v_ref, g_ref, l_ref, ov_old_ref, ma_ref, mb_ref, core_ref, out_ref, ov_ref, w_s):
+    rank, count = out_ref.shape
     ov_ref[...] = ov_old_ref[...]
     w = core_ref[...].astype(bf16).astype(f32) * 0.125 + scale * (ma_ref[...] + mb_ref[...])
     high = w.astype(bf16)
     w_s[:rank, :] = high
     w_s[rank:, :] = (w - high.astype(f32)).astype(bf16)
 
-    def send(v, at, total):
-        side = dot(w_s[...], v, 1, 0)
-        out_ref[:, at : at + total.shape[1]] = (scale * total + (side[:rank] + side[rank:])).astype(bf16)
-
-    send(v0_ref[...], 0, l0_ref[...])
-
-    def store(at, size, acc):
-        send(v1_ref[:, at : at + size], half + at, l1_ref[:, at : at + size] + acc)
-
-    sweep(kt_ref, u_ref, v1_ref, g_ref, ov_ref, store)
-
-
-def turn_body(at_ref, ov_ref, got_ref, me_ref, *refs):
-    outs, tot_s = refs[:-1], refs[-1]
+    def send_on(at, size, acc):
+        here = slice(at, at + size)
+        side = dot(w_s[...], v_ref[:, here], 1, 0)
+        total = l_ref[:, here] if acc is None else l_ref[:, here] + acc
+        out_ref[:, here] = (scale * total + (side[:rank] + side[rank:])).astype(bf16)
+
+    send_on(0, count // 2, None)
+    sweep(kt_ref, u_ref, v_ref, g_ref, ov_ref, send_on, count // 2)
+
+
+def turn_body(at_ref, ov_ref, got_ref, me_ref, up_ref, dn_ref, away_ref, tot_s):
     tot_s[...] = ov_ref[...].T + got_ref[...].astype(f32)
     rows = me_ref.shape[0]
-    n_samp = tot_s.shape[0] // rows
+    y = at_ref[2]
 
     def part(turn):
-        return tot_s[pl.ds(pl.multiple_of(((at_ref[1] + turn) % n_samp) * rows, rows), rows), :]
+        return tot_s[pl.ds(pl.multiple_of(((y + turn) % 4) * rows, rows), rows), :]
 
     me_ref[...] = part(0)
-    for turn, out_ref in enumerate(outs, 1):
-        out_ref[...] = part(turn).astype(bf16)
+    up_ref[...] = part(1).astype(bf16)
+    away_ref[...] = part(2).astype(bf16)
+    dn_ref[...] = part(3).astype(bf16)
+
+
+def pair_body(at_ref, me_ref, rc_ref, rd_ref, re_ref, mine_ref, send_ref, tot_s):
+    rows = mine_ref.shape[0]
+    tot_s[...] = (me_ref[...] + rc_ref[...].astype(f32)) + (rd_ref[...].astype(f32) + re_ref[...].astype(f32))
+    xh = at_ref[3]
+    mine_ref[...] = tot_s[pl.ds(pl.multiple_of(xh * rows, rows), rows), :]
+    send_ref[...] = tot_s[pl.ds(pl.multiple_of((1 - xh) * rows, rows), rows), :].astype(bf16)
 
 
 def done_body(scale, base_ref, mine_ref, *refs):
@@ -256,29 +227,12 @@
     where_at = jnp.stack(places).astype(jnp.int32)
     swap = ring(2, 1)
 
-    quart = half // 2
-    far = pl.BlockSpec(memory_space=pltpu.MemorySpace.HBM)
-    vmem = pl.BlockSpec(memory_space=pltpu.VMEM)
-    u0, v_keep, v_send = pl.pallas_call(
-        head_body,
-        in_specs=[pl.BlockSpec(memory_space=pltpu.SMEM), far, far],
-        out_specs=[vmem] * 3,
-        out_shape=[pltpu.VMEM((narrow, cells), bf16)] + [pltpu.VMEM((lanes, half), bf16)] * 2,
-        scratch_shapes=[
-            pltpu.VMEM(basis_u.shape, bf16),
-            pltpu.VMEM(basis_u.shape, f32),
-            pltpu.VMEM(basis_v.shape, bf16),
-            pltpu.SemaphoreType.DMA((2,)),
-        ],
-        compiler_params=pltpu.CompilerParams(vmem_limit_bytes=24 << 20),
-    )(where_at, basis_u, basis_v)
+    u0 = basis_u.reshape(narrow, cells)
     u1 = send(u0, "xh", swap)
-    v_got = send(v_send, "c", swap)
-    (v_chip,) = small(functools.partial(stack_body, 0), [v_keep, v_got], [((2 * lanes, half), bf16, True)], at=where_at)
-    v_next = send(v_chip, "xl", swap)
-    v_mine = small(functools.partial(stack_body, 5), [v_chip, v_next], [((4 * lanes, quart), bf16, True)] * 2, at=where_at)
-    v_pieces = [[m] + [send(m, "z", ring(4, k)) for k in (1, 3, 2)] for m in v_mine]
-    (pair,) = small(functools.partial(stack_body, 3), [u0, u1], [((2 * narrow, cells), bf16, True)], at=where_at)
+    v_half = jnp.transpose(basis_v.reshape(lanes, 2, half), (1, 0, 2))
+    v_wide = jnp.broadcast_to(v_half[None], (n_space // 2,) + v_half.shape).reshape(rank, half)
+    v = resident(lax.all_to_all(v_wide, SPACE, 0, 0, tiled=True))
+    (pair,) = small(functools.partial(stack_body, 3), [resident(u0), u1], [((2 * narrow, cells), bf16, True)], at=where_at)
     around = [send(pair, "y", ring(4, k)) for k in (1, 3, 2)]
     u_own, k_own, kt_own, edge = small(
         prep_body,
@@ -292,13 +246,10 @@
     halo = send(edge, SPACE, hops)
 
     growth = 0.5 + 0.5 * lax.dynamic_slice_in_dim(sample_class, core_at * half, half, 0).astype(f32)
-    growth = [resident(growth[i * quart : (i + 1) * quart].reshape(1, quart)) for i in range(2)]
+    growth = resident(growth.reshape(1, half))
     scale = step_size * cell_weight
-    l_first, ov_first, v0 = small(
-        own_body,
-        [kt_own, u_own, growth[0], *v_pieces[0]],
-        [((rank, quart), f32, True), ((cells, rank), f32, True), ((rank, quart), bf16, True)],
-        at=where_at,
+    l_first, ov_first = small(
+        own_body, [kt_own, u_own, v, growth], [((rank, half // 2), f32, True), ((cells, rank), f32, True)]
     )
     kt_oth, base, m_own = small(
         functools.partial(mid_body, rows_y, cols_z),
@@ -309,18 +260,17 @@
         held=(ov_first, kt_own, l_first),
     )
     m_oth = send(m_own, "c", swap)
-    l0, l1, ov_send, v1 = small(
+    l_most, ov_send = small(
         oth_body,
-        [kt_oth, u_oth, *growth, v0, l_first, *v_pieces[1]],
-        [((rank, quart), f32, True), ((rank, quart), f32, True), ((rank, cells), bf16, True), ((rank, quart), bf16, True)],
+        [kt_oth, u_oth, v, growth, l_first],
+        [((rank, half), f32, True), ((rank, cells), bf16, True)],
         [((cells, rank), f32)],
-        at=where_at,
         held=(ov_first, kt_own, u_own),
     )
     got = send(ov_send, "c", swap)
     l_part, ov_own = small(
         functools.partial(last_body, scale),
-        [kt_own, u_own, growth[1], v0, v1, l0, l1, ov_first, m_own, m_oth, core_s],
+        [kt_own, u_own, v, growth, l_most, ov_first, m_own, m_oth, core_s],
         [((rank, half), bf16, False), ((cells, rank), f32, True)],
         [((2 * rank, rank), bf16)],
     )
@@ -329,16 +279,26 @@
     l_new = l_got.reshape(n_space // 2, 2, lanes, half).astype(f32).sum(0)
     l_new = jnp.transpose(l_new, (1, 0, 2)).reshape(lanes, samp_rows)
 
-    me, *others = small(
+    rows = rank // 4
+    me, up, dn, away = small(
         turn_body,
         [ov_own, got],
-        [((narrow, cells), f32, True)] + [((narrow, cells), bf16, True)] * (n_samp - 1),
+        [((rows, cells), f32, True)] + [((rows, cells), bf16, True)] * 3,
         [((rank, cells), f32)],
         at=where_at,
     )
-    sums = [send(part, SAMP, ring(n_samp, turn)) for turn, part in enumerate(others, 1)]
+    near = [send(part, "y", ring(4, k)) for part, k in ((up, 1), (dn, 3), (away, 2))]
+    mine, rest = small(
+        pair_body,
+        [me, *near],
+        [((narrow, cells), f32, True), ((narrow, cells), bf16, True)],
+        [((rows, cells), f32)],
+        at=where_at,
+    )
     (k_new,) = small(
-        functools.partial(done_body, step_size * samp_weight), [base, me, *sums], [(basis_u.shape, f32, False)]
+        functools.partial(done_body, step_size * samp_weight),
+        [base, mine, send(rest, "xh", swap)],
+        [(basis_u.shape, f32, False)],
     )
     return (k_new, l_new)
 

time: 102 us -> 98.5 us (0.966)
  starting transfers between devices: 42.2 us -> 30.6 us
  waiting for transfers between devices: 22.2 us -> 30.7 us
  Pallas kernels: 33.3 us -> 31.3 us
    ppermute x23 -> x12, starting transfers between devices: 37.7 us -> 19.5 us  [send(): return resident(lax.ppermute(x, axis, hops))]
    ppermute x23 -> x12, waiting for transfers between devices: 22.2 us -> 30.7 us  [send(): return resident(lax.ppermute(x, axis, hops))]
    all_to_all x0 -> x1, starting transfers between devices: none -> 6.46 us  [per_device(): v = resident(lax.all_to_all(v_wide, SPACE, 0, 0, tiled=True))]
    broadcast_in_dim x0 -> x1, local copies, waits for them, and re-layouts: none -> 2.06 us  [per_device(): jnp.broadcast_to(v_half[None], (n_space // 2,) + v_half.shape)]
    unnamed x14 -> x13, local copies, waits for them, and re-layouts: 2.61 us -> 0.85 us
    pallas_call x10 -> x9, Pallas kernels: 32.3 us -> 31.3 us  [small(): pl.pallas_call(reading, in_specs=[pl.BlockSpec(memory_space=pltpu.SMEM)]...]
  transfers between devices with their start and end apart: 24 -> 14, of which waited for: 10 -> 9; matrix products, arithmetic and copies ran while one was open for 0% -> 1% of each run, Pallas kernels for 24% -> 22%
where the time goes in v2:
time: 98.5 us; the launch traced here: 98 us
  Pallas kernels  31.3 us (32%)
  waiting for transfers between devices  30.7 us (31%)
  starting transfers between devices  30.6 us (31%)
  local copies, waits for them, and re-layouts  2.99 us (3%)
  other arithmetic  1.57 us (2%)
    pallas_call x9, Pallas kernels, small(): pl.pallas_call(reading, in_specs=[pl.BlockSpec(memory_space=pltpu.SMEM)]...  31.3 us
    ppermute x12, waiting for transfers between devices, send(): return resident(lax.ppermute(x, axis, hops))  30.7 us
    ppermute x12, starting transfers between devices, send(): return resident(lax.ppermute(x, axis, hops))  19.5 us
    all_to_all x1, starting transfers between devices, per_device(): v = resident(lax.all_to_all(v_wide, SPACE, 0, 0, tiled=True))  6.46 us
    all_to_all x1, starting transfers between devices, per_device(): l_got = lax.all_to_all(l_part, SPACE, 0, 0, tiled=True)  4.69 us
    broadcast_in_dim x1, local copies, waits for them, and re-layouts, per_device(): jnp.broadcast_to(v_half[None], (n_space // 2,) + v_half.shape)  2.06 us
  transfers between devices with their start and end apart: 14, of which 9 were waited for; matrix products, arithmetic and copies ran while one was open for 1% of the time, Pallas kernels for 22%

profile of v2, /device:TPU:0, one launch (start us, length us, event | category | flops | bytes accessed | tf_op | source)
XLA Modules:
  0.0 98.0 jit_solution(11773236152072975532)
XLA Ops:
  0.6 2.1 %broadcast_in_dim.2 = bf16[8,2,8,4096]{3,2,1,0:T(8,128)(2,1)} broadcast(bf16[2,8,4096]{2,1,0:T(8,128)(2,1)} %bitcast.34), dimensions={1,2,3} | broadcast | bytes 1179648 | tf_op jit(solution)/shard_map/broadcast_in_dim | solution.py:233
  2.7 6.5 %all-to-all-start = ((bf16[16,8,4096]{2,1,0:T(8,128)(2,1)}), bf16[16,8,4096]{2,1,0:T(8,128)(2,1)S(1)}, u32[]{:S(2)}, u32[]{:S(2)}) async-start(bf16[16,8,4096]{2,1,0:T(8,128)(2,1)} %bitcast.8), calls=%async_computation | async-start | bytes 2097152 | tf_op jit(solution)/shard_map/all_to_all | solution.py:234
  9.2 2.8 %collective-permute-start = (bf16[16,2048]{1,0:T(8,128)(2,1)S(1)}, bf16[16,2048]{1,0:T(8,128)(2,1)S(1)}, u32[]{:S(2)}, u32[]{:S(2)}) collective-permute-start(bf16[16,2048]{1,0:T(8,128)(2,1)S(1)} %bitcast.29), channel_id=1, source_target_pairs={{0,1},{1,0},{2,3},{3,2},{4,5},{5,4},{6,7},{7,6},{8,9},{9,8},{10,11... | collective-permute-start | bytes 196616 | tf_op jit(solution)/shard_map/ppermute | solution.py:209
  12.1 14.3 %collective-permute-done.refs_2_ = bf16[16,2048]{1,0:T(8,128)(2,1)S(1)} collective-permute-done((bf16[16,2048]{1,0:T(8,128)(2,1)S(1)}, bf16[16,2048]{1,0:T(8,128)(2,1)S(1)}, u32[]{:S(2)}, u32[]{:S(2)}) %collective-permute-start) | collective-permute-done | bytes 65568 | tf_op jit(solution)/shard_map/ppermute | solution.py:209
  26.9 3.3 %collective-permute-start.3 = (bf16[32,2048]{1,0:T(8,128)(2,1)S(1)}, bf16[32,2048]{1,0:T(8,128)(2,1)S(1)}, u32[]{:S(2)}, u32[]{:S(2)}) collective-permute-start(bf16[32,2048]{1,0:T(8,128)(2,1)S(1)} %shard_map.68.refs_1_), channel_id=1, source_target_pairs={{0,4},{2,6},{4,0},{6,2},{1,5},{3,7},{5,1},{7,3},{8,12},{10,14},{12... | collective-permute-start | bytes 393224 | tf_op jit(solution)/shard_map/ppermute | solution.py:209
  30.2 1.1 %collective-permute-start.2 = (bf16[32,2048]{1,0:T(8,128)(2,1)S(1)}, bf16[32,2048]{1,0:T(8,128)(2,1)S(1)}, u32[]{:S(2)}, u32[]{:S(2)}) collective-permute-start(bf16[32,2048]{1,0:T(8,128)(2,1)S(1)} %shard_map.68.refs_1_), channel_id=1, source_target_pairs={{0,6},{2,0},{4,2},{6,4},{1,7},{3,1},{5,3},{7,5},{8,14},{10,8},{12,... | collective-permute-start | bytes 393224 | tf_op jit(solution)/shard_map/ppermute | solution.py:209
  31.3 1.0 collective-permute-start.1
  32.2 2.3 %collective-permute-done.3.refs_4_ = bf16[32,2048]{1,0:T(8,128)(2,1)S(1)} collective-permute-done((bf16[32,2048]{1,0:T(8,128)(2,1)S(1)}, bf16[32,2048]{1,0:T(8,128)(2,1)S(1)}, u32[]{:S(2)}, u32[]{:S(2)}) %collective-permute-start.3) | collective-permute-done | bytes 131104 | tf_op jit(solution)/shard_map/ppermute | solution.py:209
  34.5 2.5 %collective-permute-done.2.refs_3_ = bf16[32,2048]{1,0:T(8,128)(2,1)S(1)} collective-permute-done((bf16[32,2048]{1,0:T(8,128)(2,1)S(1)}, bf16[32,2048]{1,0:T(8,128)(2,1)S(1)}, u32[]{:S(2)}, u32[]{:S(2)}) %collective-permute-start.2) | collective-permute-done | bytes 131104 | tf_op jit(solution)/shard_map/ppermute | solution.py:209
  37.4 1.7 %shard_map.69 = (bf16[128,2048]{1,0:T(8,128)(2,1)S(1)}, bf16[128,2048]{1,0:T(8,128)(2,1)S(1)}, bf16[2048,128]{1,0:T(8,128)(2,1)S(1)}, bf16[128,1024]{1,0:T(8,128)(2,1)}) custom-call(s32[6]{0:T(128)S(1)} %stack.27.refs_0_, bf16[32,2048]{1,0:T(8,128)(2,1)S(1)} %shard_map.68.refs_1_, bf16[32,2048]{1,0:T(8,128)(2,1)S(1)} %collective-permute-done.1.refs_2_, ...), custom_call_target="tpu_custom_call" | custom-call | tf_op jit(solution)/shard_map/pallas_call | solution.py:33
  40.5 5.6 %shard_map.70 = (f32[128,2048]{1,0:T(8,128)S(1)}, f32[2048,128]{1,0:T(8,128)S(1)}) custom-call(bf16[2048,128]{1,0:T(8,128)(2,1)S(1)} %get-tuple-element.24.refs_0_.refs_8_.refs_6_, bf16[128,2048]{1,0:T(8,128)(2,1)S(1)} %get-tuple-element.21.refs_1_.refs_6_.refs_7_, bf16[128,4096]{1,0:T(8,128)(2,1)S(1)} %bitcast.23, f32[1,4096]{1,0:T(1,128)S(1)} %bitcast.26), custom_call_target="tpu_custom_call" | custom-call | tf_op jit(solution)/shard_map/pallas_call | solution.py:33
  46.2 2.5 %shard_map.71 = (bf16[2048,128]{1,0:T(8,128)(2,1)S(1)}, f32[16,2048]{1,0:T(8,128)}, f32[128,128]{1,0:T(8,128)S(1)}) custom-call(s32[6]{0:T(128)S(1)} %stack.27.refs_0_, bf16[128,2048]{1,0:T(8,128)(2,1)S(1)} %collective-permute-done.4.refs_1_, f32[128,128]{1,0:T(8,128)S(1)} %copy-done, bf16[128,2048]{1,0:T(8,128)(2,1)S(1)} %get-tuple-element.22.refs_3_, ...), custom_call_target="tpu_custom_call" | custom-call | tf_op jit(solution)/shard_map/pallas_call | solution.py:33
  48.6 4.1 %collective-permute-start.6 = (f32[128,128]{1,0:T(8,128)S(1)}, f32[128,128]{1,0:T(8,128)S(1)}, u32[]{:S(2)}, u32[]{:S(2)}) collective-permute-start(f32[128,128]{1,0:T(8,128)S(1)} %get-tuple-element.30.refs_6_), channel_id=1, source_target_pairs={{0,8},{8,0},{1,9},{9,1},{2,10},{10,2},{3,11},{11,3},{4,12},{12,4},... | collective-permute-start | bytes 196616 | tf_op jit(solution)/shard_map/ppermute | solution.py:209
  52.7 11.2 %shard_map.72 = (f32[128,4096]{1,0:T(8,128)S(1)}, bf16[128,2048]{1,0:T(8,128)(2,1)S(1)}) custom-call(bf16[2048,128]{1,0:T(8,128)(2,1)S(1)} %get-tuple-element.28.refs_0_, bf16[128,2048]{1,0:T(8,128)(2,1)S(1)} %collective-permute-done.4.refs_1_, bf16[128,4096]{1,0:T(8,128)(2,1)S(1)} %bitcast.24, f32[1,4096]{1,0:T(1,128)S(1)} %bitcast.27, ...), custom_call_target="tpu_custom_call" | custom-call | tf_op jit(solution)/shard_map/pallas_call | solution.py:33
  64.7 7.5 %shard_map.73 = (bf16[128,4096]{1,0:T(8,128)(2,1)}, f32[2048,128]{1,0:T(8,128)S(1)}) custom-call(bf16[2048,128]{1,0:T(8,128)(2,1)S(1)} %get-tuple-element.24.refs_0_.refs_8_.refs_6_, bf16[128,2048]{1,0:T(8,128)(2,1)S(1)} %get-tuple-element.21.refs_1_.refs_6_.refs_7_, bf16[128,4096]{1,0:T(8,128)(2,1)S(1)} %bitcast.25, f32[1,4096]{1,0:T(1,128)S(1)} %bitcast.28, ...), custom_call_target="tpu_custom_call" | custom-call | tf_op jit(solution)/shard_map/pallas_call | solution.py:33
  72.2 4.7 %all-to-all-start.1 = ((bf16[16,8,4096]{2,1,0:T(8,128)(2,1)}), bf16[16,8,4096]{2,1,0:T(8,128)(2,1)S(1)}, u32[]{:S(2)}, u32[]{:S(2)}) async-start(bf16[16,8,4096]{2,1,0:T(8,128)(2,1)} %bitcast.32), calls=%async_computation.1 | async-start | bytes 2097152 | tf_op jit(solution)/shard_map/all_to_all | solution.py:278
  77.4 1.6 %collective-permute-done.7.refs_2_ = bf16[128,2048]{1,0:T(8,128)(2,1)S(1)} collective-permute-done((bf16[128,2048]{1,0:T(8,128)(2,1)S(1)}, bf16[128,2048]{1,0:T(8,128)(2,1)S(1)}, u32[]{:S(2)}, u32[]{:S(2)}) %collective-permute-start.7) | collective-permute-done | bytes 524320 | tf_op jit(solution)/shard_map/ppermute | solution.py:209
  79.0 0.9 shard_map.74
  80.6 2.7 %collective-permute-start.9 = (bf16[32,2048]{1,0:T(8,128)(2,1)S(1)}, bf16[32,2048]{1,0:T(8,128)(2,1)S(1)}, u32[]{:S(2)}, u32[]{:S(2)}) collective-permute-start(bf16[32,2048]{1,0:T(8,128)(2,1)S(1)} %get-tuple-element.35), channel_id=1, source_target_pairs={{0,6},{2,0},{4,2},{6,4},{1,7},{3,1},{5,3},{7,5},{8,14},{10,8},{12,... | collective-permute-start | bytes 393224 | tf_op jit(solution)/shard_map/ppermute | solution.py:209
  84.1 2.9 %collective-permute-done.8.refs_2_ = bf16[32,2048]{1,0:T(8,128)(2,1)S(1)} collective-permute-done((bf16[32,2048]{1,0:T(8,128)(2,1)S(1)}, bf16[32,2048]{1,0:T(8,128)(2,1)S(1)}, u32[]{:S(2)}, u32[]{:S(2)}) %collective-permute-start.8) | collective-permute-done | bytes 131104 | tf_op jit(solution)/shard_map/ppermute | solution.py:209
  87.0 2.1 %collective-permute-done.9.refs_3_ = bf16[32,2048]{1,0:T(8,128)(2,1)S(1)} collective-permute-done((bf16[32,2048]{1,0:T(8,128)(2,1)S(1)}, bf16[32,2048]{1,0:T(8,128)(2,1)S(1)}, u32[]{:S(2)}, u32[]{:S(2)}) %collective-permute-start.9) | collective-permute-done | bytes 131104 | tf_op jit(solution)/shard_map/ppermute | solution.py:209
  89.1 0.9 collective-permute-done.10.refs_4_
  90.6 2.1 %collective-permute-start.11 = (bf16[16,2048]{1,0:T(8,128)(2,1)S(1)}, bf16[16,2048]{1,0:T(8,128)(2,1)S(1)}, u32[]{:S(2)}, u32[]{:S(2)}) collective-permute-start(bf16[16,2048]{1,0:T(8,128)(2,1)S(1)} %get-tuple-element.38), channel_id=1, source_target_pairs={{0,1},{1,0},{2,3},{3,2},{4,5},{5,4},{6,7},{7,6},{8,9},{9,8},{10,11... | collective-permute-start | bytes 196616 | tf_op jit(solution)/shard_map/ppermute | solution.py:209
  92.6 3.8 %collective-permute-done.11.refs_2_ = bf16[16,2048]{1,0:T(8,128)(2,1)S(1)} collective-permute-done((bf16[16,2048]{1,0:T(8,128)(2,1)S(1)}, bf16[16,2048]{1,0:T(8,128)(2,1)S(1)}, u32[]{:S(2)}, u32[]{:S(2)}) %collective-permute-start.11) | collective-permute-done | bytes 65568 | tf_op jit(solution)/shard_map/ppermute | solution.py:209
  (30 shorter events, 7.5 us)
Async XLA Ops:
  0.6 8.6 %copy-start.5 = (bf16[16,2,8,128]{3,2,1,0:T(8,128)(2,1)S(1)}, bf16[16,2,8,128]{3,2,1,0:T(8,128)(2,1)}, u32[]{:S(2)}) copy-start(bf16[16,2,8,128]{3,2,1,0:T(8,128)(2,1)} %param.5) | copy-start | bytes 196612
  0.6 36.8 %copy-start = (f32[128,128]{1,0:T(8,128)S(1)}, f32[128,128]{1,0:T(8,128)}, u32[]{:S(2)}) copy-start(f32[128,128]{1,0:T(8,128)} %refs_8_.1) | copy-start | bytes 196612
  2.7 37.8 %all-to-all-start = ((bf16[16,8,4096]{2,1,0:T(8,128)(2,1)}), bf16[16,8,4096]{2,1,0:T(8,128)(2,1)S(1)}, u32[]{:S(2)}, u32[]{:S(2)}) async-start(bf16[16,8,4096]{2,1,0:T(8,128)(2,1)} %bitcast.8), calls=%async_computation | async-start | bytes 2097152 | tf_op jit(solution)/shard_map/all_to_all | solution.py:234
  9.2 37.0 %copy-start.2 = (s32[6,2,8,128]{3,2,1,0:T(8,128)S(1)}, s32[6,2,8,128]{3,2,1,0:T(8,128)}, u32[]{:S(2)}) copy-start(s32[6,2,8,128]{3,2,1,0:T(8,128)} %refs_5_.3) | copy-start | bytes 147460
  9.2 17.1 %collective-permute-start = (bf16[16,2048]{1,0:T(8,128)(2,1)S(1)}, bf16[16,2048]{1,0:T(8,128)(2,1)S(1)}, u32[]{:S(2)}, u32[]{:S(2)}) collective-permute-start(bf16[16,2048]{1,0:T(8,128)(2,1)S(1)} %bitcast.29), channel_id=1, source_target_pairs={{0,1},{1,0},{2,3},{3,2},{4,5},{5,4},{6,7},{7,6},{8,9},{9,8},{10,11... | collective-permute-start | bytes 196616 | tf_op jit(solution)/shard_map/ppermute | solution.py:209
  26.9 7.6 %collective-permute-start.3 = (bf16[32,2048]{1,0:T(8,128)(2,1)S(1)}, bf16[32,2048]{1,0:T(8,128)(2,1)S(1)}, u32[]{:S(2)}, u32[]{:S(2)}) collective-permute-start(bf16[32,2048]{1,0:T(8,128)(2,1)S(1)} %shard_map.68.refs_1_), channel_id=1, source_target_pairs={{0,4},{2,6},{4,0},{6,2},{1,5},{3,7},{5,1},{7,3},{8,12},{10,14},{12... | collective-permute-start | bytes 393224 | tf_op jit(solution)/shard_map/ppermute | solution.py:209
  30.2 6.8 %collective-permute-start.2 = (bf16[32,2048]{1,0:T(8,128)(2,1)S(1)}, bf16[32,2048]{1,0:T(8,128)(2,1)S(1)}, u32[]{:S(2)}, u32[]{:S(2)}) collective-permute-start(bf16[32,2048]{1,0:T(8,128)(2,1)S(1)} %shard_map.68.refs_1_), channel_id=1, source_target_pairs={{0,6},{2,0},{4,2},{6,4},{1,7},{3,1},{5,3},{7,5},{8,14},{10,8},{12,... | collective-permute-start | bytes 393224 | tf_op jit(solution)/shard_map/ppermute | solution.py:209
  31.3 6.2 %collective-permute-start.1 = (bf16[32,2048]{1,0:T(8,128)(2,1)S(1)}, bf16[32,2048]{1,0:T(8,128)(2,1)S(1)}, u32[]{:S(2)}, u32[]{:S(2)}) collective-permute-start(bf16[32,2048]{1,0:T(8,128)(2,1)S(1)} %shard_map.68.refs_1_), channel_id=1, source_target_pairs={{0,2},{2,4},{4,6},{6,0},{1,3},{3,5},{5,7},{7,1},{8,10},{10,12},{12... | collective-permute-start | bytes 393224 | tf_op jit(solution)/shard_map/ppermute | solution.py:209
  39.1 7.1 %collective-permute-start.4 = (bf16[128,2048]{1,0:T(8,128)(2,1)S(1)}, bf16[128,2048]{1,0:T(8,128)(2,1)S(1)}, u32[]{:S(2)}, u32[]{:S(2)}) collective-permute-start(bf16[128,2048]{1,0:T(8,128)(2,1)S(1)} %get-tuple-element.21.refs_1_.refs_6_.refs_7_), channel_id=1, source_target_pairs={{0,8},{8,0},{1,9},{9,1},{2,10},{10,2},{3,11},{11,3},{4,12},{12,4},... | collective-permute-start | bytes 1572872 | tf_op jit(solution)/shard_map/ppermute | solution.py:209
  39.1 7.0 %collective-permute-start.5 = (bf16[128,1024]{1,0:T(8,128)(2,1)}, bf16[128,1024]{1,0:T(8,128)(2,1)S(1)}, u32[]{:S(2)}, u32[]{:S(2)}) collective-permute-start(bf16[128,1024]{1,0:T(8,128)(2,1)} %get-tuple-element.23), channel_id=1, source_target_pairs={{8,16},{24,32},{40,48},{56,64},{72,80},{88,96},{104,112},{16,8},{3... | collective-permute-start | bytes 786440 | tf_op jit(solution)/shard_map/ppermute | solution.py:209
  48.6 16.1 %collective-permute-start.6 = (f32[128,128]{1,0:T(8,128)S(1)}, f32[128,128]{1,0:T(8,128)S(1)}, u32[]{:S(2)}, u32[]{:S(2)}) collective-permute-start(f32[128,128]{1,0:T(8,128)S(1)} %get-tuple-element.30.refs_6_), channel_id=1, source_target_pairs={{0,8},{8,0},{1,9},{9,1},{2,10},{10,2},{3,11},{11,3},{4,12},{12,4},... | collective-permute-start | bytes 196616 | tf_op jit(solution)/shard_map/ppermute | solution.py:209
  63.9 0.8 copy-start.3
  72.2 4.7 %copy-start.4 = (bf16[128,2048]{1,0:T(8,128)(2,1)S(1)}, bf16[128,2048]{1,0:T(8,128)(2,1)}, u32[]{:S(2)}) copy-start(bf16[128,2048]{1,0:T(8,128)(2,1)} %copy-done.3) | copy-start | bytes 1572868
  72.2 24.2 %copy-start.1 = (f32[16,2048]{1,0:T(8,128)S(1)}, f32[16,2048]{1,0:T(8,128)}, u32[]{:S(2)}) copy-start(f32[16,2048]{1,0:T(8,128)} %get-tuple-element.27.refs_0_) | copy-start | bytes 393220
  72.2 24.9 %all-to-all-start.1 = ((bf16[16,8,4096]{2,1,0:T(8,128)(2,1)}), bf16[16,8,4096]{2,1,0:T(8,128)(2,1)S(1)}, u32[]{:S(2)}, u32[]{:S(2)}) async-start(bf16[16,8,4096]{2,1,0:T(8,128)(2,1)} %bitcast.32), calls=%async_computation.1 | async-start | bytes 2097152 | tf_op jit(solution)/shard_map/all_to_all | solution.py:278
  76.9 2.1 %collective-permute-start.7 = (bf16[128,2048]{1,0:T(8,128)(2,1)S(1)}, bf16[128,2048]{1,0:T(8,128)(2,1)S(1)}, u32[]{:S(2)}, u32[]{:S(2)}) collective-permute-start(bf16[128,2048]{1,0:T(8,128)(2,1)S(1)} %copy-done.4), channel_id=1, source_target_pairs={{0,8},{8,0},{1,9},{9,1},{2,10},{10,2},{3,11},{11,3},{4,12},{12,4},... | collective-permute-start | bytes 1572872 | tf_op jit(solution)/shard_map/ppermute | solution.py:209
  80.0 7.0 %collective-permute-start.8 = (bf16[32,2048]{1,0:T(8,128)(2,1)S(1)}, bf16[32,2048]{1,0:T(8,128)(2,1)S(1)}, u32[]{:S(2)}, u32[]{:S(2)}) collective-permute-start(bf16[32,2048]{1,0:T(8,128)(2,1)S(1)} %get-tuple-element.34), channel_id=1, source_target_pairs={{0,2},{2,4},{4,6},{6,0},{1,3},{3,5},{5,7},{7,1},{8,10},{10,12},{12... | collective-permute-start | bytes 393224 | tf_op jit(solution)/shard_map/ppermute | solution.py:209
  80.6 8.5 %collective-permute-start.9 = (bf16[32,2048]{1,0:T(8,128)(2,1)S(1)}, bf16[32,2048]{1,0:T(8,128)(2,1)S(1)}, u32[]{:S(2)}, u32[]{:S(2)}) collective-permute-start(bf16[32,2048]{1,0:T(8,128)(2,1)S(1)} %get-tuple-element.35), channel_id=1, source_target_pairs={{0,6},{2,0},{4,2},{6,4},{1,7},{3,1},{5,3},{7,5},{8,14},{10,8},{12,... | collective-permute-start | bytes 393224 | tf_op jit(solution)/shard_map/ppermute | solution.py:209
  83.3 6.6 %collective-permute-start.10 = (bf16[32,2048]{1,0:T(8,128)(2,1)S(1)}, bf16[32,2048]{1,0:T(8,128)(2,1)S(1)}, u32[]{:S(2)}, u32[]{:S(2)}) collective-permute-start(bf16[32,2048]{1,0:T(8,128)(2,1)S(1)} %get-tuple-element.36), channel_id=1, source_target_pairs={{0,4},{2,6},{4,0},{6,2},{1,5},{3,7},{5,1},{7,3},{8,12},{10,14},{12... | collective-permute-start | bytes 393224 | tf_op jit(solution)/shard_map/ppermute | solution.py:209
  90.6 5.8 %collective-permute-start.11 = (bf16[16,2048]{1,0:T(8,128)(2,1)S(1)}, bf16[16,2048]{1,0:T(8,128)(2,1)S(1)}, u32[]{:S(2)}, u32[]{:S(2)}) collective-permute-start(bf16[16,2048]{1,0:T(8,128)(2,1)S(1)} %get-tuple-element.38), channel_id=1, source_target_pairs={{0,1},{1,0},{2,3},{3,2},{4,5},{5,4},{6,7},{7,6},{8,9},{9,8},{10,11... | collective-permute-start | bytes 196616 | tf_op jit(solution)/shard_map/ppermute | solution.py:209

commit v3 on v2

--- a/solution.py
+++ b/solution.py
@@ -116,12 +116,11 @@
     m_ref[...] = dot(u_ref[...], lap_s[...], 1, 1)
 
 
-def sweep(kt_ref, u_ref, v_ref, g_ref, ov_ref, store, start=0, stop=None, tile=512):
-    stop = v_ref.shape[1] if stop is None else stop
-    block = min(BLOCK, stop - start)
-    for at in range(start, stop, block):
-        v = v_ref[:, at : at + block]
-        g = g_ref[:, at : at + block]
+def sweep(kt_ref, u_ref, v_ref, g_ref, ov_ref, start, stop, block, store, tile=512):
+    def turn(i, _):
+        here = pl.ds(pl.multiple_of(start + i * block, block), block)
+        v = v_ref[:, here]
+        g = g_ref[:, here]
         acc = None
         for row in range(0, u_ref.shape[1], tile):
             field = dot(kt_ref[row : row + tile, :], v, 1, 0)
@@ -129,45 +128,68 @@
             ov_ref[row : row + tile, :] += dot(react, v, 1, 1)
             part = dot(u_ref[:, row : row + tile], react, 1, 0)
             acc = part if acc is None else acc + part
-        store(at, block, acc)
+        store(here, acc, v)
+        return 0
+
+    lax.fori_loop(0, (stop - start) // block, turn, 0)
 
 
 def own_body(kt_ref, u_ref, v_ref, g_ref, l_ref, ov_ref):
     ov_ref[...] = jnp.zeros_like(ov_ref)
 
-    def store(at, size, acc):
-        l_ref[:, at : at + size] = acc
-
-    sweep(kt_ref, u_ref, v_ref, g_ref, ov_ref, store, 0, l_ref.shape[1])
+    def store(here, acc, v):
+        l_ref[:, here] = acc
+
+    count = l_ref.shape[1]
+    sweep(kt_ref, u_ref, v_ref, g_ref, ov_ref, 0, count, min(BLOCK, count), store)
 
 
 def oth_body(kt_ref, u_ref, v_ref, g_ref, old_ref, l_ref, send_ref, ov_s):
     ov_s[...] = jnp.zeros_like(ov_s)
-    done = old_ref.shape[1]
-
-    def store(at, size, acc):
-        l_ref[:, at : at + size] = acc + old_ref[:, at : at + size] if at < done else acc
-
-    sweep(kt_ref, u_ref, v_ref, g_ref, ov_s, store)
+    done, count = old_ref.shape[1], l_ref.shape[1]
+
+    def add(here, acc, v):
+        l_ref[:, here] = old_ref[:, here] + acc
+
+    def store(here, acc, v):
+        l_ref[:, here] = acc
+
+    sweep(kt_ref, u_ref, v_ref, g_ref, ov_s, 0, done, min(BLOCK, done), add)
+    sweep(kt_ref, u_ref, v_ref, g_ref, ov_s, done, count, min(BLOCK, count - done), store)
     send_ref[...] = ov_s[...].T.astype(bf16)
 
 
-def last_body(scale, kt_ref, u_ref, v_ref, g_ref, l_ref, ov_old_ref, ma_ref, mb_ref, core_ref, out_ref, ov_ref, w_s):
+def more_body(start, kt_ref, u_ref, v_ref, g_ref, ov_old_ref, l_ref, ov_ref):
+    ov_ref[...] = ov_old_ref[...]
+    count = l_ref.shape[1]
+
+    def store(here, acc, v):
+        l_ref[...] = acc
+
+    sweep(kt_ref, u_ref, v_ref, g_ref, ov_ref, start, start + count, count, store)
+
+
+def last_body(scale, kt_ref, u_ref, v_ref, g_ref, l_ref, more_ref, ov_old_ref, ma_ref, mb_ref, core_ref, out_ref, ov_ref, w_s):
     rank, count = out_ref.shape
+    half = count // 2
+    rest = half + more_ref.shape[1]
     ov_ref[...] = ov_old_ref[...]
     w = core_ref[...].astype(bf16).astype(f32) * 0.125 + scale * (ma_ref[...] + mb_ref[...])
     high = w.astype(bf16)
     w_s[:rank, :] = high
     w_s[rank:, :] = (w - high.astype(f32)).astype(bf16)
 
-    def send_on(at, size, acc):
-        here = slice(at, at + size)
-        side = dot(w_s[...], v_ref[:, here], 1, 0)
-        total = l_ref[:, here] if acc is None else l_ref[:, here] + acc
+    def finish(here, total, v):
+        side = dot(w_s[...], v, 1, 0)
         out_ref[:, here] = (scale * total + (side[:rank] + side[rank:])).astype(bf16)
 
-    send_on(0, count // 2, None)
-    sweep(kt_ref, u_ref, v_ref, g_ref, ov_ref, send_on, count // 2)
+    finish(slice(0, half), l_ref[:, :half], v_ref[:, :half])
+    finish(slice(half, rest), l_ref[:, half:rest] + more_ref[...], v_ref[:, half:rest])
+
+    def store(here, acc, v):
+        finish(here, l_ref[:, here] + acc, v)
+
+    sweep(kt_ref, u_ref, v_ref, g_ref, ov_ref, rest, count, count - rest, store)
 
 
 def turn_body(at_ref, ov_ref, got_ref, me_ref, up_ref, dn_ref, away_ref, tot_s):
@@ -190,6 +212,15 @@
     xh = at_ref[3]
     mine_ref[...] = tot_s[pl.ds(pl.multiple_of(xh * rows, rows), rows), :]
     send_ref[...] = tot_s[pl.ds(pl.multiple_of((1 - xh) * rows, rows), rows), :].astype(bf16)
+
+
+def gain_body(got_ref, out_ref):
+    chips, parts, _, half = got_ref.shape
+    for p in range(parts):
+        total = got_ref[0, p].astype(f32)
+        for k in range(1, chips):
+            total = total + got_ref[k, p].astype(f32)
+        out_ref[:, p * half : (p + 1) * half] = total
 
 
 def done_body(scale, base_ref, mine_ref, *refs):
@@ -254,7 +285,7 @@
     kt_oth, base, m_own = small(
         functools.partial(mid_body, rows_y, cols_z),
         [u_oth, core_s, k_own, halo, face_class, u_own],
-        [((cells, rank), bf16, True), ((narrow, cells), f32, False), ((rank, rank), f32, True)],
+        [((cells, rank), bf16, True), ((narrow, cells), f32, True), ((rank, rank), f32, True)],
         [((rank, cells), f32), ((rank, cells), bf16)],
         at=where_at,
         held=(ov_first, kt_own, l_first),
@@ -265,19 +296,27 @@
         [kt_oth, u_oth, v, growth, l_first],
         [((rank, half), f32, True), ((rank, cells), bf16, True)],
         [((cells, rank), f32)],
-        held=(ov_first, kt_own, u_own),
+        held=(ov_first, kt_own, u_own, base),
     )
     got = send(ov_send, "c", swap)
+    l_more, ov_more = small(
+        functools.partial(more_body, half // 2),
+        [kt_own, u_own, v, growth, ov_first],
+        [((rank, half // 4), f32, True), ((cells, rank), f32, True)],
+        held=(l_most, base),
+    )
     l_part, ov_own = small(
         functools.partial(last_body, scale),
-        [kt_own, u_own, v, growth, l_most, ov_first, m_own, m_oth, core_s],
+        [kt_own, u_own, v, growth, l_most, l_more, ov_more, m_own, m_oth, core_s],
         [((rank, half), bf16, False), ((cells, rank), f32, True)],
         [((2 * rank, rank), bf16)],
+        held=(base,),
     )
 
     l_got = lax.all_to_all(l_part, SPACE, 0, 0, tiled=True)
-    l_new = l_got.reshape(n_space // 2, 2, lanes, half).astype(f32).sum(0)
-    l_new = jnp.transpose(l_new, (1, 0, 2)).reshape(lanes, samp_rows)
+    (l_new,) = small(
+        gain_body, [resident(l_got.reshape(n_space // 2, 2, lanes, half))], [((lanes, samp_rows), f32, False)]
+    )
 
     rows = rank // 4
     me, up, dn, away = small(
@@ -286,6 +325,7 @@
         [((rows, cells), f32, True)] + [((rows, cells), bf16, True)] * 3,
         [((rank, cells), f32)],
         at=where_at,
+        held=(base,),
     )
     near = [send(part, "y", ring(4, k)) for part, k in ((up, 1), (dn, 3), (away, 2))]
     mine, rest = small(
@@ -294,6 +334,7 @@
         [((narrow, cells), f32, True), ((narrow, cells), bf16, True)],
         [((rows, cells), f32)],
         at=where_at,
+        held=(base,),
     )
     (k_new,) = small(
         functools.partial(done_body, step_size * samp_weight),

time: 98.5 us -> 97.9 us (level)
  other arithmetic: 1.57 us -> 0.01 us
  starting transfers between devices: 30.6 us -> 31.8 us
    ppermute x12, starting transfers between devices: 19.5 us -> 20.6 us  [send(): return resident(lax.ppermute(x, axis, hops))]
    pallas_call x9 -> x11, Pallas kernels: 31.3 us -> 32 us  [small(): pl.pallas_call(reading, in_specs=[pl.BlockSpec(memory_space=pltpu.SMEM)]...]
  transfers between devices with their start and end apart: 14 -> 14, of which waited for: 9 -> 9; matrix products, arithmetic and copies ran while one was open for 1% -> 0% of each run, Pallas kernels for 22% -> 25%
where the time goes in v3:
time: 97.9 us; the launch traced here: 97.4 us
  Pallas kernels  32 us (33%)
  starting transfers between devices  31.8 us (32%)
  waiting for transfers between devices  30.7 us (31%)
  local copies, waits for them, and re-layouts  2.17 us (2%)
    pallas_call x11, Pallas kernels, small(): pl.pallas_call(reading, in_specs=[pl.BlockSpec(memory_space=pltpu.SMEM)]...  32 us
    ppermute x12, waiting for transfers between devices, send(): return resident(lax.ppermute(x, axis, hops))  30.7 us
    ppermute x12, starting transfers between devices, send(): return resident(lax.ppermute(x, axis, hops))  20.6 us
    all_to_all x1, starting transfers between devices, per_device(): v = resident(lax.all_to_all(v_wide, SPACE, 0, 0, tiled=True))  6.46 us
    all_to_all x1, starting transfers between devices, per_device(): l_got = lax.all_to_all(l_part, SPACE, 0, 0, tiled=True)  4.69 us
    broadcast_in_dim x1, local copies, waits for them, and re-layouts, per_device(): jnp.broadcast_to(v_half[None], (n_space // 2,) + v_half.shape)  2.04 us
  transfers between devices with their start and end apart: 14, of which 9 were waited for; matrix products, arithmetic and copies ran while one was open for 0% of the time, Pallas kernels for 25%

profile of v3, /device:TPU:0, one launch (start us, length us, event | category | flops | bytes accessed | tf_op | source)
XLA Modules:
  0.0 97.4 jit_solution(673195089752251404)
XLA Ops:
  0.7 2.0 %broadcast_in_dim.2 = bf16[8,2,8,4096]{3,2,1,0:T(8,128)(2,1)} broadcast(bf16[2,8,4096]{2,1,0:T(8,128)(2,1)} %bitcast.31), dimensions={1,2,3} | broadcast | bytes 1179648 | tf_op jit(solution)/shard_map/broadcast_in_dim | solution.py:264
  2.7 6.5 %all-to-all-start = ((bf16[16,8,4096]{2,1,0:T(8,128)(2,1)}), bf16[16,8,4096]{2,1,0:T(8,128)(2,1)S(1)}, u32[]{:S(2)}, u32[]{:S(2)}) async-start(bf16[16,8,4096]{2,1,0:T(8,128)(2,1)} %bitcast.8), calls=%async_computation | async-start | bytes 2097152 | tf_op jit(solution)/shard_map/all_to_all | solution.py:265
  9.2 2.8 %collective-permute-start = (bf16[16,2048]{1,0:T(8,128)(2,1)S(1)}, bf16[16,2048]{1,0:T(8,128)(2,1)S(1)}, u32[]{:S(2)}, u32[]{:S(2)}) collective-permute-start(bf16[16,2048]{1,0:T(8,128)(2,1)S(1)} %bitcast.28), channel_id=1, source_target_pairs={{0,1},{1,0},{2,3},{3,2},{4,5},{5,4},{6,7},{7,6},{8,9},{9,8},{10,11... | collective-permute-start | bytes 196616 | tf_op jit(solution)/shard_map/ppermute | solution.py:240
  12.1 14.3 %collective-permute-done.refs_2_ = bf16[16,2048]{1,0:T(8,128)(2,1)S(1)} collective-permute-done((bf16[16,2048]{1,0:T(8,128)(2,1)S(1)}, bf16[16,2048]{1,0:T(8,128)(2,1)S(1)}, u32[]{:S(2)}, u32[]{:S(2)}) %collective-permute-start) | collective-permute-done | bytes 65568 | tf_op jit(solution)/shard_map/ppermute | solution.py:240
  26.9 3.3 %collective-permute-start.3 = (bf16[32,2048]{1,0:T(8,128)(2,1)S(1)}, bf16[32,2048]{1,0:T(8,128)(2,1)S(1)}, u32[]{:S(2)}, u32[]{:S(2)}) collective-permute-start(bf16[32,2048]{1,0:T(8,128)(2,1)S(1)} %shard_map.68.refs_1_), channel_id=1, source_target_pairs={{0,4},{2,6},{4,0},{6,2},{1,5},{3,7},{5,1},{7,3},{8,12},{10,14},{12... | collective-permute-start | bytes 393224 | tf_op jit(solution)/shard_map/ppermute | solution.py:240
  30.2 1.1 %collective-permute-start.2 = (bf16[32,2048]{1,0:T(8,128)(2,1)S(1)}, bf16[32,2048]{1,0:T(8,128)(2,1)S(1)}, u32[]{:S(2)}, u32[]{:S(2)}) collective-permute-start(bf16[32,2048]{1,0:T(8,128)(2,1)S(1)} %shard_map.68.refs_1_), channel_id=1, source_target_pairs={{0,6},{2,0},{4,2},{6,4},{1,7},{3,1},{5,3},{7,5},{8,14},{10,8},{12,... | collective-permute-start | bytes 393224 | tf_op jit(solution)/shard_map/ppermute | solution.py:240
  31.3 1.0 collective-permute-start.1
  32.2 2.3 %collective-permute-done.3.refs_4_ = bf16[32,2048]{1,0:T(8,128)(2,1)S(1)} collective-permute-done((bf16[32,2048]{1,0:T(8,128)(2,1)S(1)}, bf16[32,2048]{1,0:T(8,128)(2,1)S(1)}, u32[]{:S(2)}, u32[]{:S(2)}) %collective-permute-start.3) | collective-permute-done | bytes 131104 | tf_op jit(solution)/shard_map/ppermute | solution.py:240
  34.5 2.5 %collective-permute-done.2.refs_3_ = bf16[32,2048]{1,0:T(8,128)(2,1)S(1)} collective-permute-done((bf16[32,2048]{1,0:T(8,128)(2,1)S(1)}, bf16[32,2048]{1,0:T(8,128)(2,1)S(1)}, u32[]{:S(2)}, u32[]{:S(2)}) %collective-permute-start.2) | collective-permute-done | bytes 131104 | tf_op jit(solution)/shard_map/ppermute | solution.py:240
  37.4 1.7 %shard_map.69 = (bf16[128,2048]{1,0:T(8,128)(2,1)S(1)}, bf16[128,2048]{1,0:T(8,128)(2,1)S(1)}, bf16[2048,128]{1,0:T(8,128)(2,1)S(1)}, bf16[128,1024]{1,0:T(8,128)(2,1)}) custom-call(s32[6]{0:T(128)S(1)} %stack.27.refs_0_, bf16[32,2048]{1,0:T(8,128)(2,1)S(1)} %shard_map.68.refs_1_, bf16[32,2048]{1,0:T(8,128)(2,1)S(1)} %collective-permute-done.1.refs_2_, ...), custom_call_target="tpu_custom_call" | custom-call | tf_op jit(solution)/shard_map/pallas_call | solution.py:33
  39.1 1.4 %collective-permute-start.5 = (bf16[128,1024]{1,0:T(8,128)(2,1)}, bf16[128,1024]{1,0:T(8,128)(2,1)}, u32[]{:S(2)}, u32[]{:S(2)}) collective-permute-start(bf16[128,1024]{1,0:T(8,128)(2,1)} %get-tuple-element.25), channel_id=1, source_target_pairs={{8,16},{24,32},{40,48},{56,64},{72,80},{88,96},{104,112},{16,8},{3... | collective-permute-start | bytes 786440 | tf_op jit(solution)/shard_map/ppermute | solution.py:240
  40.5 5.6 %shard_map.70 = (f32[128,2048]{1,0:T(8,128)S(1)}, f32[2048,128]{1,0:T(8,128)S(1)}) custom-call(bf16[2048,128]{1,0:T(8,128)(2,1)S(1)} %get-tuple-element.26.refs_0_.refs_8_.refs_6_, bf16[128,2048]{1,0:T(8,128)(2,1)S(1)} %get-tuple-element.23.refs_1_.refs_6_.refs_7_, bf16[128,4096]{1,0:T(8,128)(2,1)S(1)} %bitcast.19, f32[1,4096]{1,0:T(1,128)S(1)} %bitcast.24), custom_call_target="tpu_custom_call" | custom-call | tf_op jit(solution)/shard_map/pallas_call | solution.py:33
  46.1 2.3 %shard_map.71 = (bf16[2048,128]{1,0:T(8,128)(2,1)S(1)}, f32[16,2048]{1,0:T(8,128)S(1)}, f32[128,128]{1,0:T(8,128)S(1)}) custom-call(s32[6]{0:T(128)S(1)} %stack.27.refs_0_, bf16[128,2048]{1,0:T(8,128)(2,1)S(1)} %collective-permute-done.4.refs_1_, f32[128,128]{1,0:T(8,128)S(1)} %copy-done, bf16[128,2048]{1,0:T(8,128)(2,1)S(1)} %get-tuple-element.24.refs_3_, ...), custom_call_target="tpu_custom_call" | custom-call | tf_op jit(solution)/shard_map/pallas_call | solution.py:33
  48.4 4.5 %collective-permute-start.6 = (f32[128,128]{1,0:T(8,128)S(1)}, f32[128,128]{1,0:T(8,128)S(1)}, u32[]{:S(2)}, u32[]{:S(2)}) collective-permute-start(f32[128,128]{1,0:T(8,128)S(1)} %get-tuple-element.34.refs_7_), channel_id=1, source_target_pairs={{0,8},{8,0},{1,9},{9,1},{2,10},{10,2},{3,11},{11,3},{4,12},{12,4},... | collective-permute-start | bytes 196616 | tf_op jit(solution)/shard_map/ppermute | solution.py:240
  52.9 11.2 %shard_map.72 = (f32[128,4096]{1,0:T(8,128)S(1)}, bf16[128,2048]{1,0:T(8,128)(2,1)S(1)}) custom-call(bf16[2048,128]{1,0:T(8,128)(2,1)S(1)} %get-tuple-element.30.refs_0_, bf16[128,2048]{1,0:T(8,128)(2,1)S(1)} %collective-permute-done.4.refs_1_, bf16[128,4096]{1,0:T(8,128)(2,1)S(1)} %bitcast.20, f32[1,4096]{1,0:T(1,128)S(1)} %bitcast.25, ...), custom_call_target="tpu_custom_call" | custom-call | tf_op jit(solution)/shard_map/pallas_call | solution.py:33
  64.1 3.1 %shard_map.73 = (f32[128,1024]{1,0:T(8,128)S(1)}, f32[2048,128]{1,0:T(8,128)S(1)}) custom-call(bf16[2048,128]{1,0:T(8,128)(2,1)S(1)} %get-tuple-element.26.refs_0_.refs_8_.refs_6_, bf16[128,2048]{1,0:T(8,128)(2,1)S(1)} %get-tuple-element.23.refs_1_.refs_6_.refs_7_, bf16[128,4096]{1,0:T(8,128)(2,1)S(1)} %bitcast.21, f32[1,4096]{1,0:T(1,128)S(1)} %bitcast.26, ...), custom_call_target="tpu_custom_call" | custom-call | tf_op jit(solution)/shard_map/pallas_call | solution.py:33
  67.2 4.4 %shard_map.74 = (bf16[128,4096]{1,0:T(8,128)(2,1)}, f32[2048,128]{1,0:T(8,128)S(1)}) custom-call(bf16[2048,128]{1,0:T(8,128)(2,1)S(1)} %get-tuple-element.26.refs_0_.refs_8_.refs_6_, bf16[128,2048]{1,0:T(8,128)(2,1)S(1)} %get-tuple-element.23.refs_1_.refs_6_.refs_7_, bf16[128,4096]{1,0:T(8,128)(2,1)S(1)} %bitcast.22, f32[1,4096]{1,0:T(1,128)S(1)} %bitcast.27, ...), custom_call_target="tpu_custom_call" | custom-call | tf_op jit(solution)/shard_map/pallas_call | solution.py:33
  71.7 4.7 %all-to-all-start.1 = ((bf16[16,8,4096]{2,1,0:T(8,128)(2,1)}), bf16[16,8,4096]{2,1,0:T(8,128)(2,1)S(1)}, u32[]{:S(2)}, u32[]{:S(2)}) async-start(bf16[16,8,4096]{2,1,0:T(8,128)(2,1)} %bitcast.30), calls=%async_computation.1 | async-start | bytes 2097152 | tf_op jit(solution)/shard_map/all_to_all | solution.py:316
  76.9 1.6 %collective-permute-done.7.refs_2_ = bf16[128,2048]{1,0:T(8,128)(2,1)S(1)} collective-permute-done((bf16[128,2048]{1,0:T(8,128)(2,1)S(1)}, bf16[128,2048]{1,0:T(8,128)(2,1)S(1)}, u32[]{:S(2)}, u32[]{:S(2)}) %collective-permute-start.7) | collective-permute-done | bytes 524320 | tf_op jit(solution)/shard_map/ppermute | solution.py:240
  80.0 2.7 %collective-permute-start.9 = (bf16[32,2048]{1,0:T(8,128)(2,1)S(1)}, bf16[32,2048]{1,0:T(8,128)(2,1)S(1)}, u32[]{:S(2)}, u32[]{:S(2)}) collective-permute-start(bf16[32,2048]{1,0:T(8,128)(2,1)S(1)} %get-tuple-element.39), channel_id=1, source_target_pairs={{0,6},{2,0},{4,2},{6,4},{1,7},{3,1},{5,3},{7,5},{8,14},{10,8},{12,... | collective-permute-start | bytes 393224 | tf_op jit(solution)/shard_map/ppermute | solution.py:240
  83.5 2.9 %collective-permute-done.8.refs_2_ = bf16[32,2048]{1,0:T(8,128)(2,1)S(1)} collective-permute-done((bf16[32,2048]{1,0:T(8,128)(2,1)S(1)}, bf16[32,2048]{1,0:T(8,128)(2,1)S(1)}, u32[]{:S(2)}, u32[]{:S(2)}) %collective-permute-start.8) | collective-permute-done | bytes 131104 | tf_op jit(solution)/shard_map/ppermute | solution.py:240
  86.4 2.1 %collective-permute-done.9.refs_3_ = bf16[32,2048]{1,0:T(8,128)(2,1)S(1)} collective-permute-done((bf16[32,2048]{1,0:T(8,128)(2,1)S(1)}, bf16[32,2048]{1,0:T(8,128)(2,1)S(1)}, u32[]{:S(2)}, u32[]{:S(2)}) %collective-permute-start.9) | collective-permute-done | bytes 131104 | tf_op jit(solution)/shard_map/ppermute | solution.py:240
  90.0 2.1 %collective-permute-start.11 = (bf16[16,2048]{1,0:T(8,128)(2,1)S(1)}, bf16[16,2048]{1,0:T(8,128)(2,1)S(1)}, u32[]{:S(2)}, u32[]{:S(2)}) collective-permute-start(bf16[16,2048]{1,0:T(8,128)(2,1)S(1)} %get-tuple-element.42), channel_id=1, source_target_pairs={{0,1},{1,0},{2,3},{3,2},{4,5},{5,4},{6,7},{7,6},{8,9},{9,8},{10,11... | collective-permute-start | bytes 196616 | tf_op jit(solution)/shard_map/ppermute | solution.py:240
  92.1 3.8 %collective-permute-done.11.refs_2_ = bf16[16,2048]{1,0:T(8,128)(2,1)S(1)} collective-permute-done((bf16[16,2048]{1,0:T(8,128)(2,1)S(1)}, bf16[16,2048]{1,0:T(8,128)(2,1)S(1)}, u32[]{:S(2)}, u32[]{:S(2)}) %collective-permute-start.11) | collective-permute-done | bytes 65568 | tf_op jit(solution)/shard_map/ppermute | solution.py:240
  (31 shorter events, 7.1 us)
Async XLA Ops:
  0.6 8.5 %copy-start.4 = (bf16[16,2,8,128]{3,2,1,0:T(8,128)(2,1)S(1)}, bf16[16,2,8,128]{3,2,1,0:T(8,128)(2,1)}, u32[]{:S(2)}) copy-start(bf16[16,2,8,128]{3,2,1,0:T(8,128)(2,1)} %param.5) | copy-start | bytes 196612
  0.6 36.8 %copy-start = (f32[128,128]{1,0:T(8,128)S(1)}, f32[128,128]{1,0:T(8,128)}, u32[]{:S(2)}) copy-start(f32[128,128]{1,0:T(8,128)} %refs_9_.1) | copy-start | bytes 196612
  0.7 39.8 %copy-start.5 = (s32[8192]{0:T(1024)S(1)}, s32[8192]{0:T(1024)}, u32[]{:S(2)}) copy-start(s32[8192]{0:T(1024)} %param.9) | copy-start | bytes 98308
  2.7 37.8 %all-to-all-start = ((bf16[16,8,4096]{2,1,0:T(8,128)(2,1)}), bf16[16,8,4096]{2,1,0:T(8,128)(2,1)S(1)}, u32[]{:S(2)}, u32[]{:S(2)}) async-start(bf16[16,8,4096]{2,1,0:T(8,128)(2,1)} %bitcast.8), calls=%async_computation | async-start | bytes 2097152 | tf_op jit(solution)/shard_map/all_to_all | solution.py:265
  9.2 36.9 %copy-start.1 = (s32[6,2,8,128]{3,2,1,0:T(8,128)S(1)}, s32[6,2,8,128]{3,2,1,0:T(8,128)}, u32[]{:S(2)}) copy-start(s32[6,2,8,128]{3,2,1,0:T(8,128)} %refs_5_.3) | copy-start | bytes 147460
  9.2 17.1 %collective-permute-start = (bf16[16,2048]{1,0:T(8,128)(2,1)S(1)}, bf16[16,2048]{1,0:T(8,128)(2,1)S(1)}, u32[]{:S(2)}, u32[]{:S(2)}) collective-permute-start(bf16[16,2048]{1,0:T(8,128)(2,1)S(1)} %bitcast.28), channel_id=1, source_target_pairs={{0,1},{1,0},{2,3},{3,2},{4,5},{5,4},{6,7},{7,6},{8,9},{9,8},{10,11... | collective-permute-start | bytes 196616 | tf_op jit(solution)/shard_map/ppermute | solution.py:240
  26.9 7.6 %collective-permute-start.3 = (bf16[32,2048]{1,0:T(8,128)(2,1)S(1)}, bf16[32,2048]{1,0:T(8,128)(2,1)S(1)}, u32[]{:S(2)}, u32[]{:S(2)}) collective-permute-start(bf16[32,2048]{1,0:T(8,128)(2,1)S(1)} %shard_map.68.refs_1_), channel_id=1, source_target_pairs={{0,4},{2,6},{4,0},{6,2},{1,5},{3,7},{5,1},{7,3},{8,12},{10,14},{12... | collective-permute-start | bytes 393224 | tf_op jit(solution)/shard_map/ppermute | solution.py:240
  30.2 6.8 %collective-permute-start.2 = (bf16[32,2048]{1,0:T(8,128)(2,1)S(1)}, bf16[32,2048]{1,0:T(8,128)(2,1)S(1)}, u32[]{:S(2)}, u32[]{:S(2)}) collective-permute-start(bf16[32,2048]{1,0:T(8,128)(2,1)S(1)} %shard_map.68.refs_1_), channel_id=1, source_target_pairs={{0,6},{2,0},{4,2},{6,4},{1,7},{3,1},{5,3},{7,5},{8,14},{10,8},{12,... | collective-permute-start | bytes 393224 | tf_op jit(solution)/shard_map/ppermute | solution.py:240
  31.3 6.2 %collective-permute-start.1 = (bf16[32,2048]{1,0:T(8,128)(2,1)S(1)}, bf16[32,2048]{1,0:T(8,128)(2,1)S(1)}, u32[]{:S(2)}, u32[]{:S(2)}) collective-permute-start(bf16[32,2048]{1,0:T(8,128)(2,1)S(1)} %shard_map.68.refs_1_), channel_id=1, source_target_pairs={{0,2},{2,4},{4,6},{6,0},{1,3},{3,5},{5,7},{7,1},{8,10},{10,12},{12... | collective-permute-start | bytes 393224 | tf_op jit(solution)/shard_map/ppermute | solution.py:240
  39.1 7.0 %collective-permute-start.4 = (bf16[128,2048]{1,0:T(8,128)(2,1)S(1)}, bf16[128,2048]{1,0:T(8,128)(2,1)S(1)}, u32[]{:S(2)}, u32[]{:S(2)}) collective-permute-start(bf16[128,2048]{1,0:T(8,128)(2,1)S(1)} %get-tuple-element.23.refs_1_.refs_6_.refs_7_), channel_id=1, source_target_pairs={{0,8},{8,0},{1,9},{9,1},{2,10},{10,2},{3,11},{11,3},{4,12},{12,4},... | collective-permute-start | bytes 1572872 | tf_op jit(solution)/shard_map/ppermute | solution.py:240
  39.1 7.0 %collective-permute-start.5 = (bf16[128,1024]{1,0:T(8,128)(2,1)}, bf16[128,1024]{1,0:T(8,128)(2,1)}, u32[]{:S(2)}, u32[]{:S(2)}) collective-permute-start(bf16[128,1024]{1,0:T(8,128)(2,1)} %get-tuple-element.25), channel_id=1, source_target_pairs={{8,16},{24,32},{40,48},{56,64},{72,80},{88,96},{104,112},{16,8},{3... | collective-permute-start | bytes 786440 | tf_op jit(solution)/shard_map/ppermute | solution.py:240
  48.4 18.8 %collective-permute-start.6 = (f32[128,128]{1,0:T(8,128)S(1)}, f32[128,128]{1,0:T(8,128)S(1)}, u32[]{:S(2)}, u32[]{:S(2)}) collective-permute-start(f32[128,128]{1,0:T(8,128)S(1)} %get-tuple-element.34.refs_7_), channel_id=1, source_target_pairs={{0,8},{8,0},{1,9},{9,1},{2,10},{10,2},{3,11},{11,3},{4,12},{12,4},... | collective-permute-start | bytes 196616 | tf_op jit(solution)/shard_map/ppermute | solution.py:240
  64.1 3.1 %copy-start.2 = (bf16[128,2048]{1,0:T(8,128)(2,1)}, bf16[128,2048]{1,0:T(8,128)(2,1)S(1)}, u32[]{:S(2)}) copy-start(bf16[128,2048]{1,0:T(8,128)(2,1)S(1)} %get-tuple-element.36) | copy-start | bytes 1572868
  71.7 4.7 %copy-start.3 = (bf16[128,2048]{1,0:T(8,128)(2,1)S(1)}, bf16[128,2048]{1,0:T(8,128)(2,1)}, u32[]{:S(2)}) copy-start(bf16[128,2048]{1,0:T(8,128)(2,1)} %copy-done.2) | copy-start | bytes 1572868
  71.7 24.9 %all-to-all-start.1 = ((bf16[16,8,4096]{2,1,0:T(8,128)(2,1)}), bf16[16,8,4096]{2,1,0:T(8,128)(2,1)S(1)}, u32[]{:S(2)}, u32[]{:S(2)}) async-start(bf16[16,8,4096]{2,1,0:T(8,128)(2,1)} %bitcast.30), calls=%async_computation.1 | async-start | bytes 2097152 | tf_op jit(solution)/shard_map/all_to_all | solution.py:316
  76.4 2.1 %collective-permute-start.7 = (bf16[128,2048]{1,0:T(8,128)(2,1)S(1)}, bf16[128,2048]{1,0:T(8,128)(2,1)S(1)}, u32[]{:S(2)}, u32[]{:S(2)}) collective-permute-start(bf16[128,2048]{1,0:T(8,128)(2,1)S(1)} %copy-done.3), channel_id=1, source_target_pairs={{0,8},{8,0},{1,9},{9,1},{2,10},{10,2},{3,11},{11,3},{4,12},{12,4},... | collective-permute-start | bytes 1572872 | tf_op jit(solution)/shard_map/ppermute | solution.py:240
  79.4 7.0 %collective-permute-start.8 = (bf16[32,2048]{1,0:T(8,128)(2,1)S(1)}, bf16[32,2048]{1,0:T(8,128)(2,1)S(1)}, u32[]{:S(2)}, u32[]{:S(2)}) collective-permute-start(bf16[32,2048]{1,0:T(8,128)(2,1)S(1)} %get-tuple-element.38), channel_id=1, source_target_pairs={{0,2},{2,4},{4,6},{6,0},{1,3},{3,5},{5,7},{7,1},{8,10},{10,12},{12... | collective-permute-start | bytes 393224 | tf_op jit(solution)/shard_map/ppermute | solution.py:240
  80.0 8.5 %collective-permute-start.9 = (bf16[32,2048]{1,0:T(8,128)(2,1)S(1)}, bf16[32,2048]{1,0:T(8,128)(2,1)S(1)}, u32[]{:S(2)}, u32[]{:S(2)}) collective-permute-start(bf16[32,2048]{1,0:T(8,128)(2,1)S(1)} %get-tuple-element.39), channel_id=1, source_target_pairs={{0,6},{2,0},{4,2},{6,4},{1,7},{3,1},{5,3},{7,5},{8,14},{10,8},{12,... | collective-permute-start | bytes 393224 | tf_op jit(solution)/shard_map/ppermute | solution.py:240
  82.7 6.6 %collective-permute-start.10 = (bf16[32,2048]{1,0:T(8,128)(2,1)S(1)}, bf16[32,2048]{1,0:T(8,128)(2,1)S(1)}, u32[]{:S(2)}, u32[]{:S(2)}) collective-permute-start(bf16[32,2048]{1,0:T(8,128)(2,1)S(1)} %get-tuple-element.40), channel_id=1, source_target_pairs={{0,4},{2,6},{4,0},{6,2},{1,5},{3,7},{5,1},{7,3},{8,12},{10,14},{12... | collective-permute-start | bytes 393224 | tf_op jit(solution)/shard_map/ppermute | solution.py:240
  90.0 5.8 %collective-permute-start.11 = (bf16[16,2048]{1,0:T(8,128)(2,1)S(1)}, bf16[16,2048]{1,0:T(8,128)(2,1)S(1)}, u32[]{:S(2)}, u32[]{:S(2)}) collective-permute-start(bf16[16,2048]{1,0:T(8,128)(2,1)S(1)} %get-tuple-element.42), channel_id=1, source_target_pairs={{0,1},{1,0},{2,3},{3,2},{4,5},{5,4},{6,7},{7,6},{8,9},{9,8},{10,11... | collective-permute-start | bytes 196616 | tf_op jit(solution)/shard_map/ppermute | solution.py:240

commit v4 on v0

--- a/solution.py
+++ b/solution.py
@@ -41,17 +41,20 @@
     )(*scalars, *args, *held)
 
 
-def head_body(u_ref, v_ref, flat_ref, out_ref, u_s):
-    _, depth, rows, cols = u_ref.shape
-    u_s[...] = u_ref[...].astype(f32)
-    for x in range(depth):
-        for y in range(rows):
-            at = (x * rows + y) * cols
-            flat_ref[:, at : at + cols] = u_s[:, x, y, :].astype(bf16)
-    half = out_ref.shape[-1]
-    for k in range(out_ref.shape[0]):
-        out_ref[k, 0] = v_ref[:, :half]
-        out_ref[k, 1] = v_ref[:, half:]
+def fan_body(v_hbm, out_hbm, v_s, read_sem, sems):
+    chips, parts, _, half = out_hbm.shape
+    read = pltpu.make_async_copy(v_hbm, v_s, read_sem)
+    read.start()
+    read.wait()
+    writes = [
+        pltpu.make_async_copy(v_s.at[:, p * half : (p + 1) * half], out_hbm.at[k, p], sems.at[k * parts + p])
+        for k in range(chips)
+        for p in range(parts)
+    ]
+    for write in writes:
+        write.start()
+    for write in writes:
+        write.wait()
 
 
 def prep_body(at_ref, u_ref, w_ref, a_ref, b_ref, c_ref, core_ref, full_ref, k_ref, kt_ref, halo_ref):
@@ -82,12 +85,24 @@
         halo_ref[...] = k_own[:, half:]
 
 
-def mid_body(rows, cols, c_ref, oth_ref, core_ref, k_ref, halo_ref, face_ref, u_ref, kt_ref, base_ref, m_ref, base_s, lap_s):
-    half = oth_ref.shape[1] // 2
+def other_body(at_ref, oth_ref, core_ref, kt_ref, near_ref):
+    half = near_ref.shape[1]
     k_oth = dot(core_ref[...].astype(bf16), oth_ref[...], 0, 0).astype(bf16)
     kt_ref[...] = k_oth.T
+    first = at_ref[0] == 0
+
+    @pl.when(first)
+    def _():
+        near_ref[...] = k_oth[:, :half]
+
+    @pl.when(jnp.logical_not(first))
+    def _():
+        near_ref[...] = k_oth[:, half:]
+
+
+def lap_body(rows, cols, c_ref, near_ref, k_ref, halo_ref, face_ref, u_ref, base_ref, m_ref, base_s, lap_s):
     first = c_ref[0] == 0
-    near = jnp.where(first, k_oth[:, :half].astype(f32), k_oth[:, half:].astype(f32))
+    near = near_ref[...].astype(f32)
     halo = halo_ref[...].astype(f32)
     before = jnp.where(first, halo, near)
     after = jnp.where(first, near, halo)
@@ -230,19 +245,26 @@
     where_at = jnp.stack([core_at, lax.axis_index(SAMP), lax.axis_index("y"), lax.axis_index("xh")]).astype(jnp.int32)
     swap = ring(2, 1)
 
-    u0, v_wide = small(
-        head_body,
-        [basis_u, basis_v],
-        [((narrow, cells), bf16, True), ((n_space // 2, 2, lanes, half), bf16, False)],
-        [(basis_u.shape, f32)],
-    )
+    u0 = basis_u.reshape(narrow, cells)
+    anywhere = pl.BlockSpec(memory_space=pl.ANY)
+    v_wide = pl.pallas_call(
+        fan_body,
+        in_specs=[anywhere],
+        out_specs=anywhere,
+        out_shape=jax.ShapeDtypeStruct((n_space // 2, 2, lanes, half), bf16),
+        scratch_shapes=[
+            pltpu.VMEM(basis_v.shape, bf16),
+            pltpu.SemaphoreType.DMA,
+            pltpu.SemaphoreType.DMA((n_space,)),
+        ],
+    )(basis_v)
     v = resident(lax.all_to_all(v_wide.reshape(rank, half), SPACE, 0, 0, tiled=True))
     u1 = lax.ppermute(u0, "xh", swap)
     pair = jnp.concatenate([u0, u1], 0)
     around = [resident(lax.ppermute(pair, "y", ring(4, k))) for k in (1, 3, 2)]
     u_own, k_own, kt_own, edge = small(
         prep_body,
-        [u0, resident(u1), *around, core_s],
+        [resident(u0), resident(u1), *around, core_s],
         [((rank, cells), bf16, True), ((rank, cells), bf16, True), ((cells, rank), bf16, True), ((rank, cells // 2), bf16, True)],
         at=where_at,
     )
@@ -256,16 +278,26 @@
     scale = step_size * cell_weight
     quart = half // 2
     main = lambda start, kinds, back: functools.partial(part_body, start, kinds, back)
+    kt_oth, near = small(
+        other_body,
+        [u_oth, core_s],
+        [((cells, rank), bf16, True), ((rank, cells // 2), bf16, True)],
+        at=where_at,
+        held=(k_own, kt_own, u_own),
+    )
     l_first, ov_first = small(
-        main(0, 0, False), [kt_own, u_own, v, growth], [((rank, quart), f32, True), ((cells, rank), f32, True)]
-    )
-    kt_oth, base, m_own = small(
-        functools.partial(mid_body, rows_y, cols_z),
-        [u_oth, core_s, k_own, halo, face_class, u_own],
-        [((cells, rank), bf16, True), ((narrow, cells), f32, False), ((rank, rank), f32, True)],
+        main(0, 0, False),
+        [kt_own, u_own, v, growth],
+        [((rank, quart), f32, True), ((cells, rank), f32, True)],
+        held=(kt_oth, near, k_own),
+    )
+    base, m_own = small(
+        functools.partial(lap_body, rows_y, cols_z),
+        [near, k_own, halo, face_class, u_own],
+        [((narrow, cells), f32, False), ((rank, rank), f32, True)],
         [((rank, cells), f32), ((rank, cells), bf16)],
         at=where_at,
-        held=(ov_first, kt_own, l_first),
+        held=(ov_first, kt_own, l_first, kt_oth, u_oth),
     )
     m_oth = resident(lax.ppermute(m_own, "c", swap))
     l_most, ov_send = small(
@@ -273,14 +305,14 @@
         [kt_oth, u_oth, v, growth, l_first],
         [((rank, half), f32, True), ((rank, cells), bf16, True)],
         [((cells, rank), f32)],
-        held=(ov_first, kt_own, u_own),
+        held=(ov_first, kt_own, u_own, m_own),
     )
     got = resident(lax.ppermute(ov_send, "c", swap))
     l_more, ov_more = small(
         main(quart, 2, False),
         [kt_own, u_own, v, growth, ov_first],
         [((rank, quart // 2), f32, True), ((cells, rank), f32, True)],
-        held=(l_most, ov_send),
+        held=(l_most, ov_send, m_own),
     )
     rows = rank // 4
     l_part, me, up, dn, away = small(

time: 96.3 us -> 83.7 us (0.87)
  waiting for transfers between devices: 29.2 us -> 15.6 us
  Pallas kernels: 31.7 us -> 33.7 us
  starting transfers between devices: 30.6 us -> 29.4 us
  local copies, waits for them, and re-layouts: 1.79 us -> 2.8 us
    ppermute x1, waiting for transfers between devices: 14.4 us -> 0.01 us  [per_device(): u1 = lax.ppermute(u0, 'xh', swap)]
    ppermute x1, starting transfers between devices: 3.96 us -> 1.79 us  [per_device(): got = resident(lax.ppermute(ov_send, 'c', swap))]
    pallas_call x0 -> x1, Pallas kernels: none -> 2.04 us  [per_device(): pl.pallas_call(fan_body, in_specs=[anywhere], out_specs=anywhere, out_sha...]
    all_to_all x1, starting transfers between devices: 6.59 us -> 5.46 us  [per_device(): lax.all_to_all(v_wide.reshape(rank, half), SPACE, 0, 0, tiled=True)]
    unnamed x11 -> x18, local copies, waits for them, and re-layouts: 1.78 us -> 2.79 us
  transfers between devices with their start and end apart: 14 -> 14, of which waited for: 8 -> 9; matrix products, arithmetic and copies ran while one was open for 1% -> 0% of each run, Pallas kernels for 12% -> 18%
where the time goes in v4:
time: 83.7 us; the launch traced here: 83.3 us
  Pallas kernels  33.7 us (40%)
  starting transfers between devices  29.4 us (35%)
  waiting for transfers between devices  15.6 us (19%)
  local copies, waits for them, and re-layouts  2.8 us (3%)
  other arithmetic  0.92 us (1%)
    pallas_call x9, Pallas kernels, small(): pl.pallas_call(reading, in_specs=[pl.BlockSpec(memory_space=pltpu.SMEM)]...  31.7 us
    ppermute x3, waiting for transfers between devices, per_device(): lax.ppermute(part, 'y', ring(4, k))  5.77 us
    all_to_all x1, starting transfers between devices, per_device(): lax.all_to_all(v_wide.reshape(rank, half), SPACE, 0, 0, tiled=True)  5.46 us
    ppermute x3, waiting for transfers between devices, per_device(): around = [resident(lax.ppermute(pair, 'y', ring(4, k))) for k in (1, 3, 2)]  5.41 us
    ppermute x3, starting transfers between devices, per_device(): around = [resident(lax.ppermute(pair, 'y', ring(4, k))) for k in (1, 3, 2)]  5.3 us
    all_to_all x1, starting transfers between devices, per_device(): l_got = lax.all_to_all(l_part, SPACE, 0, 0, tiled=True)  5.08 us
    ppermute x3, starting transfers between devices, per_device(): lax.ppermute(part, 'y', ring(4, k))  4.69 us
    ppermute x1, waiting for transfers between devices, per_device(): lax.ppermute(send, 'xh', swap)  3.75 us
  transfers between devices with their start and end apart: 14, of which 9 were waited for; matrix products, arithmetic and copies ran while one was open for 0% of the time, Pallas kernels for 18%

profile of v4, /device:TPU:0, one launch (start us, length us, event | category | flops | bytes accessed | tf_op | source)
XLA Modules:
  0.0 83.3 jit_solution(2613707137843840463)
XLA Ops:
  1.6 3.2 %collective-permute-start = (bf16[16,2048]{1,0:T(8,128)(2,1)S(1)}, bf16[16,2048]{1,0:T(8,128)(2,1)S(1)}, u32[]{:S(2)}, u32[]{:S(2)}) collective-permute-start(bf16[16,2048]{1,0:T(8,128)(2,1)S(1)} %bitcast.28), channel_id=1, source_target_pairs={{0,1},{1,0},{2,3},{3,2},{4,5},{5,4},{6,7},{7,6},{8,9},{9,8},{10,11... | collective-permute-start | bytes 196616 | tf_op jit(solution)/shard_map/ppermute | solution.py:262
  4.8 2.0 %shard_map.70 = bf16[8,2,8,4096]{3,2,1,0:T(8,128)(2,1)} custom-call(bf16[8,8192]{1,0:T(8,128)(2,1)} %v_hbm.1), custom_call_target="tpu_custom_call" | custom-call | tf_op jit(solution)/shard_map/pallas_call | solution.py:250
  6.8 5.5 %all-to-all-start = ((bf16[16,8,4096]{2,1,0:T(8,128)(2,1)}), bf16[16,8,4096]{2,1,0:T(8,128)(2,1)S(1)}, u32[]{:S(2)}, u32[]{:S(2)}) async-start(bf16[16,8,4096]{2,1,0:T(8,128)(2,1)} %bitcast.31), calls=%async_computation | async-start | bytes 2097152 | tf_op jit(solution)/shard_map/all_to_all | solution.py:261
  12.4 3.3 %collective-permute-start.3 = (bf16[32,2048]{1,0:T(8,128)(2,1)S(1)}, bf16[32,2048]{1,0:T(8,128)(2,1)S(1)}, u32[]{:S(2)}, u32[]{:S(2)}) collective-permute-start(bf16[32,2048]{1,0:T(8,128)(2,1)S(1)} %constant_dynamic-update-slice_fusion), channel_id=1, source_target_pairs={{0,4},{2,6},{4,0},{6,2},{1,5},{3,7},{5,1},{7,3},{8,12},{10,14},{12... | collective-permute-start | bytes 393224 | tf_op jit(solution)/shard_map/ppermute | solution.py:264
  17.7 2.6 %collective-permute-done.3.refs_5_ = bf16[32,2048]{1,0:T(8,128)(2,1)S(1)} collective-permute-done((bf16[32,2048]{1,0:T(8,128)(2,1)S(1)}, bf16[32,2048]{1,0:T(8,128)(2,1)S(1)}, u32[]{:S(2)}, u32[]{:S(2)}) %collective-permute-start.3) | collective-permute-done | bytes 131104 | tf_op jit(solution)/shard_map/ppermute | solution.py:264
  20.3 2.6 %collective-permute-done.2.refs_4_ = bf16[32,2048]{1,0:T(8,128)(2,1)S(1)} collective-permute-done((bf16[32,2048]{1,0:T(8,128)(2,1)S(1)}, bf16[32,2048]{1,0:T(8,128)(2,1)S(1)}, u32[]{:S(2)}, u32[]{:S(2)}) %collective-permute-start.2) | collective-permute-done | bytes 131104 | tf_op jit(solution)/shard_map/ppermute | solution.py:264
  23.2 1.7 %shard_map.68 = (bf16[128,2048]{1,0:T(8,128)(2,1)S(1)}, bf16[128,2048]{1,0:T(8,128)(2,1)S(1)}, bf16[2048,128]{1,0:T(8,128)(2,1)S(1)}, bf16[128,1024]{1,0:T(8,128)(2,1)}) custom-call(s32[4]{0:T(128)S(1)} %pad_add_fusion.refs_0_, bf16[16,2048]{1,0:T(8,128)(2,1)S(1)} %bitcast.29, bf16[16,2048]{1,0:T(8,128)(2,1)S(1)} %collective-permute-done.refs_2_, ...), custom_call_target="tpu_custom_call" | custom-call | tf_op jit(solution)/shard_map/pallas_call | solution.py:33
  24.8 1.4 %collective-permute-start.5 = (bf16[128,1024]{1,0:T(8,128)(2,1)}, bf16[128,1024]{1,0:T(8,128)(2,1)}, u32[]{:S(2)}, u32[]{:S(2)}) collective-permute-start(bf16[128,1024]{1,0:T(8,128)(2,1)} %get-tuple-element.27), channel_id=1, source_target_pairs={{8,16},{24,32},{40,48},{56,64},{72,80},{88,96},{104,112},{16,8},{3... | collective-permute-start | bytes 786440 | tf_op jit(solution)/shard_map/ppermute | solution.py:274
  26.7 1.1 %shard_map.69 = (bf16[2048,128]{1,0:T(8,128)(2,1)S(1)}, bf16[128,1024]{1,0:T(8,128)(2,1)S(1)}) custom-call(s32[4]{0:T(128)S(1)} %pad_add_fusion.refs_0_, bf16[128,2048]{1,0:T(8,128)(2,1)S(1)} %collective-permute-done.4.refs_1_.refs_10_, f32[128,128]{1,0:T(8,128)S(1)} %copy-done.3, bf16[128,2048]{1,0:T(8,128)(2,1)S(1)} %get-tuple-element.24.refs_3_.refs_6_.refs_2_, ...), custom_call_target="tpu_custom_call" | custom-call | tf_op jit(solution)/shard_map/pallas_call | solution.py:33
  29.9 5.6 %shard_map.71 = (f32[128,2048]{1,0:T(8,128)S(1)}, f32[2048,128]{1,0:T(8,128)S(1)}) custom-call(bf16[2048,128]{1,0:T(8,128)(2,1)S(1)} %get-tuple-element.25.refs_4_.refs_0_.refs_7_.refs_6_.refs_1_, bf16[128,2048]{1,0:T(8,128)(2,1)S(1)} %get-tuple-element.23.refs_5_.refs_1_.refs_7_.refs_2_, bf16[128,4096]{1,0:T(8,128)(2,1)S(1)} %bitcast.20, ...), custom_call_target="tpu_custom_call" | custom-call | tf_op jit(solution)/shard_map/pallas_call | solution.py:33
  35.5 2.6 %shard_map.72 = (f32[16,2048]{1,0:T(8,128)}, f32[128,128]{1,0:T(8,128)S(1)}) custom-call(s32[4]{0:T(128)S(1)} %pad_add_fusion.refs_0_, bf16[128,1024]{1,0:T(8,128)(2,1)S(1)} %get-tuple-element.26.refs_5_.refs_1_, bf16[128,2048]{1,0:T(8,128)(2,1)S(1)} %get-tuple-element.24.refs_3_.refs_6_.refs_2_, bf16[128,1024]{1,0:T(8,128)(2,1)} %collective-permute-done.5.refs_3_, ...), custom_call_target="tpu_custom_call" | custom-call | tf_op jit(solution)/shard_map/pallas_call | solution.py:33
  38.1 11.4 %shard_map.73 = (f32[128,4096]{1,0:T(8,128)S(1)}, bf16[128,2048]{1,0:T(8,128)(2,1)S(1)}) custom-call(bf16[2048,128]{1,0:T(8,128)(2,1)S(1)} %copy-done.2, bf16[128,2048]{1,0:T(8,128)(2,1)S(1)} %collective-permute-done.4.refs_1_.refs_10_, bf16[128,4096]{1,0:T(8,128)(2,1)S(1)} %bitcast.21, f32[1,4096]{1,0:T(1,128)S(1)} %bitcast.25, ...), custom_call_target="tpu_custom_call" | custom-call | tf_op jit(solution)/shard_map/pallas_call | solution.py:33
  49.6 1.8 %collective-permute-start.6 = (bf16[128,2048]{1,0:T(8,128)(2,1)S(1)}, bf16[128,2048]{1,0:T(8,128)(2,1)S(1)}, u32[]{:S(2)}, u32[]{:S(2)}) collective-permute-start(bf16[128,2048]{1,0:T(8,128)(2,1)S(1)} %get-tuple-element.34.refs_6_), channel_id=1, source_target_pairs={{0,8},{8,0},{1,9},{9,1},{2,10},{10,2},{3,11},{11,3},{4,12},{12,4},... | collective-permute-start | bytes 1572872 | tf_op jit(solution)/shard_map/ppermute | solution.py:310
  51.7 2.9 %shard_map.74 = (f32[128,1024]{1,0:T(8,128)S(1)}, f32[2048,128]{1,0:T(8,128)S(1)}) custom-call(bf16[2048,128]{1,0:T(8,128)(2,1)S(1)} %get-tuple-element.25.refs_4_.refs_0_.refs_7_.refs_6_.refs_1_, bf16[128,2048]{1,0:T(8,128)(2,1)S(1)} %get-tuple-element.23.refs_5_.refs_1_.refs_7_.refs_2_, bf16[128,4096]{1,0:T(8,128)(2,1)S(1)} %bitcast.22, ...), custom_call_target="tpu_custom_call" | custom-call | tf_op jit(solution)/shard_map/pallas_call | solution.py:33
  54.6 5.0 %shard_map.75 = (bf16[128,4096]{1,0:T(8,128)(2,1)}, f32[32,2048]{1,0:T(8,128)S(1)}, bf16[32,2048]{1,0:T(8,128)(2,1)S(1)}, bf16[32,2048]{1,0:T(8,128)(2,1)S(1)}, bf16[32,2048]{1,0:T(8,128)(2,1)S(1)}) custom-call(s32[4]{0:T(128)S(1)} %pad_add_fusion.refs_0_, bf16[2048,128]{1,0:T(8,128)(2,1)S(1)} %get-tuple-element.25.refs_4_.refs_0_.refs_7_.refs_6_.refs_1_, ...), custom_call_target="tpu_custom_call" | custom-call | tf_op jit(solution)/shard_map/pallas_call | solution.py:33
  59.6 5.1 %all-to-all-start.1 = ((bf16[16,8,4096]{2,1,0:T(8,128)(2,1)}), bf16[16,8,4096]{2,1,0:T(8,128)(2,1)S(1)}, u32[]{:S(2)}, u32[]{:S(2)}) async-start(bf16[16,8,4096]{2,1,0:T(8,128)(2,1)} %bitcast.32), calls=%async_computation.1 | async-start | bytes 2097152 | tf_op jit(solution)/shard_map/all_to_all | solution.py:326
  64.7 1.1 %collective-permute-start.8 = (bf16[32,2048]{1,0:T(8,128)(2,1)S(1)}, bf16[32,2048]{1,0:T(8,128)(2,1)S(1)}, u32[]{:S(2)}, u32[]{:S(2)}) collective-permute-start(bf16[32,2048]{1,0:T(8,128)(2,1)S(1)} %get-tuple-element.38), channel_id=1, source_target_pairs={{0,2},{2,4},{4,6},{6,0},{1,3},{3,5},{5,7},{7,1},{8,10},{10,12},{12... | collective-permute-start | bytes 393224 | tf_op jit(solution)/shard_map/ppermute | solution.py:330
  65.8 2.2 %collective-permute-start.9 = (bf16[32,2048]{1,0:T(8,128)(2,1)S(1)}, bf16[32,2048]{1,0:T(8,128)(2,1)S(1)}, u32[]{:S(2)}, u32[]{:S(2)}) collective-permute-start(bf16[32,2048]{1,0:T(8,128)(2,1)S(1)} %get-tuple-element.39), channel_id=1, source_target_pairs={{0,6},{2,0},{4,2},{6,4},{1,7},{3,1},{5,3},{7,5},{8,14},{10,8},{12,... | collective-permute-start | bytes 393224 | tf_op jit(solution)/shard_map/ppermute | solution.py:330
  68.0 1.4 %collective-permute-start.10 = (bf16[32,2048]{1,0:T(8,128)(2,1)S(1)}, bf16[32,2048]{1,0:T(8,128)(2,1)S(1)}, u32[]{:S(2)}, u32[]{:S(2)}) collective-permute-start(bf16[32,2048]{1,0:T(8,128)(2,1)S(1)} %get-tuple-element.40), channel_id=1, source_target_pairs={{0,4},{2,6},{4,0},{6,2},{1,5},{3,7},{5,1},{7,3},{8,12},{10,14},{12... | collective-permute-start | bytes 393224 | tf_op jit(solution)/shard_map/ppermute | solution.py:330
  69.4 2.3 %collective-permute-done.8.refs_2_ = bf16[32,2048]{1,0:T(8,128)(2,1)S(1)} collective-permute-done((bf16[32,2048]{1,0:T(8,128)(2,1)S(1)}, bf16[32,2048]{1,0:T(8,128)(2,1)S(1)}, u32[]{:S(2)}, u32[]{:S(2)}) %collective-permute-start.8) | collective-permute-done | bytes 131104 | tf_op jit(solution)/shard_map/ppermute | solution.py:330
  71.7 2.1 %collective-permute-done.9.refs_3_ = bf16[32,2048]{1,0:T(8,128)(2,1)S(1)} collective-permute-done((bf16[32,2048]{1,0:T(8,128)(2,1)S(1)}, bf16[32,2048]{1,0:T(8,128)(2,1)S(1)}, u32[]{:S(2)}, u32[]{:S(2)}) %collective-permute-start.9) | collective-permute-done | bytes 131104 | tf_op jit(solution)/shard_map/ppermute | solution.py:330
  73.8 1.3 %collective-permute-done.10.refs_4_ = bf16[32,2048]{1,0:T(8,128)(2,1)S(1)} collective-permute-done((bf16[32,2048]{1,0:T(8,128)(2,1)S(1)}, bf16[32,2048]{1,0:T(8,128)(2,1)S(1)}, u32[]{:S(2)}, u32[]{:S(2)}) %collective-permute-start.10) | collective-permute-done | bytes 131104 | tf_op jit(solution)/shard_map/ppermute | solution.py:330
  75.8 2.1 %collective-permute-start.11 = (bf16[16,2048]{1,0:T(8,128)(2,1)S(1)}, bf16[16,2048]{1,0:T(8,128)(2,1)S(1)}, u32[]{:S(2)}, u32[]{:S(2)}) collective-permute-start(bf16[16,2048]{1,0:T(8,128)(2,1)S(1)} %get-tuple-element.42), channel_id=1, source_target_pairs={{0,1},{1,0},{2,3},{3,2},{4,5},{5,4},{6,7},{7,6},{8,9},{9,8},{10,11... | collective-permute-start | bytes 196616 | tf_op jit(solution)/shard_map/ppermute | solution.py:340
  77.9 3.8 %collective-permute-done.11.refs_2_ = bf16[16,2048]{1,0:T(8,128)(2,1)S(1)} collective-permute-done((bf16[16,2048]{1,0:T(8,128)(2,1)S(1)}, bf16[16,2048]{1,0:T(8,128)(2,1)S(1)}, u32[]{:S(2)}, u32[]{:S(2)}) %collective-permute-start.11) | collective-permute-done | bytes 65568 | tf_op jit(solution)/shard_map/ppermute | solution.py:340
  (36 shorter events, 8.4 us)
Async XLA Ops:
  0.6 11.7 %copy-start.6 = (bf16[16,2,8,128]{3,2,1,0:T(8,128)(2,1)S(1)}, bf16[16,2,8,128]{3,2,1,0:T(8,128)(2,1)}, u32[]{:S(2)}) copy-start(bf16[16,2,8,128]{3,2,1,0:T(8,128)(2,1)} %param.5) | copy-start | bytes 196612
  0.6 22.5 %copy-start.3 = (f32[128,128]{1,0:T(8,128)S(1)}, f32[128,128]{1,0:T(8,128)}, u32[]{:S(2)}) copy-start(f32[128,128]{1,0:T(8,128)} %refs_11_.1) | copy-start | bytes 196612
  1.6 24.6 %copy-start.7 = (s32[8192]{0:T(1024)S(1)}, s32[8192]{0:T(1024)}, u32[]{:S(2)}) copy-start(s32[8192]{0:T(1024)} %param.9) | copy-start | bytes 98308
  1.6 10.8 %collective-permute-start = (bf16[16,2048]{1,0:T(8,128)(2,1)S(1)}, bf16[16,2048]{1,0:T(8,128)(2,1)S(1)}, u32[]{:S(2)}, u32[]{:S(2)}) collective-permute-start(bf16[16,2048]{1,0:T(8,128)(2,1)S(1)} %bitcast.28), channel_id=1, source_target_pairs={{0,1},{1,0},{2,3},{3,2},{4,5},{5,4},{6,7},{7,6},{8,9},{9,8},{10,11... | collective-permute-start | bytes 196616 | tf_op jit(solution)/shard_map/ppermute | solution.py:262
  6.8 22.0 %all-to-all-start = ((bf16[16,8,4096]{2,1,0:T(8,128)(2,1)}), bf16[16,8,4096]{2,1,0:T(8,128)(2,1)S(1)}, u32[]{:S(2)}, u32[]{:S(2)}) async-start(bf16[16,8,4096]{2,1,0:T(8,128)(2,1)} %bitcast.31), calls=%async_computation | async-start | bytes 2097152 | tf_op jit(solution)/shard_map/all_to_all | solution.py:261
  12.4 8.0 %collective-permute-start.3 = (bf16[32,2048]{1,0:T(8,128)(2,1)S(1)}, bf16[32,2048]{1,0:T(8,128)(2,1)S(1)}, u32[]{:S(2)}, u32[]{:S(2)}) collective-permute-start(bf16[32,2048]{1,0:T(8,128)(2,1)S(1)} %constant_dynamic-update-slice_fusion), channel_id=1, source_target_pairs={{0,4},{2,6},{4,0},{6,2},{1,5},{3,7},{5,1},{7,3},{8,12},{10,14},{12... | collective-permute-start | bytes 393224 | tf_op jit(solution)/shard_map/ppermute | solution.py:264
  15.6 7.3 %collective-permute-start.2 = (bf16[32,2048]{1,0:T(8,128)(2,1)S(1)}, bf16[32,2048]{1,0:T(8,128)(2,1)S(1)}, u32[]{:S(2)}, u32[]{:S(2)}) collective-permute-start(bf16[32,2048]{1,0:T(8,128)(2,1)S(1)} %constant_dynamic-update-slice_fusion), channel_id=1, source_target_pairs={{0,6},{2,0},{4,2},{6,4},{1,7},{3,1},{5,3},{7,5},{8,14},{10,8},{12,... | collective-permute-start | bytes 393224 | tf_op jit(solution)/shard_map/ppermute | solution.py:264
  16.7 6.5 %collective-permute-start.1 = (bf16[32,2048]{1,0:T(8,128)(2,1)S(1)}, bf16[32,2048]{1,0:T(8,128)(2,1)S(1)}, u32[]{:S(2)}, u32[]{:S(2)}) collective-permute-start(bf16[32,2048]{1,0:T(8,128)(2,1)S(1)} %constant_dynamic-update-slice_fusion), channel_id=1, source_target_pairs={{0,2},{2,4},{4,6},{6,0},{1,3},{3,5},{5,7},{7,1},{8,10},{10,12},{12... | collective-permute-start | bytes 393224 | tf_op jit(solution)/shard_map/ppermute | solution.py:264
  24.8 1.9 %collective-permute-start.4 = (bf16[128,2048]{1,0:T(8,128)(2,1)S(1)}, bf16[128,2048]{1,0:T(8,128)(2,1)S(1)}, u32[]{:S(2)}, u32[]{:S(2)}) collective-permute-start(bf16[128,2048]{1,0:T(8,128)(2,1)S(1)} %get-tuple-element.23.refs_5_.refs_1_.refs_7_.refs_2_), channel_id=1, source_target_pairs={{0,8},{8,0},{1,9},{9,1},{2,10},{10,2},{3,11},{11,3},{4,12},{12,4},... | collective-permute-start | bytes 1572872 | tf_op jit(solution)/shard_map/ppermute | solution.py:271
  24.8 10.7 %collective-permute-start.5 = (bf16[128,1024]{1,0:T(8,128)(2,1)}, bf16[128,1024]{1,0:T(8,128)(2,1)}, u32[]{:S(2)}, u32[]{:S(2)}) collective-permute-start(bf16[128,1024]{1,0:T(8,128)(2,1)} %get-tuple-element.27), channel_id=1, source_target_pairs={{8,16},{24,32},{40,48},{56,64},{72,80},{88,96},{104,112},{16,8},{3... | collective-permute-start | bytes 786440 | tf_op jit(solution)/shard_map/ppermute | solution.py:274
  26.7 8.8 %copy-start.5 = (s32[6,2,8,128]{3,2,1,0:T(8,128)S(1)}, s32[6,2,8,128]{3,2,1,0:T(8,128)}, u32[]{:S(2)}) copy-start(s32[6,2,8,128]{3,2,1,0:T(8,128)} %refs_4_.1) | copy-start | bytes 147460
  27.9 0.8 copy-start
  28.8 1.0 %copy-start.1 = (bf16[2048,128]{1,0:T(8,128)(2,1)S(1)}, bf16[2048,128]{1,0:T(8,128)(2,1)}, u32[]{:S(2)}) copy-start(bf16[2048,128]{1,0:T(8,128)(2,1)} %copy-done) | copy-start | bytes 1572868
  29.9 5.6 %copy-start.2 = (bf16[2048,128]{1,0:T(8,128)(2,1)S(1)}, bf16[2048,128]{1,0:T(8,128)(2,1)}, u32[]{:S(2)}) copy-start(bf16[2048,128]{1,0:T(8,128)(2,1)} %copy-done) | copy-start | bytes 1572868
  49.6 5.0 %collective-permute-start.6 = (bf16[128,2048]{1,0:T(8,128)(2,1)S(1)}, bf16[128,2048]{1,0:T(8,128)(2,1)S(1)}, u32[]{:S(2)}, u32[]{:S(2)}) collective-permute-start(bf16[128,2048]{1,0:T(8,128)(2,1)S(1)} %get-tuple-element.34.refs_6_), channel_id=1, source_target_pairs={{0,8},{8,0},{1,9},{9,1},{2,10},{10,2},{3,11},{11,3},{4,12},{12,4},... | collective-permute-start | bytes 1572872 | tf_op jit(solution)/shard_map/ppermute | solution.py:310
  51.4 3.2 %collective-permute-start.7 = (f32[128,128]{1,0:T(8,128)S(1)}, f32[128,128]{1,0:T(8,128)S(1)}, u32[]{:S(2)}, u32[]{:S(2)}) collective-permute-start(f32[128,128]{1,0:T(8,128)S(1)} %get-tuple-element.32.refs_8_.refs_7_.refs_9_), channel_id=1, source_target_pairs={{0,8},{8,0},{1,9},{9,1},{2,10},{10,2},{3,11},{11,3},{4,12},{12,4},... | collective-permute-start | bytes 196616 | tf_op jit(solution)/shard_map/ppermute | solution.py:302
  59.6 22.0 %copy-start.4 = (f32[16,2048]{1,0:T(8,128)S(1)}, f32[16,2048]{1,0:T(8,128)}, u32[]{:S(2)}) copy-start(f32[16,2048]{1,0:T(8,128)} %get-tuple-element.31.refs_0_) | copy-start | bytes 393220
  59.6 22.8 %all-to-all-start.1 = ((bf16[16,8,4096]{2,1,0:T(8,128)(2,1)}), bf16[16,8,4096]{2,1,0:T(8,128)(2,1)S(1)}, u32[]{:S(2)}, u32[]{:S(2)}) async-start(bf16[16,8,4096]{2,1,0:T(8,128)(2,1)} %bitcast.32), calls=%async_computation.1 | async-start | bytes 2097152 | tf_op jit(solution)/shard_map/all_to_all | solution.py:326
  64.7 7.0 %collective-permute-start.8 = (bf16[32,2048]{1,0:T(8,128)(2,1)S(1)}, bf16[32,2048]{1,0:T(8,128)(2,1)S(1)}, u32[]{:S(2)}, u32[]{:S(2)}) collective-permute-start(bf16[32,2048]{1,0:T(8,128)(2,1)S(1)} %get-tuple-element.38), channel_id=1, source_target_pairs={{0,2},{2,4},{4,6},{6,0},{1,3},{3,5},{5,7},{7,1},{8,10},{10,12},{12... | collective-permute-start | bytes 393224 | tf_op jit(solution)/shard_map/ppermute | solution.py:330
  65.8 8.0 %collective-permute-start.9 = (bf16[32,2048]{1,0:T(8,128)(2,1)S(1)}, bf16[32,2048]{1,0:T(8,128)(2,1)S(1)}, u32[]{:S(2)}, u32[]{:S(2)}) collective-permute-start(bf16[32,2048]{1,0:T(8,128)(2,1)S(1)} %get-tuple-element.39), channel_id=1, source_target_pairs={{0,6},{2,0},{4,2},{6,4},{1,7},{3,1},{5,3},{7,5},{8,14},{10,8},{12,... | collective-permute-start | bytes 393224 | tf_op jit(solution)/shard_map/ppermute | solution.py:330
  68.0 7.2 %collective-permute-start.10 = (bf16[32,2048]{1,0:T(8,128)(2,1)S(1)}, bf16[32,2048]{1,0:T(8,128)(2,1)S(1)}, u32[]{:S(2)}, u32[]{:S(2)}) collective-permute-start(bf16[32,2048]{1,0:T(8,128)(2,1)S(1)} %get-tuple-element.40), channel_id=1, source_target_pairs={{0,4},{2,6},{4,0},{6,2},{1,5},{3,7},{5,1},{7,3},{8,12},{10,14},{12... | collective-permute-start | bytes 393224 | tf_op jit(solution)/shard_map/ppermute | solution.py:330
  75.8 5.8 %collective-permute-start.11 = (bf16[16,2048]{1,0:T(8,128)(2,1)S(1)}, bf16[16,2048]{1,0:T(8,128)(2,1)S(1)}, u32[]{:S(2)}, u32[]{:S(2)}) collective-permute-start(bf16[16,2048]{1,0:T(8,128)(2,1)S(1)} %get-tuple-element.42), channel_id=1, source_target_pairs={{0,1},{1,0},{2,3},{3,2},{4,5},{5,4},{6,7},{7,6},{8,9},{9,8},{10,11... | collective-permute-start | bytes 196616 | tf_op jit(solution)/shard_map/ppermute | solution.py:340

commit v5 on v0

--- a/solution.py
+++ b/solution.py
@@ -10,7 +10,6 @@
 step_size = 0.1
 SPACE = ("z", "xl", "c")
 SAMP = ("y", "xh")
-BLOCK = 2048
 bf16, f32 = jnp.bfloat16, jnp.float32
 
 
@@ -82,7 +81,7 @@
         halo_ref[...] = k_own[:, half:]
 
 
-def mid_body(rows, cols, c_ref, oth_ref, core_ref, k_ref, halo_ref, face_ref, u_ref, kt_ref, base_ref, m_ref, base_s, lap_s):
+def mid_body(rows, cols, c_ref, oth_ref, core_ref, k_ref, halo_ref, face_ref, u_ref, kt_ref, base_ref, m_ref, base_s, lap_s, w_s, k_s):
     half = oth_ref.shape[1] // 2
     k_oth = dot(core_ref[...].astype(bf16), oth_ref[...], 0, 0).astype(bf16)
     kt_ref[...] = k_oth.T
@@ -92,22 +91,28 @@
     before = jnp.where(first, halo, near)
     after = jnp.where(first, near, halo)
     plane = rows * cols
-    lane = lax.broadcasted_iota(jnp.int32, (1, cols), 1)
+    lane = lax.broadcasted_iota(jnp.int32, (1, 1, cols), 2)
+    faces = [0.25 * lax.shift_left(1, face_ref[f]).astype(f32) for f in range(6)]
+    w_s[6] = ((faces[0] + faces[1]) + (faces[2] + faces[3])) + (faces[4] + faces[5])
+    faces[4] = jnp.where(lane == 0, 0.0, faces[4])
+    faces[5] = jnp.where(lane == cols - 1, 0.0, faces[5])
+    for f in range(6):
+        w_s[f] = faces[f]
+    k_s[...] = k_ref[...].astype(f32)
     for x in range(2):
         for y in range(rows):
             at = (x * rows + y) * cols
-            mid = k_ref[:, at : at + cols].astype(f32)
-            w = [0.25 * lax.shift_left(1, face_ref[f, x, y : y + 1, :]).astype(f32) for f in range(6)]
-            total = ((w[0] + w[1]) + (w[2] + w[3])) + (w[4] + w[5])
-            down = before[:, y * cols : (y + 1) * cols] if x == 0 else k_ref[:, at - plane : at - plane + cols].astype(f32)
-            up = after[:, y * cols : (y + 1) * cols] if x == 1 else k_ref[:, at + plane : at + plane + cols].astype(f32)
-            out = w[0] * down + w[1] * up - total * mid
+            mid = k_s[:, at : at + cols]
+            w = [w_s[f, x, y : y + 1, :] for f in range(7)]
+            down = before[:, y * cols : (y + 1) * cols] if x == 0 else k_s[:, at - plane : at - plane + cols]
+            up = after[:, y * cols : (y + 1) * cols] if x == 1 else k_s[:, at + plane : at + plane + cols]
+            out = w[0] * down + w[1] * up - w[6] * mid
             if y > 0:
-                out += w[2] * k_ref[:, at - cols : at].astype(f32)
+                out += w[2] * k_s[:, at - cols : at]
             if y < rows - 1:
-                out += w[3] * k_ref[:, at + cols : at + 2 * cols].astype(f32)
-            out += jnp.where(lane == 0, 0.0, w[4]) * pltpu.roll(mid, 1, 1)
-            out += jnp.where(lane == cols - 1, 0.0, w[5]) * pltpu.roll(mid, cols - 1, 1)
+                out += w[3] * k_s[:, at + cols : at + 2 * cols]
+            out += w[4] * pltpu.roll(mid, 1, 1)
+            out += w[5] * pltpu.roll(mid, cols - 1, 1)
             base_s[:, at : at + cols] = mid + step_size * out
             lap_s[:, at : at + cols] = out.astype(bf16)
     base_ref[...] = base_s[pl.ds(pl.multiple_of(c_ref[1] * base_ref.shape[0], 8), base_ref.shape[0]), :]
@@ -115,7 +120,7 @@
 
 
 def sweep(kt_ref, u_ref, v_ref, g_ref, ov_ref, start, stop, store, tile=512):
-    block = min(BLOCK, stop - start)
+    block = stop - start
 
     def turn(i, _):
         at = pl.multiple_of(start + i * block, block)
@@ -142,19 +147,16 @@
     ov_s = refs[2] if back else ov_ref
     ov_s[...] = jnp.zeros_like(ov_s) if far_ref is None else far_ref[...]
 
+    done = 0 if old_ref is None else old_ref.shape[1]
+
     def store(here, acc):
-        l_ref[:, here] = acc if old_ref is None else old_ref[:, here] + acc
-
-    stop = start + l_ref.shape[1]
-    done = 0 if old_ref is None else old_ref.shape[1]
-    if done:
-        sweep(kt_ref, u_ref, v_ref, g_ref, ov_s, start, start + done, store)
-    if start + done < stop:
-
-        def rest(here, acc):
-            l_ref[:, pl.ds(pl.multiple_of(here.start + done, done or BLOCK), here.size)] = acc
-
-        sweep(kt_ref, u_ref, v_ref, g_ref, ov_s, start + done, stop, rest)
+        if done:
+            l_ref[:, :done] = old_ref[...] + acc[:, :done]
+            l_ref[:, done:] = acc[:, done:]
+        else:
+            l_ref[:, here] = acc
+
+    sweep(kt_ref, u_ref, v_ref, g_ref, ov_s, start, start + l_ref.shape[1], store)
     if back:
         ov_ref[...] = ov_s[...].T.astype(bf16)
 
@@ -263,7 +265,7 @@
         functools.partial(mid_body, rows_y, cols_z),
         [u_oth, core_s, k_own, halo, face_class, u_own],
         [((cells, rank), bf16, True), ((narrow, cells), f32, False), ((rank, rank), f32, True)],
-        [((rank, cells), f32), ((rank, cells), bf16)],
+        [((rank, cells), f32), ((rank, cells), bf16), ((7,) + face_class.shape[1:], f32), ((rank, cells), f32)],
         at=where_at,
         held=(ov_first, kt_own, l_first),
     )
@@ -295,7 +297,9 @@
     l_new = l_got.reshape(n_space // 2, 2, lanes, half).astype(f32).sum(0)
     l_new = jnp.transpose(l_new, (1, 0, 2)).reshape(lanes, samp_rows)
 
-    near = [resident(lax.ppermute(part, "y", ring(4, k))) for part, k in ((up, 1), (dn, 3), (away, 2))]
+    near = []
+    for part, k in ((up, 1), (dn, 3), (away, 2)):
+        near.append(resident(lax.ppermute(part, "y", ring(4, k))))
     mine, send = small(
         pair_body,
         [me, *near],

time: 96.3 us -> 96.2 us (level)
  no operation moved by 1% of the time
where the time goes in v5:
time: 96.2 us; the launch traced here: 95.7 us
  Pallas kernels  31.6 us (33%)
  starting transfers between devices  30.7 us (32%)
  waiting for transfers between devices  29.2 us (30%)
  local copies, waits for them, and re-layouts  1.79 us (2%)
  other arithmetic  1.64 us (2%)
    pallas_call x9, Pallas kernels, small(): pl.pallas_call(reading, in_specs=[pl.BlockSpec(memory_space=pltpu.SMEM)]...  31.6 us
    ppermute x1, waiting for transfers between devices, per_device(): u1 = lax.ppermute(u0, 'xh', swap)  14.4 us
    all_to_all x1, starting transfers between devices, per_device(): lax.all_to_all(v_wide.reshape(rank, half), SPACE, 0, 0, tiled=True)  6.59 us
    ppermute x3, waiting for transfers between devices, per_device(): near.append(resident(lax.ppermute(part, 'y', ring(4, k))))  5.88 us
    ppermute x3, starting transfers between devices, per_device(): around = [resident(lax.ppermute(pair, 'y', ring(4, k))) for k in (1, 3, 2)]  5.22 us
    ppermute x3, waiting for transfers between devices, per_device(): around = [resident(lax.ppermute(pair, 'y', ring(4, k))) for k in (1, 3, 2)]  5.13 us
    all_to_all x1, starting transfers between devices, per_device(): l_got = lax.all_to_all(l_part, SPACE, 0, 0, tiled=True)  4.75 us
    ppermute x3, starting transfers between devices, per_device(): near.append(resident(lax.ppermute(part, 'y', ring(4, k))))  4.11 us
  transfers between devices with their start and end apart: 14, of which 8 were waited for; matrix products, arithmetic and copies ran while one was open for 1% of the time, Pallas kernels for 12%

profile of v5, /device:TPU:0, one launch (start us, length us, event | category | flops | bytes accessed | tf_op | source)
XLA Modules:
  0.0 95.7 jit_solution(15546827520066578948)
XLA Ops:
  0.6 0.9 copy-done.2
  2.4 1.2 %shard_map.68 = (bf16[16,2048]{1,0:T(8,128)(2,1)S(1)}, bf16[8,2,8,4096]{3,2,1,0:T(8,128)(2,1)}) custom-call(bf16[16,2,8,128]{3,2,1,0:T(8,128)(2,1)S(1)} %copy-done.3, bf16[8,8192]{1,0:T(8,128)(2,1)S(1)} %copy-done.2), custom_call_target="tpu_custom_call" | custom-call | tf_op jit(solution)/shard_map/pallas_call | solution.py:32
  3.6 6.6 %all-to-all-start = ((bf16[16,8,4096]{2,1,0:T(8,128)(2,1)}), bf16[16,8,4096]{2,1,0:T(8,128)(2,1)S(1)}, u32[]{:S(2)}, u32[]{:S(2)}) async-start(bf16[16,8,4096]{2,1,0:T(8,128)(2,1)} %bitcast.22), calls=%async_computation | async-start | bytes 2097152 | tf_op jit(solution)/shard_map/all_to_all | solution.py:241
  10.2 2.8 %collective-permute-start = (bf16[16,2048]{1,0:T(8,128)(2,1)S(1)}, bf16[16,2048]{1,0:T(8,128)(2,1)S(1)}, u32[]{:S(2)}, u32[]{:S(2)}) collective-permute-start(bf16[16,2048]{1,0:T(8,128)(2,1)S(1)} %get-tuple-element.24.refs_1_), channel_id=1, source_target_pairs={{0,1},{1,0},{2,3},{3,2},{4,5},{5,4},{6,7},{7,6},{8,9},{9,8},{10,11... | collective-permute-start | bytes 196616 | tf_op jit(solution)/shard_map/ppermute | solution.py:242
  13.0 14.4 %collective-permute-done.refs_2_ = bf16[16,2048]{1,0:T(8,128)(2,1)S(1)} collective-permute-done((bf16[16,2048]{1,0:T(8,128)(2,1)S(1)}, bf16[16,2048]{1,0:T(8,128)(2,1)S(1)}, u32[]{:S(2)}, u32[]{:S(2)}) %collective-permute-start) | collective-permute-done | bytes 65568 | tf_op jit(solution)/shard_map/ppermute | solution.py:242
  27.4 3.2 %collective-permute-start.3 = (bf16[32,2048]{1,0:T(8,128)(2,1)S(1)}, bf16[32,2048]{1,0:T(8,128)(2,1)S(1)}, u32[]{:S(2)}, u32[]{:S(2)}) collective-permute-start(bf16[32,2048]{1,0:T(8,128)(2,1)S(1)} %constant_dynamic-update-slice_fusion), channel_id=1, source_target_pairs={{0,4},{2,6},{4,0},{6,2},{1,5},{3,7},{5,1},{7,3},{8,12},{10,14},{12... | collective-permute-start | bytes 393224 | tf_op jit(solution)/shard_map/ppermute | solution.py:244
  30.6 1.1 %collective-permute-start.2 = (bf16[32,2048]{1,0:T(8,128)(2,1)S(1)}, bf16[32,2048]{1,0:T(8,128)(2,1)S(1)}, u32[]{:S(2)}, u32[]{:S(2)}) collective-permute-start(bf16[32,2048]{1,0:T(8,128)(2,1)S(1)} %constant_dynamic-update-slice_fusion), channel_id=1, source_target_pairs={{0,6},{2,0},{4,2},{6,4},{1,7},{3,1},{5,3},{7,5},{8,14},{10,8},{12,... | collective-permute-start | bytes 393224 | tf_op jit(solution)/shard_map/ppermute | solution.py:244
  31.6 1.0 %collective-permute-start.1 = (bf16[32,2048]{1,0:T(8,128)(2,1)S(1)}, bf16[32,2048]{1,0:T(8,128)(2,1)S(1)}, u32[]{:S(2)}, u32[]{:S(2)}) collective-permute-start(bf16[32,2048]{1,0:T(8,128)(2,1)S(1)} %constant_dynamic-update-slice_fusion), channel_id=1, source_target_pairs={{0,2},{2,4},{4,6},{6,0},{1,3},{3,5},{5,7},{7,1},{8,10},{10,12},{12... | collective-permute-start | bytes 393224 | tf_op jit(solution)/shard_map/ppermute | solution.py:244
  32.7 2.2 %collective-permute-done.3.refs_5_ = bf16[32,2048]{1,0:T(8,128)(2,1)S(1)} collective-permute-done((bf16[32,2048]{1,0:T(8,128)(2,1)S(1)}, bf16[32,2048]{1,0:T(8,128)(2,1)S(1)}, u32[]{:S(2)}, u32[]{:S(2)}) %collective-permute-start.3) | collective-permute-done | bytes 131104 | tf_op jit(solution)/shard_map/ppermute | solution.py:244
  34.9 2.5 %collective-permute-done.2.refs_4_ = bf16[32,2048]{1,0:T(8,128)(2,1)S(1)} collective-permute-done((bf16[32,2048]{1,0:T(8,128)(2,1)S(1)}, bf16[32,2048]{1,0:T(8,128)(2,1)S(1)}, u32[]{:S(2)}, u32[]{:S(2)}) %collective-permute-start.2) | collective-permute-done | bytes 131104 | tf_op jit(solution)/shard_map/ppermute | solution.py:244
  37.8 1.7 %shard_map.69 = (bf16[128,2048]{1,0:T(8,128)(2,1)S(1)}, bf16[128,2048]{1,0:T(8,128)(2,1)S(1)}, bf16[2048,128]{1,0:T(8,128)(2,1)S(1)}, bf16[128,1024]{1,0:T(8,128)(2,1)}) custom-call(s32[4]{0:T(128)S(1)} %pad_add_fusion.refs_0_, bf16[16,2048]{1,0:T(8,128)(2,1)S(1)} %get-tuple-element.24.refs_1_, bf16[16,2048]{1,0:T(8,128)(2,1)S(1)} %collective-permute-done.refs_2_, ...), custom_call_target="tpu_custom_call" | custom-call | tf_op jit(solution)/shard_map/pallas_call | solution.py:32
  41.1 5.6 %shard_map.70 = (f32[128,2048]{1,0:T(8,128)S(1)}, f32[2048,128]{1,0:T(8,128)S(1)}) custom-call(bf16[2048,128]{1,0:T(8,128)(2,1)S(1)} %get-tuple-element.28.refs_0_.refs_8_.refs_6_.refs_1_, bf16[128,2048]{1,0:T(8,128)(2,1)S(1)} %get-tuple-element.25.refs_1_.refs_6_.refs_7_.refs_2_, bf16[128,4096]{1,0:T(8,128)(2,1)S(1)} %bitcast.13, f32[1,4096]{1,0:T(1,128)S(1)} %bitcast.17), custom_call_target="tpu_custom_call" | custom-call | tf_op jit(solution)/shard_map/pallas_call | solution.py:32
  46.7 2.4 %shard_map.71 = (bf16[2048,128]{1,0:T(8,128)(2,1)S(1)}, f32[16,2048]{1,0:T(8,128)}, f32[128,128]{1,0:T(8,128)S(1)}) custom-call(s32[4]{0:T(128)S(1)} %pad_add_fusion.refs_0_, bf16[128,2048]{1,0:T(8,128)(2,1)S(1)} %collective-permute-done.4.refs_1_, f32[128,128]{1,0:T(8,128)S(1)} %copy-done, bf16[128,2048]{1,0:T(8,128)(2,1)S(1)} %get-tuple-element.26.refs_3_, ...), custom_call_target="tpu_custom_call" | custom-call | tf_op jit(solution)/shard_map/pallas_call | solution.py:32
  49.1 11.5 %shard_map.72 = (f32[128,4096]{1,0:T(8,128)S(1)}, bf16[128,2048]{1,0:T(8,128)(2,1)S(1)}) custom-call(bf16[2048,128]{1,0:T(8,128)(2,1)S(1)} %get-tuple-element.33.refs_0_, bf16[128,2048]{1,0:T(8,128)(2,1)S(1)} %collective-permute-done.4.refs_1_, bf16[128,4096]{1,0:T(8,128)(2,1)S(1)} %bitcast.14, f32[1,4096]{1,0:T(1,128)S(1)} %bitcast.18, ...), custom_call_target="tpu_custom_call" | custom-call | tf_op jit(solution)/shard_map/pallas_call | solution.py:32
  60.6 4.0 %collective-permute-start.6 = (bf16[128,2048]{1,0:T(8,128)(2,1)S(1)}, bf16[128,2048]{1,0:T(8,128)(2,1)S(1)}, u32[]{:S(2)}, u32[]{:S(2)}) collective-permute-start(bf16[128,2048]{1,0:T(8,128)(2,1)S(1)} %get-tuple-element.35.refs_6_), channel_id=1, source_target_pairs={{0,8},{8,0},{1,9},{9,1},{2,10},{10,2},{3,11},{11,3},{4,12},{12,4},... | collective-permute-start | bytes 1572872 | tf_op jit(solution)/shard_map/ppermute | solution.py:280
  64.9 2.9 %shard_map.73 = (f32[128,1024]{1,0:T(8,128)S(1)}, f32[2048,128]{1,0:T(8,128)S(1)}) custom-call(bf16[2048,128]{1,0:T(8,128)(2,1)S(1)} %get-tuple-element.28.refs_0_.refs_8_.refs_6_.refs_1_, bf16[128,2048]{1,0:T(8,128)(2,1)S(1)} %get-tuple-element.25.refs_1_.refs_6_.refs_7_.refs_2_, bf16[128,4096]{1,0:T(8,128)(2,1)S(1)} %bitcast.15, f32[1,4096]{1,0:T(1,128)S(1)} %bitcast.19, ...), custom_call_target="tpu_custom_call" | custom-call | tf_op jit(solution)/shard_map/pallas_call | solution.py:32
  67.8 5.1 %shard_map.74 = (bf16[128,4096]{1,0:T(8,128)(2,1)}, f32[32,2048]{1,0:T(8,128)S(1)}, bf16[32,2048]{1,0:T(8,128)(2,1)S(1)}, bf16[32,2048]{1,0:T(8,128)(2,1)S(1)}, bf16[32,2048]{1,0:T(8,128)(2,1)S(1)}) custom-call(s32[4]{0:T(128)S(1)} %pad_add_fusion.refs_0_, bf16[2048,128]{1,0:T(8,128)(2,1)S(1)} %get-tuple-element.28.refs_0_.refs_8_.refs_6_.refs_1_, ...), custom_call_target="tpu_custom_call" | custom-call | tf_op jit(solution)/shard_map/pallas_call | solution.py:32
  72.9 4.8 %all-to-all-start.1 = ((bf16[16,8,4096]{2,1,0:T(8,128)(2,1)}), bf16[16,8,4096]{2,1,0:T(8,128)(2,1)S(1)}, u32[]{:S(2)}, u32[]{:S(2)}) async-start(bf16[16,8,4096]{2,1,0:T(8,128)(2,1)} %bitcast.23), calls=%async_computation.1 | async-start | bytes 2097152 | tf_op jit(solution)/shard_map/all_to_all | solution.py:296
  78.3 2.7 %collective-permute-start.9 = (bf16[32,2048]{1,0:T(8,128)(2,1)S(1)}, bf16[32,2048]{1,0:T(8,128)(2,1)S(1)}, u32[]{:S(2)}, u32[]{:S(2)}) collective-permute-start(bf16[32,2048]{1,0:T(8,128)(2,1)S(1)} %get-tuple-element.41), channel_id=1, source_target_pairs={{0,6},{2,0},{4,2},{6,4},{1,7},{3,1},{5,3},{7,5},{8,14},{10,8},{12,... | collective-permute-start | bytes 393224 | tf_op jit(solution)/shard_map/ppermute | solution.py:302
  81.8 2.9 %collective-permute-done.8.refs_2_ = bf16[32,2048]{1,0:T(8,128)(2,1)S(1)} collective-permute-done((bf16[32,2048]{1,0:T(8,128)(2,1)S(1)}, bf16[32,2048]{1,0:T(8,128)(2,1)S(1)}, u32[]{:S(2)}, u32[]{:S(2)}) %collective-permute-start.8) | collective-permute-done | bytes 131104 | tf_op jit(solution)/shard_map/ppermute | solution.py:302
  84.7 2.1 %collective-permute-done.9.refs_3_ = bf16[32,2048]{1,0:T(8,128)(2,1)S(1)} collective-permute-done((bf16[32,2048]{1,0:T(8,128)(2,1)S(1)}, bf16[32,2048]{1,0:T(8,128)(2,1)S(1)}, u32[]{:S(2)}, u32[]{:S(2)}) %collective-permute-start.9) | collective-permute-done | bytes 131104 | tf_op jit(solution)/shard_map/ppermute | solution.py:302
  86.8 0.9 collective-permute-done.10.refs_4_
  88.3 2.0 %collective-permute-start.11 = (bf16[16,2048]{1,0:T(8,128)(2,1)S(1)}, bf16[16,2048]{1,0:T(8,128)(2,1)S(1)}, u32[]{:S(2)}, u32[]{:S(2)}) collective-permute-start(bf16[16,2048]{1,0:T(8,128)(2,1)S(1)} %get-tuple-element.44), channel_id=1, source_target_pairs={{0,1},{1,0},{2,3},{3,2},{4,5},{5,4},{6,7},{7,6},{8,9},{9,8},{10,11... | collective-permute-start | bytes 196616 | tf_op jit(solution)/shard_map/ppermute | solution.py:312
  90.3 3.8 %collective-permute-done.11.refs_2_ = bf16[16,2048]{1,0:T(8,128)(2,1)S(1)} collective-permute-done((bf16[16,2048]{1,0:T(8,128)(2,1)S(1)}, bf16[16,2048]{1,0:T(8,128)(2,1)S(1)}, u32[]{:S(2)}, u32[]{:S(2)}) %collective-permute-start.11) | collective-permute-done | bytes 65568 | tf_op jit(solution)/shard_map/ppermute | solution.py:312
  (28 shorter events, 7.0 us)
Async XLA Ops:
  0.6 37.2 %copy-start = (f32[128,128]{1,0:T(8,128)S(1)}, f32[128,128]{1,0:T(8,128)}, u32[]{:S(2)}) copy-start(f32[128,128]{1,0:T(8,128)} %refs_11_.1) | copy-start | bytes 196612
  0.6 0.9 copy-start.2
  1.6 0.8 copy-start.3
  3.6 43.1 %copy-start.4 = (s32[6,2,8,128]{3,2,1,0:T(8,128)S(1)}, s32[6,2,8,128]{3,2,1,0:T(8,128)}, u32[]{:S(2)}) copy-start(s32[6,2,8,128]{3,2,1,0:T(8,128)} %refs_5_.1) | copy-start | bytes 147460
  3.6 37.5 %all-to-all-start = ((bf16[16,8,4096]{2,1,0:T(8,128)(2,1)}), bf16[16,8,4096]{2,1,0:T(8,128)(2,1)S(1)}, u32[]{:S(2)}, u32[]{:S(2)}) async-start(bf16[16,8,4096]{2,1,0:T(8,128)(2,1)} %bitcast.22), calls=%async_computation | async-start | bytes 2097152 | tf_op jit(solution)/shard_map/all_to_all | solution.py:241
  10.2 17.2 %collective-permute-start = (bf16[16,2048]{1,0:T(8,128)(2,1)S(1)}, bf16[16,2048]{1,0:T(8,128)(2,1)S(1)}, u32[]{:S(2)}, u32[]{:S(2)}) collective-permute-start(bf16[16,2048]{1,0:T(8,128)(2,1)S(1)} %get-tuple-element.24.refs_1_), channel_id=1, source_target_pairs={{0,1},{1,0},{2,3},{3,2},{4,5},{5,4},{6,7},{7,6},{8,9},{9,8},{10,11... | collective-permute-start | bytes 196616 | tf_op jit(solution)/shard_map/ppermute | solution.py:242
  27.4 7.5 %collective-permute-start.3 = (bf16[32,2048]{1,0:T(8,128)(2,1)S(1)}, bf16[32,2048]{1,0:T(8,128)(2,1)S(1)}, u32[]{:S(2)}, u32[]{:S(2)}) collective-permute-start(bf16[32,2048]{1,0:T(8,128)(2,1)S(1)} %constant_dynamic-update-slice_fusion), channel_id=1, source_target_pairs={{0,4},{2,6},{4,0},{6,2},{1,5},{3,7},{5,1},{7,3},{8,12},{10,14},{12... | collective-permute-start | bytes 393224 | tf_op jit(solution)/shard_map/ppermute | solution.py:244
  30.6 6.8 %collective-permute-start.2 = (bf16[32,2048]{1,0:T(8,128)(2,1)S(1)}, bf16[32,2048]{1,0:T(8,128)(2,1)S(1)}, u32[]{:S(2)}, u32[]{:S(2)}) collective-permute-start(bf16[32,2048]{1,0:T(8,128)(2,1)S(1)} %constant_dynamic-update-slice_fusion), channel_id=1, source_target_pairs={{0,6},{2,0},{4,2},{6,4},{1,7},{3,1},{5,3},{7,5},{8,14},{10,8},{12,... | collective-permute-start | bytes 393224 | tf_op jit(solution)/shard_map/ppermute | solution.py:244
  31.6 6.2 %collective-permute-start.1 = (bf16[32,2048]{1,0:T(8,128)(2,1)S(1)}, bf16[32,2048]{1,0:T(8,128)(2,1)S(1)}, u32[]{:S(2)}, u32[]{:S(2)}) collective-permute-start(bf16[32,2048]{1,0:T(8,128)(2,1)S(1)} %constant_dynamic-update-slice_fusion), channel_id=1, source_target_pairs={{0,2},{2,4},{4,6},{6,0},{1,3},{3,5},{5,7},{7,1},{8,10},{10,12},{12... | collective-permute-start | bytes 393224 | tf_op jit(solution)/shard_map/ppermute | solution.py:244
  39.5 7.2 %collective-permute-start.4 = (bf16[128,2048]{1,0:T(8,128)(2,1)S(1)}, bf16[128,2048]{1,0:T(8,128)(2,1)S(1)}, u32[]{:S(2)}, u32[]{:S(2)}) collective-permute-start(bf16[128,2048]{1,0:T(8,128)(2,1)S(1)} %get-tuple-element.25.refs_1_.refs_6_.refs_7_.refs_2_), channel_id=1, source_target_pairs={{0,8},{8,0},{1,9},{9,1},{2,10},{10,2},{3,11},{11,3},{4,12},{12,4},... | collective-permute-start | bytes 1572872 | tf_op jit(solution)/shard_map/ppermute | solution.py:251
  39.5 7.2 %collective-permute-start.5 = (bf16[128,1024]{1,0:T(8,128)(2,1)}, bf16[128,1024]{1,0:T(8,128)(2,1)S(1)}, u32[]{:S(2)}, u32[]{:S(2)}) collective-permute-start(bf16[128,1024]{1,0:T(8,128)(2,1)} %get-tuple-element.27), channel_id=1, source_target_pairs={{8,16},{24,32},{40,48},{56,64},{72,80},{88,96},{104,112},{16,8},{3... | collective-permute-start | bytes 786440 | tf_op jit(solution)/shard_map/ppermute | solution.py:254
  60.6 7.2 %collective-permute-start.6 = (bf16[128,2048]{1,0:T(8,128)(2,1)S(1)}, bf16[128,2048]{1,0:T(8,128)(2,1)S(1)}, u32[]{:S(2)}, u32[]{:S(2)}) collective-permute-start(bf16[128,2048]{1,0:T(8,128)(2,1)S(1)} %get-tuple-element.35.refs_6_), channel_id=1, source_target_pairs={{0,8},{8,0},{1,9},{9,1},{2,10},{10,2},{3,11},{11,3},{4,12},{12,4},... | collective-permute-start | bytes 1572872 | tf_op jit(solution)/shard_map/ppermute | solution.py:280
  64.5 3.3 %collective-permute-start.7 = (f32[128,128]{1,0:T(8,128)S(1)}, f32[128,128]{1,0:T(8,128)S(1)}, u32[]{:S(2)}, u32[]{:S(2)}) collective-permute-start(f32[128,128]{1,0:T(8,128)S(1)} %get-tuple-element.38.refs_9_), channel_id=1, source_target_pairs={{0,8},{8,0},{1,9},{9,1},{2,10},{10,2},{3,11},{11,3},{4,12},{12,4},... | collective-permute-start | bytes 196616 | tf_op jit(solution)/shard_map/ppermute | solution.py:272
  72.9 21.2 %copy-start.1 = (f32[16,2048]{1,0:T(8,128)S(1)}, f32[16,2048]{1,0:T(8,128)}, u32[]{:S(2)}) copy-start(f32[16,2048]{1,0:T(8,128)} %get-tuple-element.32.refs_0_) | copy-start | bytes 393220
  72.9 22.0 %all-to-all-start.1 = ((bf16[16,8,4096]{2,1,0:T(8,128)(2,1)}), bf16[16,8,4096]{2,1,0:T(8,128)(2,1)S(1)}, u32[]{:S(2)}, u32[]{:S(2)}) async-start(bf16[16,8,4096]{2,1,0:T(8,128)(2,1)} %bitcast.23), calls=%async_computation.1 | async-start | bytes 2097152 | tf_op jit(solution)/shard_map/all_to_all | solution.py:296
  77.6 7.0 %collective-permute-start.8 = (bf16[32,2048]{1,0:T(8,128)(2,1)S(1)}, bf16[32,2048]{1,0:T(8,128)(2,1)S(1)}, u32[]{:S(2)}, u32[]{:S(2)}) collective-permute-start(bf16[32,2048]{1,0:T(8,128)(2,1)S(1)} %get-tuple-element.40), channel_id=1, source_target_pairs={{0,2},{2,4},{4,6},{6,0},{1,3},{3,5},{5,7},{7,1},{8,10},{10,12},{12... | collective-permute-start | bytes 393224 | tf_op jit(solution)/shard_map/ppermute | solution.py:302
  78.3 8.5 %collective-permute-start.9 = (bf16[32,2048]{1,0:T(8,128)(2,1)S(1)}, bf16[32,2048]{1,0:T(8,128)(2,1)S(1)}, u32[]{:S(2)}, u32[]{:S(2)}) collective-permute-start(bf16[32,2048]{1,0:T(8,128)(2,1)S(1)} %get-tuple-element.41), channel_id=1, source_target_pairs={{0,6},{2,0},{4,2},{6,4},{1,7},{3,1},{5,3},{7,5},{8,14},{10,8},{12,... | collective-permute-start | bytes 393224 | tf_op jit(solution)/shard_map/ppermute | solution.py:302
  81.0 6.7 %collective-permute-start.10 = (bf16[32,2048]{1,0:T(8,128)(2,1)S(1)}, bf16[32,2048]{1,0:T(8,128)(2,1)S(1)}, u32[]{:S(2)}, u32[]{:S(2)}) collective-permute-start(bf16[32,2048]{1,0:T(8,128)(2,1)S(1)} %get-tuple-element.42), channel_id=1, source_target_pairs={{0,4},{2,6},{4,0},{6,2},{1,5},{3,7},{5,1},{7,3},{8,12},{10,14},{12... | collective-permute-start | bytes 393224 | tf_op jit(solution)/shard_map/ppermute | solution.py:302
  88.3 5.8 %collective-permute-start.11 = (bf16[16,2048]{1,0:T(8,128)(2,1)S(1)}, bf16[16,2048]{1,0:T(8,128)(2,1)S(1)}, u32[]{:S(2)}, u32[]{:S(2)}) collective-permute-start(bf16[16,2048]{1,0:T(8,128)(2,1)S(1)} %get-tuple-element.44), channel_id=1, source_target_pairs={{0,1},{1,0},{2,3},{3,2},{4,5},{5,4},{6,7},{7,6},{8,9},{9,8},{10,11... | collective-permute-start | bytes 196616 | tf_op jit(solution)/shard_map/ppermute | solution.py:312

commit v6 on v5

--- a/solution.py
+++ b/solution.py
@@ -40,21 +40,25 @@
     )(*scalars, *args, *held)
 
 
-def head_body(u_ref, v_ref, flat_ref, out_ref, u_s):
-    _, depth, rows, cols = u_ref.shape
-    u_s[...] = u_ref[...].astype(f32)
-    for x in range(depth):
-        for y in range(rows):
-            at = (x * rows + y) * cols
-            flat_ref[:, at : at + cols] = u_s[:, x, y, :].astype(bf16)
+def fan_body(v_ref, out_ref):
     half = out_ref.shape[-1]
     for k in range(out_ref.shape[0]):
         out_ref[k, 0] = v_ref[:, :half]
         out_ref[k, 1] = v_ref[:, half:]
 
 
-def prep_body(at_ref, u_ref, w_ref, a_ref, b_ref, c_ref, core_ref, full_ref, k_ref, kt_ref, halo_ref):
-    narrow, cells = u_ref.shape
+def flat_body(own_ref, got_ref, out_ref, u_s):
+    narrow, depth, rows, cols = own_ref.shape
+    for i, ref in enumerate((own_ref, got_ref)):
+        u_s[...] = ref[...].astype(f32)
+        for x in range(depth):
+            for y in range(rows):
+                at = (x * rows + y) * cols
+                out_ref[i * narrow : (i + 1) * narrow, at : at + cols] = u_s[:, x, y, :].astype(bf16)
+
+
+def prep_body(at_ref, u_ref, a_ref, b_ref, c_ref, core_ref, full_ref, k_ref, kt_ref, halo_ref):
+    narrow, cells = u_ref.shape[0] // 2, u_ref.shape[1]
     half = cells // 2
     y, xh = at_ref[2], at_ref[3]
 
@@ -62,9 +66,7 @@
         row = (((y + turn) % 4) * 2 + (xh if flip == 0 else 1 - xh)) * narrow
         full_ref[pl.ds(pl.multiple_of(row, narrow), narrow), :] = value
 
-    put(0, 0, u_ref[...])
-    put(0, 1, w_ref[...])
-    for turn, ref in ((3, a_ref), (1, b_ref), (2, c_ref)):
+    for turn, ref in ((0, u_ref), (3, a_ref), (1, b_ref), (2, c_ref)):
         put(turn, 0, ref[:narrow, :])
         put(turn, 1, ref[narrow:, :])
     k_own = dot(core_ref[...].astype(bf16), full_ref[...], 0, 0).astype(bf16)
@@ -232,19 +234,14 @@
     where_at = jnp.stack([core_at, lax.axis_index(SAMP), lax.axis_index("y"), lax.axis_index("xh")]).astype(jnp.int32)
     swap = ring(2, 1)
 
-    u0, v_wide = small(
-        head_body,
-        [basis_u, basis_v],
-        [((narrow, cells), bf16, True), ((n_space // 2, 2, lanes, half), bf16, False)],
-        [(basis_u.shape, f32)],
-    )
+    (v_wide,) = small(fan_body, [basis_v], [((n_space // 2, 2, lanes, half), bf16, False)])
     v = resident(lax.all_to_all(v_wide.reshape(rank, half), SPACE, 0, 0, tiled=True))
-    u1 = lax.ppermute(u0, "xh", swap)
-    pair = jnp.concatenate([u0, u1], 0)
+    u1 = resident(lax.ppermute(basis_u, "xh", swap))
+    (pair,) = small(flat_body, [basis_u, u1], [((2 * narrow, cells), bf16, True)], [(basis_u.shape, f32)])
     around = [resident(lax.ppermute(pair, "y", ring(4, k))) for k in (1, 3, 2)]
     u_own, k_own, kt_own, edge = small(
         prep_body,
-        [u0, resident(u1), *around, core_s],
+        [pair, *around, core_s],
         [((rank, cells), bf16, True), ((rank, cells), bf16, True), ((cells, rank), bf16, True), ((rank, cells // 2), bf16, True)],
         at=where_at,
     )

time: 96.2 us -> 95.8 us (level)
    pallas_call x9 -> x10, Pallas kernels: 31.6 us -> 31.8 us  [small(): pl.pallas_call(reading, in_specs=[pl.BlockSpec(memory_space=pltpu.SMEM)]...]
where the time goes in v6:
time: 95.8 us; the launch traced here: 95.1 us
  Pallas kernels  31.8 us (33%)
  starting transfers between devices  30.8 us (32%)
  waiting for transfers between devices  29.2 us (30%)
  other arithmetic  1.64 us (2%)
    pallas_call x10, Pallas kernels, small(): pl.pallas_call(reading, in_specs=[pl.BlockSpec(memory_space=pltpu.SMEM)]...  31.8 us
    ppermute x1, waiting for transfers between devices, per_device(): u1 = resident(lax.ppermute(basis_u, 'xh', swap))  14.4 us
    all_to_all x1, starting transfers between devices, per_device(): lax.all_to_all(v_wide.reshape(rank, half), SPACE, 0, 0, tiled=True)  6.59 us
    ppermute x3, waiting for transfers between devices, per_device(): near.append(resident(lax.ppermute(part, 'y', ring(4, k))))  5.87 us
    ppermute x3, starting transfers between devices, per_device(): around = [resident(lax.ppermute(pair, 'y', ring(4, k))) for k in (1, 3, 2)]  5.3 us
    ppermute x3, waiting for transfers between devices, per_device(): around = [resident(lax.ppermute(pair, 'y', ring(4, k))) for k in (1, 3, 2)]  5.13 us
    all_to_all x1, starting transfers between devices, per_device(): l_got = lax.all_to_all(l_part, SPACE, 0, 0, tiled=True)  4.74 us
    ppermute x3, starting transfers between devices, per_device(): near.append(resident(lax.ppermute(part, 'y', ring(4, k))))  4.12 us
  transfers between devices with their start and end apart: 14, of which 8 were waited for; matrix products, arithmetic and copies ran while one was open for 1% of the time, Pallas kernels for 12%

profile of v6, /device:TPU:0, one launch (start us, length us, event | category | flops | bytes accessed | tf_op | source)
XLA Modules:
  0.0 95.1 jit_solution(18433437211969402028)
XLA Ops:
  0.6 0.9 copy-done.1
  1.6 1.1 %shard_map.70 = bf16[8,2,8,4096]{3,2,1,0:T(8,128)(2,1)} custom-call(bf16[8,8192]{1,0:T(8,128)(2,1)S(1)} %copy-done.1), custom_call_target="tpu_custom_call" | custom-call | tf_op jit(solution)/shard_map/pallas_call | solution.py:32
  2.7 6.6 %all-to-all-start = ((bf16[16,8,4096]{2,1,0:T(8,128)(2,1)}), bf16[16,8,4096]{2,1,0:T(8,128)(2,1)S(1)}, u32[]{:S(2)}, u32[]{:S(2)}) async-start(bf16[16,8,4096]{2,1,0:T(8,128)(2,1)} %bitcast.22), calls=%async_computation | async-start | bytes 2097152 | tf_op jit(solution)/shard_map/all_to_all | solution.py:238
  9.3 2.8 %collective-permute-start = (bf16[16,2,8,128]{3,2,1,0:T(8,128)(2,1)S(1)}, bf16[16,2,8,128]{3,2,1,0:T(8,128)(2,1)S(1)}, u32[]{:S(2)}, u32[]{:S(2)}) collective-permute-start(bf16[16,2,8,128]{3,2,1,0:T(8,128)(2,1)S(1)} %copy-done.3), channel_id=1, source_target_pairs={{0,1},{1,0},{2,3},{3,2},{4,5},{5,4},{6,7},{7,6},{8,9},{9,8},{10,11... | collective-permute-start | bytes 196616 | tf_op jit(solution)/shard_map/ppermute | solution.py:239
  12.1 14.4 %collective-permute-done.refs_1_ = bf16[16,2,8,128]{3,2,1,0:T(8,128)(2,1)S(1)} collective-permute-done((bf16[16,2,8,128]{3,2,1,0:T(8,128)(2,1)S(1)}, bf16[16,2,8,128]{3,2,1,0:T(8,128)(2,1)S(1)}, u32[]{:S(2)}, u32[]{:S(2)}) %collective-permute-start) | collective-permute-done | bytes 65568 | tf_op jit(solution)/shard_map/ppermute | solution.py:239
  26.7 3.3 %collective-permute-start.3 = (bf16[32,2048]{1,0:T(8,128)(2,1)S(1)}, bf16[32,2048]{1,0:T(8,128)(2,1)S(1)}, u32[]{:S(2)}, u32[]{:S(2)}) collective-permute-start(bf16[32,2048]{1,0:T(8,128)(2,1)S(1)} %shard_map.68.refs_1_), channel_id=1, source_target_pairs={{0,4},{2,6},{4,0},{6,2},{1,5},{3,7},{5,1},{7,3},{8,12},{10,14},{12... | collective-permute-start | bytes 393224 | tf_op jit(solution)/shard_map/ppermute | solution.py:241
  30.0 1.1 %collective-permute-start.2 = (bf16[32,2048]{1,0:T(8,128)(2,1)S(1)}, bf16[32,2048]{1,0:T(8,128)(2,1)S(1)}, u32[]{:S(2)}, u32[]{:S(2)}) collective-permute-start(bf16[32,2048]{1,0:T(8,128)(2,1)S(1)} %shard_map.68.refs_1_), channel_id=1, source_target_pairs={{0,6},{2,0},{4,2},{6,4},{1,7},{3,1},{5,3},{7,5},{8,14},{10,8},{12,... | collective-permute-start | bytes 393224 | tf_op jit(solution)/shard_map/ppermute | solution.py:241
  31.1 1.0 %collective-permute-start.1 = (bf16[32,2048]{1,0:T(8,128)(2,1)S(1)}, bf16[32,2048]{1,0:T(8,128)(2,1)S(1)}, u32[]{:S(2)}, u32[]{:S(2)}) collective-permute-start(bf16[32,2048]{1,0:T(8,128)(2,1)S(1)} %shard_map.68.refs_1_), channel_id=1, source_target_pairs={{0,2},{2,4},{4,6},{6,0},{1,3},{3,5},{5,7},{7,1},{8,10},{10,12},{12... | collective-permute-start | bytes 393224 | tf_op jit(solution)/shard_map/ppermute | solution.py:241
  32.1 2.2 %collective-permute-done.3.refs_4_ = bf16[32,2048]{1,0:T(8,128)(2,1)S(1)} collective-permute-done((bf16[32,2048]{1,0:T(8,128)(2,1)S(1)}, bf16[32,2048]{1,0:T(8,128)(2,1)S(1)}, u32[]{:S(2)}, u32[]{:S(2)}) %collective-permute-start.3) | collective-permute-done | bytes 131104 | tf_op jit(solution)/shard_map/ppermute | solution.py:241
  34.3 2.5 %collective-permute-done.2.refs_3_ = bf16[32,2048]{1,0:T(8,128)(2,1)S(1)} collective-permute-done((bf16[32,2048]{1,0:T(8,128)(2,1)S(1)}, bf16[32,2048]{1,0:T(8,128)(2,1)S(1)}, u32[]{:S(2)}, u32[]{:S(2)}) %collective-permute-start.2) | collective-permute-done | bytes 131104 | tf_op jit(solution)/shard_map/ppermute | solution.py:241
  37.2 1.7 %shard_map.69 = (bf16[128,2048]{1,0:T(8,128)(2,1)S(1)}, bf16[128,2048]{1,0:T(8,128)(2,1)S(1)}, bf16[2048,128]{1,0:T(8,128)(2,1)S(1)}, bf16[128,1024]{1,0:T(8,128)(2,1)}) custom-call(s32[4]{0:T(128)S(1)} %pad_add_fusion.refs_0_, bf16[32,2048]{1,0:T(8,128)(2,1)S(1)} %shard_map.68.refs_1_, bf16[32,2048]{1,0:T(8,128)(2,1)S(1)} %collective-permute-done.1.refs_2_, ...), custom_call_target="tpu_custom_call" | custom-call | tf_op jit(solution)/shard_map/pallas_call | solution.py:32
  40.5 5.6 %shard_map.71 = (f32[128,2048]{1,0:T(8,128)S(1)}, f32[2048,128]{1,0:T(8,128)S(1)}) custom-call(bf16[2048,128]{1,0:T(8,128)(2,1)S(1)} %get-tuple-element.25.refs_0_.refs_8_.refs_6_.refs_1_, bf16[128,2048]{1,0:T(8,128)(2,1)S(1)} %get-tuple-element.22.refs_1_.refs_6_.refs_7_.refs_2_, bf16[128,4096]{1,0:T(8,128)(2,1)S(1)} %bitcast.13, f32[1,4096]{1,0:T(1,128)S(1)} %bitcast.17), custom_call_target="tpu_custom_call" | custom-call | tf_op jit(solution)/shard_map/pallas_call | solution.py:32
  46.2 2.4 %shard_map.72 = (bf16[2048,128]{1,0:T(8,128)(2,1)S(1)}, f32[16,2048]{1,0:T(8,128)}, f32[128,128]{1,0:T(8,128)S(1)}) custom-call(s32[4]{0:T(128)S(1)} %pad_add_fusion.refs_0_, bf16[128,2048]{1,0:T(8,128)(2,1)S(1)} %collective-permute-done.4.refs_1_, f32[128,128]{1,0:T(8,128)S(1)} %copy-done, bf16[128,2048]{1,0:T(8,128)(2,1)S(1)} %get-tuple-element.23.refs_3_, ...), custom_call_target="tpu_custom_call" | custom-call | tf_op jit(solution)/shard_map/pallas_call | solution.py:32
  48.5 11.5 %shard_map.73 = (f32[128,4096]{1,0:T(8,128)S(1)}, bf16[128,2048]{1,0:T(8,128)(2,1)S(1)}) custom-call(bf16[2048,128]{1,0:T(8,128)(2,1)S(1)} %get-tuple-element.29.refs_0_, bf16[128,2048]{1,0:T(8,128)(2,1)S(1)} %collective-permute-done.4.refs_1_, bf16[128,4096]{1,0:T(8,128)(2,1)S(1)} %bitcast.14, f32[1,4096]{1,0:T(1,128)S(1)} %bitcast.18, ...), custom_call_target="tpu_custom_call" | custom-call | tf_op jit(solution)/shard_map/pallas_call | solution.py:32
  60.0 4.0 %collective-permute-start.6 = (bf16[128,2048]{1,0:T(8,128)(2,1)S(1)}, bf16[128,2048]{1,0:T(8,128)(2,1)S(1)}, u32[]{:S(2)}, u32[]{:S(2)}) collective-permute-start(bf16[128,2048]{1,0:T(8,128)(2,1)S(1)} %get-tuple-element.31.refs_6_), channel_id=1, source_target_pairs={{0,8},{8,0},{1,9},{9,1},{2,10},{10,2},{3,11},{11,3},{4,12},{12,4},... | collective-permute-start | bytes 1572872 | tf_op jit(solution)/shard_map/ppermute | solution.py:277
  64.3 2.9 %shard_map.74 = (f32[128,1024]{1,0:T(8,128)S(1)}, f32[2048,128]{1,0:T(8,128)S(1)}) custom-call(bf16[2048,128]{1,0:T(8,128)(2,1)S(1)} %get-tuple-element.25.refs_0_.refs_8_.refs_6_.refs_1_, bf16[128,2048]{1,0:T(8,128)(2,1)S(1)} %get-tuple-element.22.refs_1_.refs_6_.refs_7_.refs_2_, bf16[128,4096]{1,0:T(8,128)(2,1)S(1)} %bitcast.15, f32[1,4096]{1,0:T(1,128)S(1)} %bitcast.19, ...), custom_call_target="tpu_custom_call" | custom-call | tf_op jit(solution)/shard_map/pallas_call | solution.py:32
  67.2 5.1 %shard_map.75 = (bf16[128,4096]{1,0:T(8,128)(2,1)}, f32[32,2048]{1,0:T(8,128)S(1)}, bf16[32,2048]{1,0:T(8,128)(2,1)S(1)}, bf16[32,2048]{1,0:T(8,128)(2,1)S(1)}, bf16[32,2048]{1,0:T(8,128)(2,1)S(1)}) custom-call(s32[4]{0:T(128)S(1)} %pad_add_fusion.refs_0_, bf16[2048,128]{1,0:T(8,128)(2,1)S(1)} %get-tuple-element.25.refs_0_.refs_8_.refs_6_.refs_1_, ...), custom_call_target="tpu_custom_call" | custom-call | tf_op jit(solution)/shard_map/pallas_call | solution.py:32
  72.3 4.7 %all-to-all-start.1 = ((bf16[16,8,4096]{2,1,0:T(8,128)(2,1)}), bf16[16,8,4096]{2,1,0:T(8,128)(2,1)S(1)}, u32[]{:S(2)}, u32[]{:S(2)}) async-start(bf16[16,8,4096]{2,1,0:T(8,128)(2,1)} %bitcast.23), calls=%async_computation.1 | async-start | bytes 2097152 | tf_op jit(solution)/shard_map/all_to_all | solution.py:293
  77.7 2.7 %collective-permute-start.9 = (bf16[32,2048]{1,0:T(8,128)(2,1)S(1)}, bf16[32,2048]{1,0:T(8,128)(2,1)S(1)}, u32[]{:S(2)}, u32[]{:S(2)}) collective-permute-start(bf16[32,2048]{1,0:T(8,128)(2,1)S(1)} %get-tuple-element.37), channel_id=1, source_target_pairs={{0,6},{2,0},{4,2},{6,4},{1,7},{3,1},{5,3},{7,5},{8,14},{10,8},{12,... | collective-permute-start | bytes 393224 | tf_op jit(solution)/shard_map/ppermute | solution.py:299
  81.2 2.9 %collective-permute-done.8.refs_2_ = bf16[32,2048]{1,0:T(8,128)(2,1)S(1)} collective-permute-done((bf16[32,2048]{1,0:T(8,128)(2,1)S(1)}, bf16[32,2048]{1,0:T(8,128)(2,1)S(1)}, u32[]{:S(2)}, u32[]{:S(2)}) %collective-permute-start.8) | collective-permute-done | bytes 131104 | tf_op jit(solution)/shard_map/ppermute | solution.py:299
  84.1 2.1 %collective-permute-done.9.refs_3_ = bf16[32,2048]{1,0:T(8,128)(2,1)S(1)} collective-permute-done((bf16[32,2048]{1,0:T(8,128)(2,1)S(1)}, bf16[32,2048]{1,0:T(8,128)(2,1)S(1)}, u32[]{:S(2)}, u32[]{:S(2)}) %collective-permute-start.9) | collective-permute-done | bytes 131104 | tf_op jit(solution)/shard_map/ppermute | solution.py:299
  86.2 0.9 collective-permute-done.10.refs_4_
  87.7 2.0 %collective-permute-start.11 = (bf16[16,2048]{1,0:T(8,128)(2,1)S(1)}, bf16[16,2048]{1,0:T(8,128)(2,1)S(1)}, u32[]{:S(2)}, u32[]{:S(2)}) collective-permute-start(bf16[16,2048]{1,0:T(8,128)(2,1)S(1)} %get-tuple-element.40), channel_id=1, source_target_pairs={{0,1},{1,0},{2,3},{3,2},{4,5},{5,4},{6,7},{7,6},{8,9},{9,8},{10,11... | collective-permute-start | bytes 196616 | tf_op jit(solution)/shard_map/ppermute | solution.py:309
  89.7 3.8 %collective-permute-done.11.refs_2_ = bf16[16,2048]{1,0:T(8,128)(2,1)S(1)} collective-permute-done((bf16[16,2048]{1,0:T(8,128)(2,1)S(1)}, bf16[16,2048]{1,0:T(8,128)(2,1)S(1)}, u32[]{:S(2)}, u32[]{:S(2)}) %collective-permute-start.11) | collective-permute-done | bytes 65568 | tf_op jit(solution)/shard_map/ppermute | solution.py:309
  (27 shorter events, 6.4 us)
Async XLA Ops:
  0.6 36.6 %copy-start = (f32[128,128]{1,0:T(8,128)S(1)}, f32[128,128]{1,0:T(8,128)}, u32[]{:S(2)}) copy-start(f32[128,128]{1,0:T(8,128)} %refs_11_.1) | copy-start | bytes 196612
  0.6 0.9 copy-start.1
  1.6 7.7 %copy-start.3 = (bf16[16,2,8,128]{3,2,1,0:T(8,128)(2,1)S(1)}, bf16[16,2,8,128]{3,2,1,0:T(8,128)(2,1)}, u32[]{:S(2)}) copy-start(bf16[16,2,8,128]{3,2,1,0:T(8,128)(2,1)} %refs_0_.2) | copy-start | bytes 196612
  2.6 43.5 %copy-start.4 = (s32[6,2,8,128]{3,2,1,0:T(8,128)S(1)}, s32[6,2,8,128]{3,2,1,0:T(8,128)}, u32[]{:S(2)}) copy-start(s32[6,2,8,128]{3,2,1,0:T(8,128)} %refs_5_.3) | copy-start | bytes 147460
  2.7 37.8 %all-to-all-start = ((bf16[16,8,4096]{2,1,0:T(8,128)(2,1)}), bf16[16,8,4096]{2,1,0:T(8,128)(2,1)S(1)}, u32[]{:S(2)}, u32[]{:S(2)}) async-start(bf16[16,8,4096]{2,1,0:T(8,128)(2,1)} %bitcast.22), calls=%async_computation | async-start | bytes 2097152 | tf_op jit(solution)/shard_map/all_to_all | solution.py:238
  9.3 17.2 %collective-permute-start = (bf16[16,2,8,128]{3,2,1,0:T(8,128)(2,1)S(1)}, bf16[16,2,8,128]{3,2,1,0:T(8,128)(2,1)S(1)}, u32[]{:S(2)}, u32[]{:S(2)}) collective-permute-start(bf16[16,2,8,128]{3,2,1,0:T(8,128)(2,1)S(1)} %copy-done.3), channel_id=1, source_target_pairs={{0,1},{1,0},{2,3},{3,2},{4,5},{5,4},{6,7},{7,6},{8,9},{9,8},{10,11... | collective-permute-start | bytes 196616 | tf_op jit(solution)/shard_map/ppermute | solution.py:239
  26.7 7.6 %collective-permute-start.3 = (bf16[32,2048]{1,0:T(8,128)(2,1)S(1)}, bf16[32,2048]{1,0:T(8,128)(2,1)S(1)}, u32[]{:S(2)}, u32[]{:S(2)}) collective-permute-start(bf16[32,2048]{1,0:T(8,128)(2,1)S(1)} %shard_map.68.refs_1_), channel_id=1, source_target_pairs={{0,4},{2,6},{4,0},{6,2},{1,5},{3,7},{5,1},{7,3},{8,12},{10,14},{12... | collective-permute-start | bytes 393224 | tf_op jit(solution)/shard_map/ppermute | solution.py:241
  30.0 6.8 %collective-permute-start.2 = (bf16[32,2048]{1,0:T(8,128)(2,1)S(1)}, bf16[32,2048]{1,0:T(8,128)(2,1)S(1)}, u32[]{:S(2)}, u32[]{:S(2)}) collective-permute-start(bf16[32,2048]{1,0:T(8,128)(2,1)S(1)} %shard_map.68.refs_1_), channel_id=1, source_target_pairs={{0,6},{2,0},{4,2},{6,4},{1,7},{3,1},{5,3},{7,5},{8,14},{10,8},{12,... | collective-permute-start | bytes 393224 | tf_op jit(solution)/shard_map/ppermute | solution.py:241
  31.1 6.2 %collective-permute-start.1 = (bf16[32,2048]{1,0:T(8,128)(2,1)S(1)}, bf16[32,2048]{1,0:T(8,128)(2,1)S(1)}, u32[]{:S(2)}, u32[]{:S(2)}) collective-permute-start(bf16[32,2048]{1,0:T(8,128)(2,1)S(1)} %shard_map.68.refs_1_), channel_id=1, source_target_pairs={{0,2},{2,4},{4,6},{6,0},{1,3},{3,5},{5,7},{7,1},{8,10},{10,12},{12... | collective-permute-start | bytes 393224 | tf_op jit(solution)/shard_map/ppermute | solution.py:241
  38.9 7.2 %collective-permute-start.4 = (bf16[128,2048]{1,0:T(8,128)(2,1)S(1)}, bf16[128,2048]{1,0:T(8,128)(2,1)S(1)}, u32[]{:S(2)}, u32[]{:S(2)}) collective-permute-start(bf16[128,2048]{1,0:T(8,128)(2,1)S(1)} %get-tuple-element.22.refs_1_.refs_6_.refs_7_.refs_2_), channel_id=1, source_target_pairs={{0,8},{8,0},{1,9},{9,1},{2,10},{10,2},{3,11},{11,3},{4,12},{12,4},... | collective-permute-start | bytes 1572872 | tf_op jit(solution)/shard_map/ppermute | solution.py:248
  38.9 7.2 %collective-permute-start.5 = (bf16[128,1024]{1,0:T(8,128)(2,1)}, bf16[128,1024]{1,0:T(8,128)(2,1)S(1)}, u32[]{:S(2)}, u32[]{:S(2)}) collective-permute-start(bf16[128,1024]{1,0:T(8,128)(2,1)} %get-tuple-element.24), channel_id=1, source_target_pairs={{8,16},{24,32},{40,48},{56,64},{72,80},{88,96},{104,112},{16,8},{3... | collective-permute-start | bytes 786440 | tf_op jit(solution)/shard_map/ppermute | solution.py:251
  60.0 7.2 %collective-permute-start.6 = (bf16[128,2048]{1,0:T(8,128)(2,1)S(1)}, bf16[128,2048]{1,0:T(8,128)(2,1)S(1)}, u32[]{:S(2)}, u32[]{:S(2)}) collective-permute-start(bf16[128,2048]{1,0:T(8,128)(2,1)S(1)} %get-tuple-element.31.refs_6_), channel_id=1, source_target_pairs={{0,8},{8,0},{1,9},{9,1},{2,10},{10,2},{3,11},{11,3},{4,12},{12,4},... | collective-permute-start | bytes 1572872 | tf_op jit(solution)/shard_map/ppermute | solution.py:277
  64.0 3.3 %collective-permute-start.7 = (f32[128,128]{1,0:T(8,128)S(1)}, f32[128,128]{1,0:T(8,128)S(1)}, u32[]{:S(2)}, u32[]{:S(2)}) collective-permute-start(f32[128,128]{1,0:T(8,128)S(1)} %get-tuple-element.34.refs_9_), channel_id=1, source_target_pairs={{0,8},{8,0},{1,9},{9,1},{2,10},{10,2},{3,11},{11,3},{4,12},{12,4},... | collective-permute-start | bytes 196616 | tf_op jit(solution)/shard_map/ppermute | solution.py:269
  72.3 21.2 %copy-start.2 = (f32[16,2048]{1,0:T(8,128)S(1)}, f32[16,2048]{1,0:T(8,128)}, u32[]{:S(2)}) copy-start(f32[16,2048]{1,0:T(8,128)} %get-tuple-element.28.refs_0_) | copy-start | bytes 393220
  72.3 22.0 %all-to-all-start.1 = ((bf16[16,8,4096]{2,1,0:T(8,128)(2,1)}), bf16[16,8,4096]{2,1,0:T(8,128)(2,1)S(1)}, u32[]{:S(2)}, u32[]{:S(2)}) async-start(bf16[16,8,4096]{2,1,0:T(8,128)(2,1)} %bitcast.23), calls=%async_computation.1 | async-start | bytes 2097152 | tf_op jit(solution)/shard_map/all_to_all | solution.py:293
  77.1 7.0 %collective-permute-start.8 = (bf16[32,2048]{1,0:T(8,128)(2,1)S(1)}, bf16[32,2048]{1,0:T(8,128)(2,1)S(1)}, u32[]{:S(2)}, u32[]{:S(2)}) collective-permute-start(bf16[32,2048]{1,0:T(8,128)(2,1)S(1)} %get-tuple-element.36), channel_id=1, source_target_pairs={{0,2},{2,4},{4,6},{6,0},{1,3},{3,5},{5,7},{7,1},{8,10},{10,12},{12... | collective-permute-start | bytes 393224 | tf_op jit(solution)/shard_map/ppermute | solution.py:299
  77.7 8.5 %collective-permute-start.9 = (bf16[32,2048]{1,0:T(8,128)(2,1)S(1)}, bf16[32,2048]{1,0:T(8,128)(2,1)S(1)}, u32[]{:S(2)}, u32[]{:S(2)}) collective-permute-start(bf16[32,2048]{1,0:T(8,128)(2,1)S(1)} %get-tuple-element.37), channel_id=1, source_target_pairs={{0,6},{2,0},{4,2},{6,4},{1,7},{3,1},{5,3},{7,5},{8,14},{10,8},{12,... | collective-permute-start | bytes 393224 | tf_op jit(solution)/shard_map/ppermute | solution.py:299
  80.4 6.7 %collective-permute-start.10 = (bf16[32,2048]{1,0:T(8,128)(2,1)S(1)}, bf16[32,2048]{1,0:T(8,128)(2,1)S(1)}, u32[]{:S(2)}, u32[]{:S(2)}) collective-permute-start(bf16[32,2048]{1,0:T(8,128)(2,1)S(1)} %get-tuple-element.38), channel_id=1, source_target_pairs={{0,4},{2,6},{4,0},{6,2},{1,5},{3,7},{5,1},{7,3},{8,12},{10,14},{12... | collective-permute-start | bytes 393224 | tf_op jit(solution)/shard_map/ppermute | solution.py:299
  87.7 5.8 %collective-permute-start.11 = (bf16[16,2048]{1,0:T(8,128)(2,1)S(1)}, bf16[16,2048]{1,0:T(8,128)(2,1)S(1)}, u32[]{:S(2)}, u32[]{:S(2)}) collective-permute-start(bf16[16,2048]{1,0:T(8,128)(2,1)S(1)} %get-tuple-element.40), channel_id=1, source_target_pairs={{0,1},{1,0},{2,3},{3,2},{4,5},{5,4},{6,7},{7,6},{8,9},{9,8},{10,11... | collective-permute-start | bytes 196616 | tf_op jit(solution)/shard_map/ppermute | solution.py:309

commit v7 on v6

--- a/solution.py
+++ b/solution.py
@@ -33,9 +33,9 @@
         reading,
         in_specs=[pl.BlockSpec(memory_space=pltpu.SMEM)] * len(scalars)
         + [vm] * (len(args) + len(held)),
-        out_specs=[vm] * len(outs),
+        out_specs=[pl.BlockSpec(memory_space=pl.ANY) if keep is None else vm for _, _, keep in outs],
         out_shape=[(pltpu.VMEM if keep else pltpu.HBM)(shape, dtype) for shape, dtype, keep in outs],
-        scratch_shapes=[pltpu.VMEM(shape, dtype) for shape, dtype in scratch],
+        scratch_shapes=[pltpu.VMEM(*kind) if isinstance(kind, tuple) else kind for kind in scratch],
         compiler_params=pltpu.CompilerParams(vmem_limit_bytes=limit << 20),
     )(*scalars, *args, *held)
 
@@ -165,7 +165,7 @@
 
 def last_body(
     scale, at_ref, kt_ref, u_ref, v_ref, g_ref, l_ref, more_ref, ov_ref, got_ref, ma_ref, mb_ref, core_ref,
-    out_ref, me_ref, up_ref, dn_ref, away_ref, ov_s, tot_s, w_s,
+    out_hbm, me_ref, up_ref, dn_ref, away_ref, ov_s, tot_s, w_s, out_ref, sems,
 ):
     rank, count = out_ref.shape
     middle = count - count // 2
@@ -182,11 +182,17 @@
 
     send(0, middle, l_ref[:, :middle])
     send(middle, start - middle, l_ref[:, middle:start] + more_ref[...])
+    leave = [
+        pltpu.make_async_copy(out_ref.at[:, :start], out_hbm.at[:, :start], sems.at[0]),
+        pltpu.make_async_copy(out_ref.at[:, start:], out_hbm.at[:, start:], sems.at[1]),
+    ]
+    leave[0].start()
 
     def store(here, acc):
         send(start, count - start, l_ref[:, start:] + acc)
 
     sweep(kt_ref, u_ref, v_ref, g_ref, ov_s, start, count, store)
+    leave[1].start()
     tot_s[...] = ov_s[...].T + got_ref[...].astype(f32)
     rows = me_ref.shape[0]
     y = at_ref[2]
@@ -198,6 +204,17 @@
     up_ref[...] = part(1).astype(bf16)
     away_ref[...] = part(2).astype(bf16)
     dn_ref[...] = part(3).astype(bf16)
+    for copy in leave:
+        copy.wait()
+
+
+def gain_body(got_ref, out_ref):
+    chips, parts, _, half = got_ref.shape
+    for p in range(parts):
+        total = got_ref[0, p].astype(f32)
+        for k in range(1, chips):
+            total = total + got_ref[k, p].astype(f32)
+        out_ref[:, p * half : (p + 1) * half] = total
 
 
 def done_body(scale, base_ref, mine_ref, got_ref, out_ref):
@@ -285,14 +302,21 @@
     l_part, me, up, dn, away = small(
         functools.partial(last_body, scale),
         [kt_own, u_own, v, growth, l_most, l_more, ov_more, got, m_own, m_oth, core_s],
-        [((rank, half), bf16, False), ((rows, cells), f32, True)] + [((rows, cells), bf16, True)] * 3,
-        [((cells, rank), f32), ((rank, cells), f32), ((2 * rank, rank), bf16)],
+        [((rank, half), bf16, None), ((rows, cells), f32, True)] + [((rows, cells), bf16, True)] * 3,
+        [
+            ((cells, rank), f32),
+            ((rank, cells), f32),
+            ((2 * rank, rank), bf16),
+            ((rank, half), bf16),
+            pltpu.SemaphoreType.DMA((2,)),
+        ],
         at=where_at,
     )
 
     l_got = lax.all_to_all(l_part, SPACE, 0, 0, tiled=True)
-    l_new = l_got.reshape(n_space // 2, 2, lanes, half).astype(f32).sum(0)
-    l_new = jnp.transpose(l_new, (1, 0, 2)).reshape(lanes, samp_rows)
+    (l_new,) = small(
+        gain_body, [resident(l_got.reshape(n_space // 2, 2, lanes, half))], [((lanes, samp_rows), f32, False)]
+    )
 
     near = []
     for part, k in ((up, 1), (dn, 3), (away, 2)):
@@ -304,9 +328,10 @@
         [((rows, cells), f32)],
         at=where_at,
     )
+    last = resident(lax.ppermute(send, "xh", swap))
     (k_new,) = small(
         functools.partial(done_body, step_size * samp_weight),
-        [base, mine, resident(lax.ppermute(send, "xh", swap))],
+        [base, mine, last],
         [(basis_u.shape, f32, False)],
     )
     return (k_new, l_new)

time: 95.8 us -> 95.7 us (level)
    pallas_call x10 -> x11, Pallas kernels: 31.8 us -> 32.5 us  [small(): pl.pallas_call(reading, in_specs=[pl.BlockSpec(memory_space=pltpu.SMEM)]...]
where the time goes in v7:
time: 95.7 us; the launch traced here: 95 us
  Pallas kernels  32.5 us (34%)
  starting transfers between devices  30.8 us (32%)
  waiting for transfers between devices  29.2 us (31%)
    pallas_call x11, Pallas kernels, small(): pl.pallas_call(reading, in_specs=[pl.BlockSpec(memory_space=pltpu.SMEM)]...  32.5 us
    ppermute x1, waiting for transfers between devices, per_device(): u1 = resident(lax.ppermute(basis_u, 'xh', swap))  14.4 us
    all_to_all x1, starting transfers between devices, per_device(): lax.all_to_all(v_wide.reshape(rank, half), SPACE, 0, 0, tiled=True)  6.59 us
    ppermute x3, waiting for transfers between devices, per_device(): near.append(resident(lax.ppermute(part, 'y', ring(4, k))))  5.87 us
    ppermute x3, starting transfers between devices, per_device(): around = [resident(lax.ppermute(pair, 'y', ring(4, k))) for k in (1, 3, 2)]  5.3 us
    ppermute x3, waiting for transfers between devices, per_device(): around = [resident(lax.ppermute(pair, 'y', ring(4, k))) for k in (1, 3, 2)]  5.13 us
    all_to_all x1, starting transfers between devices, per_device(): l_got = lax.all_to_all(l_part, SPACE, 0, 0, tiled=True)  4.75 us
    ppermute x3, starting transfers between devices, per_device(): near.append(resident(lax.ppermute(part, 'y', ring(4, k))))  4.12 us
  transfers between devices with their start and end apart: 14, of which 8 were waited for; matrix products, arithmetic and copies ran while one was open for 1% of the time, Pallas kernels for 12%

profile of v7, /device:TPU:0, one launch (start us, length us, event | category | flops | bytes accessed | tf_op | source)
XLA Modules:
  0.0 95.0 jit_solution(16583850478983764535)
XLA Ops:
  0.6 0.9 copy-done.1
  1.6 1.1 %shard_map.70 = bf16[8,2,8,4096]{3,2,1,0:T(8,128)(2,1)} custom-call(bf16[8,8192]{1,0:T(8,128)(2,1)S(1)} %copy-done.1), custom_call_target="tpu_custom_call" | custom-call | tf_op jit(solution)/shard_map/pallas_call | solution.py:32
  2.7 6.6 %all-to-all-start = ((bf16[16,8,4096]{2,1,0:T(8,128)(2,1)}), bf16[16,8,4096]{2,1,0:T(8,128)(2,1)S(1)}, u32[]{:S(2)}, u32[]{:S(2)}) async-start(bf16[16,8,4096]{2,1,0:T(8,128)(2,1)} %bitcast.18), calls=%async_computation | async-start | bytes 2097152 | tf_op jit(solution)/shard_map/all_to_all | solution.py:255
  9.3 2.8 %collective-permute-start = (bf16[16,2,8,128]{3,2,1,0:T(8,128)(2,1)S(1)}, bf16[16,2,8,128]{3,2,1,0:T(8,128)(2,1)S(1)}, u32[]{:S(2)}, u32[]{:S(2)}) collective-permute-start(bf16[16,2,8,128]{3,2,1,0:T(8,128)(2,1)S(1)} %copy-done.3), channel_id=1, source_target_pairs={{0,1},{1,0},{2,3},{3,2},{4,5},{5,4},{6,7},{7,6},{8,9},{9,8},{10,11... | collective-permute-start | bytes 196616 | tf_op jit(solution)/shard_map/ppermute | solution.py:256
  12.1 14.4 %collective-permute-done.refs_1_ = bf16[16,2,8,128]{3,2,1,0:T(8,128)(2,1)S(1)} collective-permute-done((bf16[16,2,8,128]{3,2,1,0:T(8,128)(2,1)S(1)}, bf16[16,2,8,128]{3,2,1,0:T(8,128)(2,1)S(1)}, u32[]{:S(2)}, u32[]{:S(2)}) %collective-permute-start) | collective-permute-done | bytes 65568 | tf_op jit(solution)/shard_map/ppermute | solution.py:256
  26.7 3.3 %collective-permute-start.3 = (bf16[32,2048]{1,0:T(8,128)(2,1)S(1)}, bf16[32,2048]{1,0:T(8,128)(2,1)S(1)}, u32[]{:S(2)}, u32[]{:S(2)}) collective-permute-start(bf16[32,2048]{1,0:T(8,128)(2,1)S(1)} %shard_map.68.refs_1_), channel_id=1, source_target_pairs={{0,4},{2,6},{4,0},{6,2},{1,5},{3,7},{5,1},{7,3},{8,12},{10,14},{12... | collective-permute-start | bytes 393224 | tf_op jit(solution)/shard_map/ppermute | solution.py:258
  30.0 1.1 %collective-permute-start.2 = (bf16[32,2048]{1,0:T(8,128)(2,1)S(1)}, bf16[32,2048]{1,0:T(8,128)(2,1)S(1)}, u32[]{:S(2)}, u32[]{:S(2)}) collective-permute-start(bf16[32,2048]{1,0:T(8,128)(2,1)S(1)} %shard_map.68.refs_1_), channel_id=1, source_target_pairs={{0,6},{2,0},{4,2},{6,4},{1,7},{3,1},{5,3},{7,5},{8,14},{10,8},{12,... | collective-permute-start | bytes 393224 | tf_op jit(solution)/shard_map/ppermute | solution.py:258
  31.1 1.0 %collective-permute-start.1 = (bf16[32,2048]{1,0:T(8,128)(2,1)S(1)}, bf16[32,2048]{1,0:T(8,128)(2,1)S(1)}, u32[]{:S(2)}, u32[]{:S(2)}) collective-permute-start(bf16[32,2048]{1,0:T(8,128)(2,1)S(1)} %shard_map.68.refs_1_), channel_id=1, source_target_pairs={{0,2},{2,4},{4,6},{6,0},{1,3},{3,5},{5,7},{7,1},{8,10},{10,12},{12... | collective-permute-start | bytes 393224 | tf_op jit(solution)/shard_map/ppermute | solution.py:258
  32.1 2.2 %collective-permute-done.3.refs_4_ = bf16[32,2048]{1,0:T(8,128)(2,1)S(1)} collective-permute-done((bf16[32,2048]{1,0:T(8,128)(2,1)S(1)}, bf16[32,2048]{1,0:T(8,128)(2,1)S(1)}, u32[]{:S(2)}, u32[]{:S(2)}) %collective-permute-start.3) | collective-permute-done | bytes 131104 | tf_op jit(solution)/shard_map/ppermute | solution.py:258
  34.3 2.5 %collective-permute-done.2.refs_3_ = bf16[32,2048]{1,0:T(8,128)(2,1)S(1)} collective-permute-done((bf16[32,2048]{1,0:T(8,128)(2,1)S(1)}, bf16[32,2048]{1,0:T(8,128)(2,1)S(1)}, u32[]{:S(2)}, u32[]{:S(2)}) %collective-permute-start.2) | collective-permute-done | bytes 131104 | tf_op jit(solution)/shard_map/ppermute | solution.py:258
  37.3 1.7 %shard_map.69 = (bf16[128,2048]{1,0:T(8,128)(2,1)S(1)}, bf16[128,2048]{1,0:T(8,128)(2,1)S(1)}, bf16[2048,128]{1,0:T(8,128)(2,1)S(1)}, bf16[128,1024]{1,0:T(8,128)(2,1)}) custom-call(s32[4]{0:T(128)S(1)} %pad_add_fusion.refs_0_, bf16[32,2048]{1,0:T(8,128)(2,1)S(1)} %shard_map.68.refs_1_, bf16[32,2048]{1,0:T(8,128)(2,1)S(1)} %collective-permute-done.1.refs_2_, ...), custom_call_target="tpu_custom_call" | custom-call | tf_op jit(solution)/shard_map/pallas_call | solution.py:32
  40.5 5.6 %shard_map.71 = (f32[128,2048]{1,0:T(8,128)S(1)}, f32[2048,128]{1,0:T(8,128)S(1)}) custom-call(bf16[2048,128]{1,0:T(8,128)(2,1)S(1)} %get-tuple-element.25.refs_0_.refs_8_.refs_6_.refs_1_, bf16[128,2048]{1,0:T(8,128)(2,1)S(1)} %get-tuple-element.22.refs_1_.refs_6_.refs_7_.refs_2_, bf16[128,4096]{1,0:T(8,128)(2,1)S(1)} %bitcast.9, f32[1,4096]{1,0:T(1,128)S(1)} %bitcast.14), custom_call_target="tpu_custom_call" | custom-call | tf_op jit(solution)/shard_map/pallas_call | solution.py:32
  46.2 2.4 %shard_map.72 = (bf16[2048,128]{1,0:T(8,128)(2,1)S(1)}, f32[16,2048]{1,0:T(8,128)}, f32[128,128]{1,0:T(8,128)S(1)}) custom-call(s32[4]{0:T(128)S(1)} %pad_add_fusion.refs_0_, bf16[128,2048]{1,0:T(8,128)(2,1)S(1)} %collective-permute-done.4.refs_1_, f32[128,128]{1,0:T(8,128)S(1)} %copy-done, bf16[128,2048]{1,0:T(8,128)(2,1)S(1)} %get-tuple-element.23.refs_3_, ...), custom_call_target="tpu_custom_call" | custom-call | tf_op jit(solution)/shard_map/pallas_call | solution.py:32
  48.5 11.5 %shard_map.73 = (f32[128,4096]{1,0:T(8,128)S(1)}, bf16[128,2048]{1,0:T(8,128)(2,1)S(1)}) custom-call(bf16[2048,128]{1,0:T(8,128)(2,1)S(1)} %get-tuple-element.29.refs_0_, bf16[128,2048]{1,0:T(8,128)(2,1)S(1)} %collective-permute-done.4.refs_1_, bf16[128,4096]{1,0:T(8,128)(2,1)S(1)} %bitcast.10, f32[1,4096]{1,0:T(1,128)S(1)} %bitcast.15, ...), custom_call_target="tpu_custom_call" | custom-call | tf_op jit(solution)/shard_map/pallas_call | solution.py:32
  60.0 4.0 %collective-permute-start.6 = (bf16[128,2048]{1,0:T(8,128)(2,1)S(1)}, bf16[128,2048]{1,0:T(8,128)(2,1)S(1)}, u32[]{:S(2)}, u32[]{:S(2)}) collective-permute-start(bf16[128,2048]{1,0:T(8,128)(2,1)S(1)} %get-tuple-element.31.refs_6_), channel_id=1, source_target_pairs={{0,8},{8,0},{1,9},{9,1},{2,10},{10,2},{3,11},{11,3},{4,12},{12,4},... | collective-permute-start | bytes 1572872 | tf_op jit(solution)/shard_map/ppermute | solution.py:294
  64.3 2.9 %shard_map.74 = (f32[128,1024]{1,0:T(8,128)S(1)}, f32[2048,128]{1,0:T(8,128)S(1)}) custom-call(bf16[2048,128]{1,0:T(8,128)(2,1)S(1)} %get-tuple-element.25.refs_0_.refs_8_.refs_6_.refs_1_, bf16[128,2048]{1,0:T(8,128)(2,1)S(1)} %get-tuple-element.22.refs_1_.refs_6_.refs_7_.refs_2_, bf16[128,4096]{1,0:T(8,128)(2,1)S(1)} %bitcast.11, f32[1,4096]{1,0:T(1,128)S(1)} %bitcast.16, ...), custom_call_target="tpu_custom_call" | custom-call | tf_op jit(solution)/shard_map/pallas_call | solution.py:32
  67.3 4.9 %shard_map.75 = (bf16[128,4096]{1,0:T(8,128)(2,1)}, f32[32,2048]{1,0:T(8,128)S(1)}, bf16[32,2048]{1,0:T(8,128)(2,1)S(1)}, bf16[32,2048]{1,0:T(8,128)(2,1)S(1)}, bf16[32,2048]{1,0:T(8,128)(2,1)S(1)}) custom-call(s32[4]{0:T(128)S(1)} %pad_add_fusion.refs_0_, bf16[2048,128]{1,0:T(8,128)(2,1)S(1)} %get-tuple-element.25.refs_0_.refs_8_.refs_6_.refs_1_, ...), custom_call_target="tpu_custom_call" | custom-call | tf_op jit(solution)/shard_map/pallas_call | solution.py:32
  72.2 4.7 %all-to-all-start.1 = ((bf16[16,8,4096]{2,1,0:T(8,128)(2,1)}), bf16[16,8,4096]{2,1,0:T(8,128)(2,1)S(1)}, u32[]{:S(2)}, u32[]{:S(2)}) async-start(bf16[16,8,4096]{2,1,0:T(8,128)(2,1)} %bitcast.19), calls=%async_computation.1 | async-start | bytes 2097152 | tf_op jit(solution)/shard_map/all_to_all | solution.py:316
  77.6 2.7 %collective-permute-start.9 = (bf16[32,2048]{1,0:T(8,128)(2,1)S(1)}, bf16[32,2048]{1,0:T(8,128)(2,1)S(1)}, u32[]{:S(2)}, u32[]{:S(2)}) collective-permute-start(bf16[32,2048]{1,0:T(8,128)(2,1)S(1)} %get-tuple-element.37), channel_id=1, source_target_pairs={{0,6},{2,0},{4,2},{6,4},{1,7},{3,1},{5,3},{7,5},{8,14},{10,8},{12,... | collective-permute-start | bytes 393224 | tf_op jit(solution)/shard_map/ppermute | solution.py:323
  81.1 2.9 %collective-permute-done.8.refs_2_ = bf16[32,2048]{1,0:T(8,128)(2,1)S(1)} collective-permute-done((bf16[32,2048]{1,0:T(8,128)(2,1)S(1)}, bf16[32,2048]{1,0:T(8,128)(2,1)S(1)}, u32[]{:S(2)}, u32[]{:S(2)}) %collective-permute-start.8) | collective-permute-done | bytes 131104 | tf_op jit(solution)/shard_map/ppermute | solution.py:323
  84.0 2.1 %collective-permute-done.9.refs_3_ = bf16[32,2048]{1,0:T(8,128)(2,1)S(1)} collective-permute-done((bf16[32,2048]{1,0:T(8,128)(2,1)S(1)}, bf16[32,2048]{1,0:T(8,128)(2,1)S(1)}, u32[]{:S(2)}, u32[]{:S(2)}) %collective-permute-start.9) | collective-permute-done | bytes 131104 | tf_op jit(solution)/shard_map/ppermute | solution.py:323
  86.1 0.9 collective-permute-done.10.refs_4_
  87.6 2.0 %collective-permute-start.11 = (bf16[16,2048]{1,0:T(8,128)(2,1)S(1)}, bf16[16,2048]{1,0:T(8,128)(2,1)S(1)}, u32[]{:S(2)}, u32[]{:S(2)}) collective-permute-start(bf16[16,2048]{1,0:T(8,128)(2,1)S(1)} %get-tuple-element.40), channel_id=1, source_target_pairs={{0,1},{1,0},{2,3},{3,2},{4,5},{5,4},{6,7},{7,6},{8,9},{9,8},{10,11... | collective-permute-start | bytes 196616 | tf_op jit(solution)/shard_map/ppermute | solution.py:331
  89.6 3.8 %collective-permute-done.11.refs_2_ = bf16[16,2048]{1,0:T(8,128)(2,1)S(1)} collective-permute-done((bf16[16,2048]{1,0:T(8,128)(2,1)S(1)}, bf16[16,2048]{1,0:T(8,128)(2,1)S(1)}, u32[]{:S(2)}, u32[]{:S(2)}) %collective-permute-start.11) | collective-permute-done | bytes 65568 | tf_op jit(solution)/shard_map/ppermute | solution.py:331
  (27 shorter events, 6.4 us)
Async XLA Ops:
  0.6 36.6 %copy-start = (f32[128,128]{1,0:T(8,128)S(1)}, f32[128,128]{1,0:T(8,128)}, u32[]{:S(2)}) copy-start(f32[128,128]{1,0:T(8,128)} %refs_11_.1) | copy-start | bytes 196612
  0.6 0.9 copy-start.1
  1.6 7.7 %copy-start.3 = (bf16[16,2,8,128]{3,2,1,0:T(8,128)(2,1)S(1)}, bf16[16,2,8,128]{3,2,1,0:T(8,128)(2,1)}, u32[]{:S(2)}) copy-start(bf16[16,2,8,128]{3,2,1,0:T(8,128)(2,1)} %refs_0_.2) | copy-start | bytes 196612
  2.7 43.5 %copy-start.4 = (s32[6,2,8,128]{3,2,1,0:T(8,128)S(1)}, s32[6,2,8,128]{3,2,1,0:T(8,128)}, u32[]{:S(2)}) copy-start(s32[6,2,8,128]{3,2,1,0:T(8,128)} %refs_5_.3) | copy-start | bytes 147460
  2.7 37.8 %all-to-all-start = ((bf16[16,8,4096]{2,1,0:T(8,128)(2,1)}), bf16[16,8,4096]{2,1,0:T(8,128)(2,1)S(1)}, u32[]{:S(2)}, u32[]{:S(2)}) async-start(bf16[16,8,4096]{2,1,0:T(8,128)(2,1)} %bitcast.18), calls=%async_computation | async-start | bytes 2097152 | tf_op jit(solution)/shard_map/all_to_all | solution.py:255
  9.3 17.2 %collective-permute-start = (bf16[16,2,8,128]{3,2,1,0:T(8,128)(2,1)S(1)}, bf16[16,2,8,128]{3,2,1,0:T(8,128)(2,1)S(1)}, u32[]{:S(2)}, u32[]{:S(2)}) collective-permute-start(bf16[16,2,8,128]{3,2,1,0:T(8,128)(2,1)S(1)} %copy-done.3), channel_id=1, source_target_pairs={{0,1},{1,0},{2,3},{3,2},{4,5},{5,4},{6,7},{7,6},{8,9},{9,8},{10,11... | collective-permute-start | bytes 196616 | tf_op jit(solution)/shard_map/ppermute | solution.py:256
  26.7 7.6 %collective-permute-start.3 = (bf16[32,2048]{1,0:T(8,128)(2,1)S(1)}, bf16[32,2048]{1,0:T(8,128)(2,1)S(1)}, u32[]{:S(2)}, u32[]{:S(2)}) collective-permute-start(bf16[32,2048]{1,0:T(8,128)(2,1)S(1)} %shard_map.68.refs_1_), channel_id=1, source_target_pairs={{0,4},{2,6},{4,0},{6,2},{1,5},{3,7},{5,1},{7,3},{8,12},{10,14},{12... | collective-permute-start | bytes 393224 | tf_op jit(solution)/shard_map/ppermute | solution.py:258
  30.0 6.8 %collective-permute-start.2 = (bf16[32,2048]{1,0:T(8,128)(2,1)S(1)}, bf16[32,2048]{1,0:T(8,128)(2,1)S(1)}, u32[]{:S(2)}, u32[]{:S(2)}) collective-permute-start(bf16[32,2048]{1,0:T(8,128)(2,1)S(1)} %shard_map.68.refs_1_), channel_id=1, source_target_pairs={{0,6},{2,0},{4,2},{6,4},{1,7},{3,1},{5,3},{7,5},{8,14},{10,8},{12,... | collective-permute-start | bytes 393224 | tf_op jit(solution)/shard_map/ppermute | solution.py:258
  31.1 6.2 %collective-permute-start.1 = (bf16[32,2048]{1,0:T(8,128)(2,1)S(1)}, bf16[32,2048]{1,0:T(8,128)(2,1)S(1)}, u32[]{:S(2)}, u32[]{:S(2)}) collective-permute-start(bf16[32,2048]{1,0:T(8,128)(2,1)S(1)} %shard_map.68.refs_1_), channel_id=1, source_target_pairs={{0,2},{2,4},{4,6},{6,0},{1,3},{3,5},{5,7},{7,1},{8,10},{10,12},{12... | collective-permute-start | bytes 393224 | tf_op jit(solution)/shard_map/ppermute | solution.py:258
  38.9 7.2 %collective-permute-start.4 = (bf16[128,2048]{1,0:T(8,128)(2,1)S(1)}, bf16[128,2048]{1,0:T(8,128)(2,1)S(1)}, u32[]{:S(2)}, u32[]{:S(2)}) collective-permute-start(bf16[128,2048]{1,0:T(8,128)(2,1)S(1)} %get-tuple-element.22.refs_1_.refs_6_.refs_7_.refs_2_), channel_id=1, source_target_pairs={{0,8},{8,0},{1,9},{9,1},{2,10},{10,2},{3,11},{11,3},{4,12},{12,4},... | collective-permute-start | bytes 1572872 | tf_op jit(solution)/shard_map/ppermute | solution.py:265
  38.9 7.2 %collective-permute-start.5 = (bf16[128,1024]{1,0:T(8,128)(2,1)}, bf16[128,1024]{1,0:T(8,128)(2,1)S(1)}, u32[]{:S(2)}, u32[]{:S(2)}) collective-permute-start(bf16[128,1024]{1,0:T(8,128)(2,1)} %get-tuple-element.24), channel_id=1, source_target_pairs={{8,16},{24,32},{40,48},{56,64},{72,80},{88,96},{104,112},{16,8},{3... | collective-permute-start | bytes 786440 | tf_op jit(solution)/shard_map/ppermute | solution.py:268
  60.0 7.2 %collective-permute-start.6 = (bf16[128,2048]{1,0:T(8,128)(2,1)S(1)}, bf16[128,2048]{1,0:T(8,128)(2,1)S(1)}, u32[]{:S(2)}, u32[]{:S(2)}) collective-permute-start(bf16[128,2048]{1,0:T(8,128)(2,1)S(1)} %get-tuple-element.31.refs_6_), channel_id=1, source_target_pairs={{0,8},{8,0},{1,9},{9,1},{2,10},{10,2},{3,11},{11,3},{4,12},{12,4},... | collective-permute-start | bytes 1572872 | tf_op jit(solution)/shard_map/ppermute | solution.py:294
  64.0 3.3 %collective-permute-start.7 = (f32[128,128]{1,0:T(8,128)S(1)}, f32[128,128]{1,0:T(8,128)S(1)}, u32[]{:S(2)}, u32[]{:S(2)}) collective-permute-start(f32[128,128]{1,0:T(8,128)S(1)} %get-tuple-element.34.refs_9_), channel_id=1, source_target_pairs={{0,8},{8,0},{1,9},{9,1},{2,10},{10,2},{3,11},{11,3},{4,12},{12,4},... | collective-permute-start | bytes 196616 | tf_op jit(solution)/shard_map/ppermute | solution.py:286
  72.2 21.3 %copy-start.2 = (f32[16,2048]{1,0:T(8,128)S(1)}, f32[16,2048]{1,0:T(8,128)}, u32[]{:S(2)}) copy-start(f32[16,2048]{1,0:T(8,128)} %get-tuple-element.28.refs_0_) | copy-start | bytes 393220
  72.2 22.0 %all-to-all-start.1 = ((bf16[16,8,4096]{2,1,0:T(8,128)(2,1)}), bf16[16,8,4096]{2,1,0:T(8,128)(2,1)S(1)}, u32[]{:S(2)}, u32[]{:S(2)}) async-start(bf16[16,8,4096]{2,1,0:T(8,128)(2,1)} %bitcast.19), calls=%async_computation.1 | async-start | bytes 2097152 | tf_op jit(solution)/shard_map/all_to_all | solution.py:316
  77.0 7.0 %collective-permute-start.8 = (bf16[32,2048]{1,0:T(8,128)(2,1)S(1)}, bf16[32,2048]{1,0:T(8,128)(2,1)S(1)}, u32[]{:S(2)}, u32[]{:S(2)}) collective-permute-start(bf16[32,2048]{1,0:T(8,128)(2,1)S(1)} %get-tuple-element.36), channel_id=1, source_target_pairs={{0,2},{2,4},{4,6},{6,0},{1,3},{3,5},{5,7},{7,1},{8,10},{10,12},{12... | collective-permute-start | bytes 393224 | tf_op jit(solution)/shard_map/ppermute | solution.py:323
  77.6 8.5 %collective-permute-start.9 = (bf16[32,2048]{1,0:T(8,128)(2,1)S(1)}, bf16[32,2048]{1,0:T(8,128)(2,1)S(1)}, u32[]{:S(2)}, u32[]{:S(2)}) collective-permute-start(bf16[32,2048]{1,0:T(8,128)(2,1)S(1)} %get-tuple-element.37), channel_id=1, source_target_pairs={{0,6},{2,0},{4,2},{6,4},{1,7},{3,1},{5,3},{7,5},{8,14},{10,8},{12,... | collective-permute-start | bytes 393224 | tf_op jit(solution)/shard_map/ppermute | solution.py:323
  80.3 6.7 %collective-permute-start.10 = (bf16[32,2048]{1,0:T(8,128)(2,1)S(1)}, bf16[32,2048]{1,0:T(8,128)(2,1)S(1)}, u32[]{:S(2)}, u32[]{:S(2)}) collective-permute-start(bf16[32,2048]{1,0:T(8,128)(2,1)S(1)} %get-tuple-element.38), channel_id=1, source_target_pairs={{0,4},{2,6},{4,0},{6,2},{1,5},{3,7},{5,1},{7,3},{8,12},{10,14},{12... | collective-permute-start | bytes 393224 | tf_op jit(solution)/shard_map/ppermute | solution.py:323
  87.6 5.8 %collective-permute-start.11 = (bf16[16,2048]{1,0:T(8,128)(2,1)S(1)}, bf16[16,2048]{1,0:T(8,128)(2,1)S(1)}, u32[]{:S(2)}, u32[]{:S(2)}) collective-permute-start(bf16[16,2048]{1,0:T(8,128)(2,1)S(1)} %get-tuple-element.40), channel_id=1, source_target_pairs={{0,1},{1,0},{2,3},{3,2},{4,5},{5,4},{6,7},{7,6},{8,9},{9,8},{10,11... | collective-permute-start | bytes 196616 | tf_op jit(solution)/shard_map/ppermute | solution.py:331

commit v8 on v7

--- a/solution.py
+++ b/solution.py
@@ -121,7 +121,7 @@
     m_ref[...] = dot(u_ref[...], lap_s[...], 1, 1)
 
 
-def sweep(kt_ref, u_ref, v_ref, g_ref, ov_ref, start, stop, store, tile=512):
+def sweep(kt_ref, u_ref, v_ref, g_ref, was_ref, ov_ref, start, stop, store, tile=512):
     block = stop - start
 
     def turn(i, _):
@@ -132,7 +132,8 @@
         for row in range(0, u_ref.shape[1], tile):
             field = dot(kt_ref[row : row + tile, :], v, 1, 0)
             react = (field * (g - field * field)).astype(bf16)
-            ov_ref[row : row + tile, :] += dot(react, v, 1, 1)
+            onto = dot(react, v, 1, 1)
+            ov_ref[row : row + tile, :] = onto if was_ref is None else was_ref[row : row + tile, :] + onto
             part = dot(u_ref[:, row : row + tile], react, 1, 0)
             acc = part if acc is None else acc + part
         store(pl.ds(pl.multiple_of(at - start, block), block), acc)
@@ -147,7 +148,6 @@
     far_ref = refs.pop(0) if has_old & 2 else None
     l_ref, ov_ref = refs[:2]
     ov_s = refs[2] if back else ov_ref
-    ov_s[...] = jnp.zeros_like(ov_s) if far_ref is None else far_ref[...]
 
     done = 0 if old_ref is None else old_ref.shape[1]
 
@@ -158,7 +158,7 @@
         else:
             l_ref[:, here] = acc
 
-    sweep(kt_ref, u_ref, v_ref, g_ref, ov_s, start, start + l_ref.shape[1], store)
+    sweep(kt_ref, u_ref, v_ref, g_ref, far_ref, ov_s, start, start + l_ref.shape[1], store)
     if back:
         ov_ref[...] = ov_s[...].T.astype(bf16)
 
@@ -170,7 +170,6 @@
     rank, count = out_ref.shape
     middle = count - count // 2
     start = middle + more_ref.shape[1]
-    ov_s[...] = ov_ref[...]
     w = core_ref[...].astype(bf16).astype(f32) * 0.125 + scale * (ma_ref[...] + mb_ref[...])
     high = w.astype(bf16)
     w_s[:rank, :] = high
@@ -191,7 +190,7 @@
     def store(here, acc):
         send(start, count - start, l_ref[:, start:] + acc)
 
-    sweep(kt_ref, u_ref, v_ref, g_ref, ov_s, start, count, store)
+    sweep(kt_ref, u_ref, v_ref, g_ref, ov_ref, ov_s, start, count, store)
     leave[1].start()
     tot_s[...] = ov_s[...].T + got_ref[...].astype(f32)
     rows = me_ref.shape[0]

time: 95.7 us -> 95.7 us (level)
  no operation moved by 1% of the time
where the time goes in v8:
time: 95.7 us; the launch traced here: 95 us
  Pallas kernels  32.5 us (34%)
  starting transfers between devices  30.8 us (32%)
  waiting for transfers between devices  29.2 us (31%)
    pallas_call x11, Pallas kernels, small(): pl.pallas_call(reading, in_specs=[pl.BlockSpec(memory_space=pltpu.SMEM)]...  32.5 us
    ppermute x1, waiting for transfers between devices, per_device(): u1 = resident(lax.ppermute(basis_u, 'xh', swap))  14.4 us
    all_to_all x1, starting transfers between devices, per_device(): lax.all_to_all(v_wide.reshape(rank, half), SPACE, 0, 0, tiled=True)  6.59 us
    ppermute x3, waiting for transfers between devices, per_device(): near.append(resident(lax.ppermute(part, 'y', ring(4, k))))  5.88 us
    ppermute x3, starting transfers between devices, per_device(): around = [resident(lax.ppermute(pair, 'y', ring(4, k))) for k in (1, 3, 2)]  5.3 us
    ppermute x3, waiting for transfers between devices, per_device(): around = [resident(lax.ppermute(pair, 'y', ring(4, k))) for k in (1, 3, 2)]  5.13 us
    all_to_all x1, starting transfers between devices, per_device(): l_got = lax.all_to_all(l_part, SPACE, 0, 0, tiled=True)  4.75 us
    ppermute x3, starting transfers between devices, per_device(): near.append(resident(lax.ppermute(part, 'y', ring(4, k))))  4.11 us
  transfers between devices with their start and end apart: 14, of which 8 were waited for; matrix products, arithmetic and copies ran while one was open for 1% of the time, Pallas kernels for 12%

profile of v8, /device:TPU:0, one launch (start us, length us, event | category | flops | bytes accessed | tf_op | source)
XLA Modules:
  0.0 95.0 jit_solution(2265067035651611988)
XLA Ops:
  0.6 0.9 copy-done.1
  1.6 1.1 %shard_map.70 = bf16[8,2,8,4096]{3,2,1,0:T(8,128)(2,1)} custom-call(bf16[8,8192]{1,0:T(8,128)(2,1)S(1)} %copy-done.1), custom_call_target="tpu_custom_call" | custom-call | tf_op jit(solution)/shard_map/pallas_call | solution.py:32
  2.7 6.6 %all-to-all-start = ((bf16[16,8,4096]{2,1,0:T(8,128)(2,1)}), bf16[16,8,4096]{2,1,0:T(8,128)(2,1)S(1)}, u32[]{:S(2)}, u32[]{:S(2)}) async-start(bf16[16,8,4096]{2,1,0:T(8,128)(2,1)} %bitcast.18), calls=%async_computation | async-start | bytes 2097152 | tf_op jit(solution)/shard_map/all_to_all | solution.py:254
  9.3 2.8 %collective-permute-start = (bf16[16,2,8,128]{3,2,1,0:T(8,128)(2,1)S(1)}, bf16[16,2,8,128]{3,2,1,0:T(8,128)(2,1)S(1)}, u32[]{:S(2)}, u32[]{:S(2)}) collective-permute-start(bf16[16,2,8,128]{3,2,1,0:T(8,128)(2,1)S(1)} %copy-done.3), channel_id=1, source_target_pairs={{0,1},{1,0},{2,3},{3,2},{4,5},{5,4},{6,7},{7,6},{8,9},{9,8},{10,11... | collective-permute-start | bytes 196616 | tf_op jit(solution)/shard_map/ppermute | solution.py:255
  12.1 14.4 %collective-permute-done.refs_1_ = bf16[16,2,8,128]{3,2,1,0:T(8,128)(2,1)S(1)} collective-permute-done((bf16[16,2,8,128]{3,2,1,0:T(8,128)(2,1)S(1)}, bf16[16,2,8,128]{3,2,1,0:T(8,128)(2,1)S(1)}, u32[]{:S(2)}, u32[]{:S(2)}) %collective-permute-start) | collective-permute-done | bytes 65568 | tf_op jit(solution)/shard_map/ppermute | solution.py:255
  26.7 3.3 %collective-permute-start.3 = (bf16[32,2048]{1,0:T(8,128)(2,1)S(1)}, bf16[32,2048]{1,0:T(8,128)(2,1)S(1)}, u32[]{:S(2)}, u32[]{:S(2)}) collective-permute-start(bf16[32,2048]{1,0:T(8,128)(2,1)S(1)} %shard_map.68.refs_1_), channel_id=1, source_target_pairs={{0,4},{2,6},{4,0},{6,2},{1,5},{3,7},{5,1},{7,3},{8,12},{10,14},{12... | collective-permute-start | bytes 393224 | tf_op jit(solution)/shard_map/ppermute | solution.py:257
  30.0 1.1 %collective-permute-start.2 = (bf16[32,2048]{1,0:T(8,128)(2,1)S(1)}, bf16[32,2048]{1,0:T(8,128)(2,1)S(1)}, u32[]{:S(2)}, u32[]{:S(2)}) collective-permute-start(bf16[32,2048]{1,0:T(8,128)(2,1)S(1)} %shard_map.68.refs_1_), channel_id=1, source_target_pairs={{0,6},{2,0},{4,2},{6,4},{1,7},{3,1},{5,3},{7,5},{8,14},{10,8},{12,... | collective-permute-start | bytes 393224 | tf_op jit(solution)/shard_map/ppermute | solution.py:257
  31.1 1.0 %collective-permute-start.1 = (bf16[32,2048]{1,0:T(8,128)(2,1)S(1)}, bf16[32,2048]{1,0:T(8,128)(2,1)S(1)}, u32[]{:S(2)}, u32[]{:S(2)}) collective-permute-start(bf16[32,2048]{1,0:T(8,128)(2,1)S(1)} %shard_map.68.refs_1_), channel_id=1, source_target_pairs={{0,2},{2,4},{4,6},{6,0},{1,3},{3,5},{5,7},{7,1},{8,10},{10,12},{12... | collective-permute-start | bytes 393224 | tf_op jit(solution)/shard_map/ppermute | solution.py:257
  32.1 2.2 %collective-permute-done.3.refs_4_ = bf16[32,2048]{1,0:T(8,128)(2,1)S(1)} collective-permute-done((bf16[32,2048]{1,0:T(8,128)(2,1)S(1)}, bf16[32,2048]{1,0:T(8,128)(2,1)S(1)}, u32[]{:S(2)}, u32[]{:S(2)}) %collective-permute-start.3) | collective-permute-done | bytes 131104 | tf_op jit(solution)/shard_map/ppermute | solution.py:257
  34.3 2.5 %collective-permute-done.2.refs_3_ = bf16[32,2048]{1,0:T(8,128)(2,1)S(1)} collective-permute-done((bf16[32,2048]{1,0:T(8,128)(2,1)S(1)}, bf16[32,2048]{1,0:T(8,128)(2,1)S(1)}, u32[]{:S(2)}, u32[]{:S(2)}) %collective-permute-start.2) | collective-permute-done | bytes 131104 | tf_op jit(solution)/shard_map/ppermute | solution.py:257
  37.3 1.7 %shard_map.69 = (bf16[128,2048]{1,0:T(8,128)(2,1)S(1)}, bf16[128,2048]{1,0:T(8,128)(2,1)S(1)}, bf16[2048,128]{1,0:T(8,128)(2,1)S(1)}, bf16[128,1024]{1,0:T(8,128)(2,1)}) custom-call(s32[4]{0:T(128)S(1)} %pad_add_fusion.refs_0_, bf16[32,2048]{1,0:T(8,128)(2,1)S(1)} %shard_map.68.refs_1_, bf16[32,2048]{1,0:T(8,128)(2,1)S(1)} %collective-permute-done.1.refs_2_, ...), custom_call_target="tpu_custom_call" | custom-call | tf_op jit(solution)/shard_map/pallas_call | solution.py:32
  40.5 5.6 %shard_map.71 = (f32[128,2048]{1,0:T(8,128)S(1)}, f32[2048,128]{1,0:T(8,128)S(1)}) custom-call(bf16[2048,128]{1,0:T(8,128)(2,1)S(1)} %get-tuple-element.25.refs_0_.refs_8_.refs_6_.refs_1_, bf16[128,2048]{1,0:T(8,128)(2,1)S(1)} %get-tuple-element.22.refs_1_.refs_6_.refs_7_.refs_2_, bf16[128,4096]{1,0:T(8,128)(2,1)S(1)} %bitcast.9, f32[1,4096]{1,0:T(1,128)S(1)} %bitcast.14), custom_call_target="tpu_custom_call" | custom-call | tf_op jit(solution)/shard_map/pallas_call | solution.py:32
  46.2 2.4 %shard_map.72 = (bf16[2048,128]{1,0:T(8,128)(2,1)S(1)}, f32[16,2048]{1,0:T(8,128)}, f32[128,128]{1,0:T(8,128)S(1)}) custom-call(s32[4]{0:T(128)S(1)} %pad_add_fusion.refs_0_, bf16[128,2048]{1,0:T(8,128)(2,1)S(1)} %collective-permute-done.4.refs_1_, f32[128,128]{1,0:T(8,128)S(1)} %copy-done, bf16[128,2048]{1,0:T(8,128)(2,1)S(1)} %get-tuple-element.23.refs_3_, ...), custom_call_target="tpu_custom_call" | custom-call | tf_op jit(solution)/shard_map/pallas_call | solution.py:32
  48.5 11.5 %shard_map.73 = (f32[128,4096]{1,0:T(8,128)S(1)}, bf16[128,2048]{1,0:T(8,128)(2,1)S(1)}) custom-call(bf16[2048,128]{1,0:T(8,128)(2,1)S(1)} %get-tuple-element.29.refs_0_, bf16[128,2048]{1,0:T(8,128)(2,1)S(1)} %collective-permute-done.4.refs_1_, bf16[128,4096]{1,0:T(8,128)(2,1)S(1)} %bitcast.10, f32[1,4096]{1,0:T(1,128)S(1)} %bitcast.15, ...), custom_call_target="tpu_custom_call" | custom-call | tf_op jit(solution)/shard_map/pallas_call | solution.py:32
  60.0 4.0 %collective-permute-start.6 = (bf16[128,2048]{1,0:T(8,128)(2,1)S(1)}, bf16[128,2048]{1,0:T(8,128)(2,1)S(1)}, u32[]{:S(2)}, u32[]{:S(2)}) collective-permute-start(bf16[128,2048]{1,0:T(8,128)(2,1)S(1)} %get-tuple-element.31.refs_6_), channel_id=1, source_target_pairs={{0,8},{8,0},{1,9},{9,1},{2,10},{10,2},{3,11},{11,3},{4,12},{12,4},... | collective-permute-start | bytes 1572872 | tf_op jit(solution)/shard_map/ppermute | solution.py:293
  64.3 2.9 %shard_map.74 = (f32[128,1024]{1,0:T(8,128)S(1)}, f32[2048,128]{1,0:T(8,128)S(1)}) custom-call(bf16[2048,128]{1,0:T(8,128)(2,1)S(1)} %get-tuple-element.25.refs_0_.refs_8_.refs_6_.refs_1_, bf16[128,2048]{1,0:T(8,128)(2,1)S(1)} %get-tuple-element.22.refs_1_.refs_6_.refs_7_.refs_2_, bf16[128,4096]{1,0:T(8,128)(2,1)S(1)} %bitcast.11, f32[1,4096]{1,0:T(1,128)S(1)} %bitcast.16, ...), custom_call_target="tpu_custom_call" | custom-call | tf_op jit(solution)/shard_map/pallas_call | solution.py:32
  67.3 4.9 %shard_map.75 = (bf16[128,4096]{1,0:T(8,128)(2,1)}, f32[32,2048]{1,0:T(8,128)S(1)}, bf16[32,2048]{1,0:T(8,128)(2,1)S(1)}, bf16[32,2048]{1,0:T(8,128)(2,1)S(1)}, bf16[32,2048]{1,0:T(8,128)(2,1)S(1)}) custom-call(s32[4]{0:T(128)S(1)} %pad_add_fusion.refs_0_, bf16[2048,128]{1,0:T(8,128)(2,1)S(1)} %get-tuple-element.25.refs_0_.refs_8_.refs_6_.refs_1_, ...), custom_call_target="tpu_custom_call" | custom-call | tf_op jit(solution)/shard_map/pallas_call | solution.py:32
  72.2 4.8 %all-to-all-start.1 = ((bf16[16,8,4096]{2,1,0:T(8,128)(2,1)}), bf16[16,8,4096]{2,1,0:T(8,128)(2,1)S(1)}, u32[]{:S(2)}, u32[]{:S(2)}) async-start(bf16[16,8,4096]{2,1,0:T(8,128)(2,1)} %bitcast.19), calls=%async_computation.1 | async-start | bytes 2097152 | tf_op jit(solution)/shard_map/all_to_all | solution.py:315
  77.6 2.7 %collective-permute-start.9 = (bf16[32,2048]{1,0:T(8,128)(2,1)S(1)}, bf16[32,2048]{1,0:T(8,128)(2,1)S(1)}, u32[]{:S(2)}, u32[]{:S(2)}) collective-permute-start(bf16[32,2048]{1,0:T(8,128)(2,1)S(1)} %get-tuple-element.37), channel_id=1, source_target_pairs={{0,6},{2,0},{4,2},{6,4},{1,7},{3,1},{5,3},{7,5},{8,14},{10,8},{12,... | collective-permute-start | bytes 393224 | tf_op jit(solution)/shard_map/ppermute | solution.py:322
  81.1 2.9 %collective-permute-done.8.refs_2_ = bf16[32,2048]{1,0:T(8,128)(2,1)S(1)} collective-permute-done((bf16[32,2048]{1,0:T(8,128)(2,1)S(1)}, bf16[32,2048]{1,0:T(8,128)(2,1)S(1)}, u32[]{:S(2)}, u32[]{:S(2)}) %collective-permute-start.8) | collective-permute-done | bytes 131104 | tf_op jit(solution)/shard_map/ppermute | solution.py:322
  84.0 2.1 %collective-permute-done.9.refs_3_ = bf16[32,2048]{1,0:T(8,128)(2,1)S(1)} collective-permute-done((bf16[32,2048]{1,0:T(8,128)(2,1)S(1)}, bf16[32,2048]{1,0:T(8,128)(2,1)S(1)}, u32[]{:S(2)}, u32[]{:S(2)}) %collective-permute-start.9) | collective-permute-done | bytes 131104 | tf_op jit(solution)/shard_map/ppermute | solution.py:322
  86.1 0.9 collective-permute-done.10.refs_4_
  87.6 2.0 %collective-permute-start.11 = (bf16[16,2048]{1,0:T(8,128)(2,1)S(1)}, bf16[16,2048]{1,0:T(8,128)(2,1)S(1)}, u32[]{:S(2)}, u32[]{:S(2)}) collective-permute-start(bf16[16,2048]{1,0:T(8,128)(2,1)S(1)} %get-tuple-element.40), channel_id=1, source_target_pairs={{0,1},{1,0},{2,3},{3,2},{4,5},{5,4},{6,7},{7,6},{8,9},{9,8},{10,11... | collective-permute-start | bytes 196616 | tf_op jit(solution)/shard_map/ppermute | solution.py:330
  89.6 3.8 %collective-permute-done.11.refs_2_ = bf16[16,2048]{1,0:T(8,128)(2,1)S(1)} collective-permute-done((bf16[16,2048]{1,0:T(8,128)(2,1)S(1)}, bf16[16,2048]{1,0:T(8,128)(2,1)S(1)}, u32[]{:S(2)}, u32[]{:S(2)}) %collective-permute-start.11) | collective-permute-done | bytes 65568 | tf_op jit(solution)/shard_map/ppermute | solution.py:330
  (27 shorter events, 6.4 us)
Async XLA Ops:
  0.6 36.6 %copy-start = (f32[128,128]{1,0:T(8,128)S(1)}, f32[128,128]{1,0:T(8,128)}, u32[]{:S(2)}) copy-start(f32[128,128]{1,0:T(8,128)} %refs_11_.1) | copy-start | bytes 196612
  0.6 0.9 copy-start.1
  1.6 7.7 %copy-start.3 = (bf16[16,2,8,128]{3,2,1,0:T(8,128)(2,1)S(1)}, bf16[16,2,8,128]{3,2,1,0:T(8,128)(2,1)}, u32[]{:S(2)}) copy-start(bf16[16,2,8,128]{3,2,1,0:T(8,128)(2,1)} %refs_0_.2) | copy-start | bytes 196612
  2.7 43.5 %copy-start.4 = (s32[6,2,8,128]{3,2,1,0:T(8,128)S(1)}, s32[6,2,8,128]{3,2,1,0:T(8,128)}, u32[]{:S(2)}) copy-start(s32[6,2,8,128]{3,2,1,0:T(8,128)} %refs_5_.3) | copy-start | bytes 147460
  2.7 37.8 %all-to-all-start = ((bf16[16,8,4096]{2,1,0:T(8,128)(2,1)}), bf16[16,8,4096]{2,1,0:T(8,128)(2,1)S(1)}, u32[]{:S(2)}, u32[]{:S(2)}) async-start(bf16[16,8,4096]{2,1,0:T(8,128)(2,1)} %bitcast.18), calls=%async_computation | async-start | bytes 2097152 | tf_op jit(solution)/shard_map/all_to_all | solution.py:254
  9.3 17.2 %collective-permute-start = (bf16[16,2,8,128]{3,2,1,0:T(8,128)(2,1)S(1)}, bf16[16,2,8,128]{3,2,1,0:T(8,128)(2,1)S(1)}, u32[]{:S(2)}, u32[]{:S(2)}) collective-permute-start(bf16[16,2,8,128]{3,2,1,0:T(8,128)(2,1)S(1)} %copy-done.3), channel_id=1, source_target_pairs={{0,1},{1,0},{2,3},{3,2},{4,5},{5,4},{6,7},{7,6},{8,9},{9,8},{10,11... | collective-permute-start | bytes 196616 | tf_op jit(solution)/shard_map/ppermute | solution.py:255
  26.7 7.6 %collective-permute-start.3 = (bf16[32,2048]{1,0:T(8,128)(2,1)S(1)}, bf16[32,2048]{1,0:T(8,128)(2,1)S(1)}, u32[]{:S(2)}, u32[]{:S(2)}) collective-permute-start(bf16[32,2048]{1,0:T(8,128)(2,1)S(1)} %shard_map.68.refs_1_), channel_id=1, source_target_pairs={{0,4},{2,6},{4,0},{6,2},{1,5},{3,7},{5,1},{7,3},{8,12},{10,14},{12... | collective-permute-start | bytes 393224 | tf_op jit(solution)/shard_map/ppermute | solution.py:257
  30.0 6.8 %collective-permute-start.2 = (bf16[32,2048]{1,0:T(8,128)(2,1)S(1)}, bf16[32,2048]{1,0:T(8,128)(2,1)S(1)}, u32[]{:S(2)}, u32[]{:S(2)}) collective-permute-start(bf16[32,2048]{1,0:T(8,128)(2,1)S(1)} %shard_map.68.refs_1_), channel_id=1, source_target_pairs={{0,6},{2,0},{4,2},{6,4},{1,7},{3,1},{5,3},{7,5},{8,14},{10,8},{12,... | collective-permute-start | bytes 393224 | tf_op jit(solution)/shard_map/ppermute | solution.py:257
  31.1 6.2 %collective-permute-start.1 = (bf16[32,2048]{1,0:T(8,128)(2,1)S(1)}, bf16[32,2048]{1,0:T(8,128)(2,1)S(1)}, u32[]{:S(2)}, u32[]{:S(2)}) collective-permute-start(bf16[32,2048]{1,0:T(8,128)(2,1)S(1)} %shard_map.68.refs_1_), channel_id=1, source_target_pairs={{0,2},{2,4},{4,6},{6,0},{1,3},{3,5},{5,7},{7,1},{8,10},{10,12},{12... | collective-permute-start | bytes 393224 | tf_op jit(solution)/shard_map/ppermute | solution.py:257
  38.9 7.2 %collective-permute-start.4 = (bf16[128,2048]{1,0:T(8,128)(2,1)S(1)}, bf16[128,2048]{1,0:T(8,128)(2,1)S(1)}, u32[]{:S(2)}, u32[]{:S(2)}) collective-permute-start(bf16[128,2048]{1,0:T(8,128)(2,1)S(1)} %get-tuple-element.22.refs_1_.refs_6_.refs_7_.refs_2_), channel_id=1, source_target_pairs={{0,8},{8,0},{1,9},{9,1},{2,10},{10,2},{3,11},{11,3},{4,12},{12,4},... | collective-permute-start | bytes 1572872 | tf_op jit(solution)/shard_map/ppermute | solution.py:264
  38.9 7.2 %collective-permute-start.5 = (bf16[128,1024]{1,0:T(8,128)(2,1)}, bf16[128,1024]{1,0:T(8,128)(2,1)S(1)}, u32[]{:S(2)}, u32[]{:S(2)}) collective-permute-start(bf16[128,1024]{1,0:T(8,128)(2,1)} %get-tuple-element.24), channel_id=1, source_target_pairs={{8,16},{24,32},{40,48},{56,64},{72,80},{88,96},{104,112},{16,8},{3... | collective-permute-start | bytes 786440 | tf_op jit(solution)/shard_map/ppermute | solution.py:267
  60.0 7.2 %collective-permute-start.6 = (bf16[128,2048]{1,0:T(8,128)(2,1)S(1)}, bf16[128,2048]{1,0:T(8,128)(2,1)S(1)}, u32[]{:S(2)}, u32[]{:S(2)}) collective-permute-start(bf16[128,2048]{1,0:T(8,128)(2,1)S(1)} %get-tuple-element.31.refs_6_), channel_id=1, source_target_pairs={{0,8},{8,0},{1,9},{9,1},{2,10},{10,2},{3,11},{11,3},{4,12},{12,4},... | collective-permute-start | bytes 1572872 | tf_op jit(solution)/shard_map/ppermute | solution.py:293
  64.0 3.3 %collective-permute-start.7 = (f32[128,128]{1,0:T(8,128)S(1)}, f32[128,128]{1,0:T(8,128)S(1)}, u32[]{:S(2)}, u32[]{:S(2)}) collective-permute-start(f32[128,128]{1,0:T(8,128)S(1)} %get-tuple-element.34.refs_9_), channel_id=1, source_target_pairs={{0,8},{8,0},{1,9},{9,1},{2,10},{10,2},{3,11},{11,3},{4,12},{12,4},... | collective-permute-start | bytes 196616 | tf_op jit(solution)/shard_map/ppermute | solution.py:285
  72.2 21.3 %copy-start.2 = (f32[16,2048]{1,0:T(8,128)S(1)}, f32[16,2048]{1,0:T(8,128)}, u32[]{:S(2)}) copy-start(f32[16,2048]{1,0:T(8,128)} %get-tuple-element.28.refs_0_) | copy-start | bytes 393220
  72.2 22.0 %all-to-all-start.1 = ((bf16[16,8,4096]{2,1,0:T(8,128)(2,1)}), bf16[16,8,4096]{2,1,0:T(8,128)(2,1)S(1)}, u32[]{:S(2)}, u32[]{:S(2)}) async-start(bf16[16,8,4096]{2,1,0:T(8,128)(2,1)} %bitcast.19), calls=%async_computation.1 | async-start | bytes 2097152 | tf_op jit(solution)/shard_map/all_to_all | solution.py:315
  77.0 7.0 %collective-permute-start.8 = (bf16[32,2048]{1,0:T(8,128)(2,1)S(1)}, bf16[32,2048]{1,0:T(8,128)(2,1)S(1)}, u32[]{:S(2)}, u32[]{:S(2)}) collective-permute-start(bf16[32,2048]{1,0:T(8,128)(2,1)S(1)} %get-tuple-element.36), channel_id=1, source_target_pairs={{0,2},{2,4},{4,6},{6,0},{1,3},{3,5},{5,7},{7,1},{8,10},{10,12},{12... | collective-permute-start | bytes 393224 | tf_op jit(solution)/shard_map/ppermute | solution.py:322
  77.6 8.5 %collective-permute-start.9 = (bf16[32,2048]{1,0:T(8,128)(2,1)S(1)}, bf16[32,2048]{1,0:T(8,128)(2,1)S(1)}, u32[]{:S(2)}, u32[]{:S(2)}) collective-permute-start(bf16[32,2048]{1,0:T(8,128)(2,1)S(1)} %get-tuple-element.37), channel_id=1, source_target_pairs={{0,6},{2,0},{4,2},{6,4},{1,7},{3,1},{5,3},{7,5},{8,14},{10,8},{12,... | collective-permute-start | bytes 393224 | tf_op jit(solution)/shard_map/ppermute | solution.py:322
  80.3 6.7 %collective-permute-start.10 = (bf16[32,2048]{1,0:T(8,128)(2,1)S(1)}, bf16[32,2048]{1,0:T(8,128)(2,1)S(1)}, u32[]{:S(2)}, u32[]{:S(2)}) collective-permute-start(bf16[32,2048]{1,0:T(8,128)(2,1)S(1)} %get-tuple-element.38), channel_id=1, source_target_pairs={{0,4},{2,6},{4,0},{6,2},{1,5},{3,7},{5,1},{7,3},{8,12},{10,14},{12... | collective-permute-start | bytes 393224 | tf_op jit(solution)/shard_map/ppermute | solution.py:322
  87.6 5.8 %collective-permute-start.11 = (bf16[16,2048]{1,0:T(8,128)(2,1)S(1)}, bf16[16,2048]{1,0:T(8,128)(2,1)S(1)}, u32[]{:S(2)}, u32[]{:S(2)}) collective-permute-start(bf16[16,2048]{1,0:T(8,128)(2,1)S(1)} %get-tuple-element.40), channel_id=1, source_target_pairs={{0,1},{1,0},{2,3},{3,2},{4,5},{5,4},{6,7},{7,6},{8,9},{9,8},{10,11... | collective-permute-start | bytes 196616 | tf_op jit(solution)/shard_map/ppermute | solution.py:330
